TPU v7x, 128 devices: a whole 4x4x4 slice. The times are simulated.
128 devices in a mesh: px: 8 (over z, core), pz: 16 (over x, y).
Axes of the slice: x: 4, y: 4, z: 4, core: 2. Of those that a mesh axis runs over, the one named last changes fastest.
Arguments:
- charge: float32 [32768, 128], P(('px', 'pz')), may hold values from -6 to 6
- dest: int32 [32768, 1], P(('px', 'pz')), may hold values from 0 to 127; in each aligned block of 256 rows (0 to 255, 256 to 511, ...) at most 4 rows name the same one
- local_ids: int32 [32768], P(('px', 'pz')), may hold values from 0 to 255
- green_hat: float32 [128, 128, 2048], P(None, 'px', 'pz'), may hold values from 0.1 to 10, as said below
Outputs:
- potential: float32 [32768, 128], P(('px', 'pz'))
Inputs may be any that keep to these rules, and one draw needn't show every extreme that they name: `dest`: among the 256 slots of one box, no pencil is named by more than 4; some pencil is named by exactly 4. green_hat is even in every dimension: its value at frequencies (k1, k2, k3) equals that at ((128 - k1) mod 2 * 64, (128 - k2) mod 2 * 64, (2048 - k3) mod 2 * 1024) taken in any single dimension.
All inputs are finite; a program needn't handle non-finite values.
Results may differ from a plain program's by a relative error of at most 0.00007.
Values sent between devices are 32-bit elements; how exact they have to be, the bound alone decides.
No kernel may reach another device: no remote copies, remote signals or barrier semaphores. Data moves between devices by JAX's collectives and lax.ppermute only.
A program may use at most 64 MiB of HBM per device.

v0:
```python
import math

import jax
import jax.numpy as jnp
from jax import lax
from jax.sharding import PartitionSpec as P

CXP = 8
CYP = 4
NZP = 1024


def dft_table(n_in, n_out, period, sign):
    rows = lax.broadcasted_iota(jnp.int32, (n_in, n_out), 0)
    cols = lax.broadcasted_iota(jnp.int32, (n_in, n_out), 1)
    phase = (rows * cols % period).astype(jnp.float32) * (2.0 * math.pi / period)
    return (jnp.cos(phase), sign * jnp.sin(phase))


def rotate(real_part, imag_part, cosine, sine, form):
    first = jnp.einsum(form, real_part, cosine, precision=lax.Precision.HIGHEST)
    second = jnp.einsum(form, imag_part, sine, precision=lax.Precision.HIGHEST)
    third = jnp.einsum(form, imag_part, cosine, precision=lax.Precision.HIGHEST)
    fourth = jnp.einsum(form, real_part, sine, precision=lax.Precision.HIGHEST)
    return (first - second, third + fourth)


def solve_field(field, green_hat, wide_x, wide_y):
    cosine, sine = dft_table(NZP, 2 * NZP, 2 * NZP, -1.0)
    real_part = jnp.einsum("xyz,zk->xyk", field, cosine, precision=lax.Precision.HIGHEST)
    imag_part = jnp.einsum("xyz,zk->xyk", field, sine, precision=lax.Precision.HIGHEST)
    turned = lax.all_to_all(
        jnp.stack((real_part, imag_part)), "pz", split_axis=3, concat_axis=2, tiled=True
    )
    cosine, sine = dft_table(wide_y, 2 * wide_y, 2 * wide_y, -1.0)
    real_part, imag_part = rotate(turned[0], turned[1], cosine, sine, "xyk,yq->xqk")
    turned = lax.all_to_all(
        jnp.stack((real_part, imag_part)), "px", split_axis=2, concat_axis=1, tiled=True
    )
    cosine, sine = dft_table(wide_x, 2 * wide_x, 2 * wide_x, -1.0)
    real_part, imag_part = rotate(turned[0], turned[1], cosine, sine, "xyk,xq->qyk")
    real_part = real_part * green_hat
    imag_part = imag_part * green_hat
    cosine, sine = dft_table(2 * wide_x, wide_x, 2 * wide_x, 1.0)
    real_part, imag_part = rotate(real_part, imag_part, cosine, sine, "qyk,qx->xyk")
    turned = lax.all_to_all(
        jnp.stack((real_part, imag_part)), "px", split_axis=1, concat_axis=2, tiled=True
    )
    cosine, sine = dft_table(2 * wide_y, wide_y, 2 * wide_y, 1.0)
    real_part, imag_part = rotate(turned[0], turned[1], cosine, sine, "xqk,qy->xyk")
    turned = lax.all_to_all(
        jnp.stack((real_part, imag_part)), "pz", split_axis=2, concat_axis=3, tiled=True
    )
    cosine, sine = dft_table(2 * NZP, NZP, 2 * NZP, 1.0)
    result = jnp.einsum("xyk,kz->xyz", turned[0], cosine, precision=lax.Precision.HIGHEST)
    result = result - jnp.einsum("xyk,kz->xyz", turned[1], sine, precision=lax.Precision.HIGHEST)
    return result * (1.0 / (8.0 * wide_x * wide_y * NZP))


def local(charge, dest, local_ids, green_hat):
    n_dev = lax.axis_size(("px", "pz"))
    wide_x = CXP * lax.axis_size("px")
    wide_y = CYP * lax.axis_size("pz")
    pencil_blocks = CXP * CYP * NZP // 128
    route = dest[:, 0]
    dense = (
        jnp.zeros((n_dev * pencil_blocks, 128), jnp.float32)
        .at[route * pencil_blocks + local_ids]
        .add(charge)
    )
    pencil = lax.psum_scatter(dense, ("px", "pz"), scatter_dimension=0, tiled=True)
    field = pencil.reshape(CXP, CYP, NZP)
    phi = solve_field(field, green_hat, wide_x, wide_y)
    phi_blocks = phi.reshape(pencil_blocks, 128)
    whole = lax.all_gather(phi_blocks, ("px", "pz"), axis=0, tiled=True)
    return whole[route * pencil_blocks + local_ids]


def solution(mesh):
    return jax.shard_map(
        local,
        mesh=mesh,
        in_specs=(
            P(("px", "pz"), None),
            P(("px", "pz"), None),
            P(("px", "pz")),
            P(None, "px", "pz"),
        ),
        out_specs=P(("px", "pz"), None),
        check_vma=False,
    )
```

profile of v0, /device:TPU:1, one launch (start us, length us, event | category | flops | bytes accessed | tf_op | source)
XLA Modules:
  0.0 1049.4 jit_solution(2361567284407666978)
XLA Ops:
  6.5 0.0 reduce-scatter.2.cloned.1.call-start
  6.5 0.7 broadcast_multiply_fusion
  7.2 0.7 compare_select_fusion
  7.9 8.5 scatter_custom_fusion
  16.4 0.0 reduce-scatter.2.cloned.1.call-update
  16.5 0.6 all-gather.2.cloned.1.call-start
  17.0 645.7 %reduce-scatter.2.cloned.1.call-done = f32[256,128]{1,0:T(8,128)} async-done(((f32[32768,128]{1,0:T(8,128)}), f32[256,128]{1,0:T(8,128)}) %reduce-scatter.2.cloned.1.call-update) | async-done | bytes 131088 | tf_op jit(solution)/shard_map/reduce_scatter | solution.py:71
  662.7 0.9 reshape.24
  663.6 35.7 %fusion.32 = f32[1,8,4,2048]{3,1,2,0:T(8,128)S(1)} fusion(f32[8,4,1024]{2,1,0:T(4,128)S(1)} %reshape.24), kind=kOutput, calls=%fused_computation.36 | convolution fusion | flops 834666496 | bytes 393216 | tf_op jit(solution)/shard_map/xyz,zk->xyk/dot_general | solution.py:30
  699.3 36.1 %fusion.35 = f32[1,8,4,2048]{3,1,2,0:T(8,128)S(1)} fusion(f32[8,4,1024]{2,1,0:T(4,128)S(1)} %reshape.24), kind=kOutput, calls=%fused_computation.37 | convolution fusion | flops 836763648 | bytes 393216 | tf_op jit(solution)/shard_map/xyz,zk->xyk/dot_general | solution.py:31
  735.5 5.8 copy.30
  741.3 11.4 %reshape.54 = f32[16,1,8192]{2,1,0:T(1,128)S(1)} reshape(f32[2048,2,4,8]{3,2,1,0:T(4,128)} %bitcast.127) | data formatting | bytes 1048576
  752.7 11.7 %all_to_all.60 = f32[16,1,8192]{2,1,0:T(1,128)S(1)} all-to-all(f32[16,1,8192]{2,1,0:T(1,128)S(1)} %reshape.54), channel_id=1, replica_groups=mesh['px'=8,'pz'=16] {'pz'}, dimensions={0} | all-to-all | bytes 1048576 | tf_op jit(solution)/shard_map/all_to_all | solution.py:32
  764.5 0.5 broadcast.213
  765.0 1.9 reduce
  766.9 11.9 %reshape.55 = f32[2048,2,4,8]{3,2,1,0:T(4,128)} reshape(f32[16,8192]{1,0:T(8,128)S(1)} %reduce) | data formatting | bytes 1048576
  778.8 6.7 copy.31
  785.5 0.0 copy-start
  785.6 0.7 fusion.74
  786.3 0.7 fusion.72
  787.1 0.8 fusion.43
  787.9 0.8 fusion.42
  788.6 0.1 pad_maximum_fusion
  788.7 0.6 copy.32
  789.3 51.9 %all_to_all.61 = f32[2,8,128,128]{3,1,0,2:T(8,128)S(1)} all-to-all(f32[2,8,128,128]{3,1,0,2:T(8,128)S(1)} %copy.32), channel_id=1, replica_groups=mesh['px'=8,'pz'=16] {'px'}, dimensions={2} | all-to-all | bytes 2097152 | tf_op jit(solution)/shard_map/all_to_all | solution.py:37
  841.3 0.1 copy.51
  841.4 1.2 fusion.52
  842.5 1.2 fusion.53
  843.7 0.0 copy-done
  843.7 1.4 fusion.39
  845.2 0.8 fusion.82
  846.0 1.4 fusion.38
  847.4 0.8 fusion.80
  848.2 0.8 fusion.41
  849.0 0.8 fusion.40
  849.8 0.1 pad_maximum_fusion.1
  849.9 0.6 copy.36
  850.6 18.5 %all_to_all.62 = f32[2,64,16,128]{3,2,0,1:T(8,128)S(1)} all-to-all(f32[2,64,16,128]{3,2,0,1:T(8,128)S(1)} %copy.36), channel_id=1, replica_groups=mesh['px'=8,'pz'=16] {'px'}, dimensions={1} | all-to-all | bytes 2097152 | tf_op jit(solution)/shard_map/all_to_all | solution.py:46
  869.1 0.1 copy.50
  869.2 0.1 fusion.198
  869.3 0.5 fusion.78
  869.8 0.5 fusion.76
  870.4 0.5 fusion.45
  870.9 0.5 fusion.44
  871.5 0.3 copy.38
  871.9 12.4 %all_to_all.63 = f32[2,8,64,128]{3,1,0,2:T(8,128)S(1)} all-to-all(f32[2,8,64,128]{3,1,0,2:T(8,128)S(1)} %copy.38), channel_id=1, replica_groups=mesh['px'=8,'pz'=16] {'pz'}, dimensions={2} | all-to-all | bytes 1048576 | tf_op jit(solution)/shard_map/all_to_all | solution.py:51
  884.3 35.3 %fusion.6 = f32[8,4,1024]{2,0,1:T(8,128)S(1)} fusion(f32[2,8,4,16,128]{4,1,3,2,0:T(8,128)S(1)} %bitcast.146), kind=kOutput, calls=%fused_computation.14 | convolution fusion | flops 834666496 | bytes 393216 | tf_op jit(solution)/shard_map/xyk,kz->xyz/dot_general | solution.py:56
  919.6 35.3 %fusion.49 = f32[8,4,1024]{2,0,1:T(8,128)S(1)} fusion(f32[8,4,1024]{2,0,1:T(8,128)S(1)} %fusion.6, f32[2,8,4,16,128]{4,1,3,2,0:T(8,128)S(1)} %bitcast.147), kind=kOutput, calls=%fused_computation.55 | convolution fusion | flops 834732032 | bytes 524288 | tf_op jit(solution)/shard_map/xyk,kz->xyz/dot_general | solution.py:55
  954.9 0.1 copy.40
  955.0 0.7 reshape.25
  955.7 0.0 all-gather.2.cloned.1.call-update
  955.7 79.6 %all-gather.2.cloned.1.call-done = f32[32768,128]{1,0:T(8,128)} async-done(((f32[256,128]{1,0:T(8,128)}), f32[32768,128]{1,0:T(8,128)}) %all-gather.2.cloned.1.call-update) | async-done | bytes 16777232 | tf_op jit(solution)/shard_map/all_gather | solution.py:75
  1035.3 7.1 gather_fusion
  (5 shorter events, 0.2 us)
Async XLA Ops:
  6.5 656.2 %reduce-scatter.2.cloned.1.call-start = ((), (), s32[]{:S(2)}) async-start(), calls=%async_computation.5 | async-start | bytes 16908288 | tf_op jit(solution)/shard_map/reduce_scatter | solution.py:71
  16.5 1018.8 %all-gather.2.cloned.1.call-start = ((), (), s32[]{:S(2)}) async-start(), calls=%async_computation.6 | async-start | bytes 16908288 | tf_op jit(solution)/shard_map/all_gather | solution.py:75
  785.5 58.2 %copy-start = (f32[128,16,128]{2,1,0:T(8,128)S(1)}, f32[128,16,128]{2,1,0:T(8,128)}, u32[]{:S(2)}) copy-start(f32[128,16,128]{2,1,0:T(8,128)} %param.7) | copy-start | bytes 3145732
Sparse Core Ops, SparseCore 0:
  16.6 646.0 reduce-scatter.1
  955.8 79.3 all-gather.1
where the time goes:
time: 1050 us
  waiting for transfers between devices  725 us (69%)
  matrix products  156 us (15%)
  blocking collectives  94.5 us (9%)
  local copies, waits for them, and re-layouts  47.1 us (4%)
  between operations  13.9 us (1%)
  other arithmetic  12.1 us (1%)
    reduce_scatter x1, waiting for transfers between devices, local(): lax.psum_scatter(dense, ('px', 'pz'), scatter_dimension=0, tiled=True)  646 us
    all_gather x1, waiting for transfers between devices, local(): whole = lax.all_gather(phi_blocks, ('px', 'pz'), axis=0, tiled=True)  79.6 us
    all_to_all x1, blocking collectives, solve_field(): lax.all_to_all(jnp.stack((real_part, imag_part)), 'px', split_axis=2, con...  51.9 us
    dot_general x1, matrix products, solve_field(): jnp.einsum('xyz,zk->xyk', field, sine, precision=lax.Precision.HIGHEST)  36.1 us
    dot_general x1, matrix products, solve_field(): jnp.einsum('xyz,zk->xyk', field, cosine, precision=lax.Precision.HIGHEST)  35.7 us
    dot_general x1, matrix products, solve_field(): jnp.einsum('xyk,kz->xyz', turned[1], sine, precision=lax.Precision.HIGHEST)  35.3 us
    dot_general x1, matrix products, solve_field(): jnp.einsum('xyk,kz->xyz', turned[0], cosine, precision=lax.Precision.HIGH...  35.3 us
    unnamed x4, local copies, waits for them, and re-layouts  23.3 us
  transfers between devices with their start and end apart: 2, of which 2 were waited for; matrix products, arithmetic and copies ran while one was open for 0% of the time, Pallas kernels for 0%

commit v1 on v0

v1 whole, which is shorter than its diff:
```python
import jax
import jax.numpy as jnp
import ml_dtypes
import numpy as np
from jax import lax
from jax.experimental import pallas as pl
from jax.experimental.pallas import tpu as pltpu
from jax.sharding import PartitionSpec as P

CXP = 8
CYP = 4
CAP = 4
N_PX = 8
N_PZ = 16
N_DEV = 128
BOTH = ("px", "pz")
RESIDUE = [0, 8] + [g for g in range(1, 8) for _ in range(2)]
BF = jnp.bfloat16
F32 = jnp.float32
VMEM = pl.BlockSpec(memory_space=pltpu.VMEM)
PARAMS = pltpu.CompilerParams(vmem_limit_bytes=48 << 20)


def split_table(table):
    high = table.astype(np.float32).astype(ml_dtypes.bfloat16)
    low = (table - high.astype(np.float64)).astype(ml_dtypes.bfloat16)
    return high, low


def z_tables():
    device = np.arange(N_DEV)
    q = 8 * (device % N_PZ) + device // N_PZ
    l = np.arange(128)
    wave = []
    for r in range(9):
        angle = 2.0 * np.pi * ((q[:, None] * 16 + r) * l[None, :] % 2048) / 2048.0
        wave.append(np.concatenate([np.cos(angle), np.sin(angle)], axis=1))
    wave = np.stack(wave)
    mix = np.zeros((8, 4, 8, 2, 4, 16, 8))
    for c in range(8):
        for kk in range(16):
            r = RESIDUE[kk]
            angle = 2.0 * np.pi * ((r * c) % 16) / 16.0
            if kk < 2:
                cosine_part, sine_part, weight = np.cos(angle), np.cos(angle), 1.0
            elif kk % 2 == 0:
                cosine_part, sine_part, weight = np.cos(angle), -np.sin(angle), 2.0
            else:
                cosine_part, sine_part, weight = np.sin(angle), np.cos(angle), 2.0
            scale = np.sqrt(weight / 2048.0)
            for b in range(4):
                for a in range(8):
                    mix[c, b, a, 0, b, kk, a] = cosine_part * scale
                    mix[c, b, a, 1, b, kk, a] = sine_part * scale
    return wave, mix.reshape(256, 1024)


def plane_table():
    angle = 2.0 * np.pi * (np.arange(64)[:, None] * np.arange(128)[None, :] % 128) / 128.0
    return (np.cos(angle) + np.sin(angle)) / np.sqrt(128.0)


def iota(shape, axis):
    return lax.broadcasted_iota(jnp.int32, shape, axis)


def two(x):
    high = x.astype(BF)
    return high, (x - high.astype(F32)).astype(BF)


def three(x):
    high = x.astype(BF)
    rest = x - high.astype(F32)
    middle = rest.astype(BF)
    return high, middle, (rest - middle.astype(F32)).astype(BF)


def dot(a, b, a_axis=1, b_axis=0):
    return lax.dot_general(a, b, (((a_axis,), (b_axis,)), ((), ())), preferred_element_type=F32)


def pack_kernel(charge_ref, dest_ref, ids_ref, send_ref, place_ref):
    dest = jnp.broadcast_to(dest_ref[...], (256, 256))
    row, col = iota((256, 256), 0), iota((256, 256), 1)
    dest_f = dest.astype(F32)
    dest_col = jnp.sum(jnp.where(row == col, dest_f, 0.0), axis=1, keepdims=True)
    earlier = (dest_col == dest_f) & (row < col)
    rank = jnp.sum(jnp.where(earlier, 1.0, 0.0), axis=0, keepdims=True)
    place_ref[...] = dest_f[0:1] * CAP + rank
    here = iota((128, 256), 0) == dest[:128]
    rank = jnp.broadcast_to(rank, (128, 256))
    ids = jnp.broadcast_to(ids_ref[...], (128, 256)).astype(F32)
    lane = iota((128, 128), 1)
    named = jnp.zeros((128, 128), F32)
    hots = []
    for slot in range(CAP):
        chosen = here & (rank == slot)
        hots.append(jnp.where(chosen, 1.0, 0.0).astype(BF))
        number = jnp.sum(jnp.where(chosen, ids + 1.0, 0.0), axis=1, keepdims=True) - 1.0
        named = jnp.where(lane == slot, number, named)
    parts = jnp.concatenate(three(charge_ref[...]), axis=1)
    moved = dot(jnp.concatenate(hots, axis=0), parts)
    moved = moved[:, :128] + moved[:, 128:256] + moved[:, 256:]
    for slot in range(CAP):
        send_ref[pl.ds(slot, 128, stride=5), :] = moved[slot * 128 : (slot + 1) * 128]
    send_ref[pl.ds(4, 128, stride=5), :] = named


def slot_hots(recv_ref):
    lane = iota((128, 256), 1)
    block = ((lane % 8) * 4 + (lane // 8) % 4) * 8 + lane // 32
    block = block.astype(F32)
    names = recv_ref[pl.ds(4, 128, stride=5), :]
    hots = [jnp.where(names[:, s : s + 1] == block, 1.0, 0.0).astype(BF) for s in range(CAP)]
    return jnp.concatenate(hots, axis=0)


def lane_residue(shape):
    kk = (iota(shape, 1) // 8) % 16
    return jnp.where(kk == 0, 0, jnp.where(kk == 1, 8, kk // 2))


def z_forward_kernel(recv_ref, wave_hi_ref, wave_lo_ref, mix_hi_ref, mix_lo_ref, out_ref):
    hots = slot_hots(recv_ref)
    rows = jnp.concatenate([recv_ref[pl.ds(s, 128, stride=5), :] for s in range(CAP)], axis=0)
    parts = jnp.concatenate(three(rows), axis=1)
    field = dot(parts, hots, 0, 0)
    field = field[:128] + field[128:256] + field[256:]
    high, low = two(field)
    mixed = dot(high, mix_hi_ref[...]) + dot(low, mix_hi_ref[...]) + dot(high, mix_lo_ref[...])
    mixed = jnp.concatenate([mixed[:, :512], mixed[:, 512:]], axis=0)
    high, low = two(mixed)
    residue = lane_residue((128, 512))
    out = jnp.zeros((128, 512), F32)
    for r in range(9):
        rows = slice(r * 128, (r + 1) * 128)
        block = dot(wave_hi_ref[rows, :], high) + dot(wave_hi_ref[rows, :], low) + dot(wave_lo_ref[rows, :], high)
        out = jnp.where(residue == r, block, out)
    for b in range(CYP):
        out_ref[pl.ds(b, 128, stride=4), :] = out[:, b * 128 : (b + 1) * 128]


def plane_kernel(spec_ref, green_ref, fwd_ref, back_ref, back_lo_ref, out_ref, first_ref, second_ref):
    fwd = fwd_ref[...]
    back, back_lo = back_ref[...], back_lo_ref[...]
    for i in range(N_PX):
        high, low = two(spec_ref[i * 64 : (i + 1) * 64, :])
        turned = dot(jnp.concatenate([high, low, high], axis=0), fwd, 0, 0)
        for kk in range(16):
            first_ref[kk, i * 8 : (i + 1) * 8, :] = turned[kk * 8 : (kk + 1) * 8]
    for kk in range(16):
        high, low = two(first_ref[kk])
        full = dot(jnp.concatenate([high, low, high], axis=0), fwd, 0, 0)
        full = full * green_ref[pl.ds(RESIDUE[kk], 128, stride=16), :]
        high, low = two(full)
        second_ref[kk] = dot(back, jnp.concatenate([high, low], axis=1), 1, 1) + dot(back_lo, high, 1, 1)
    for i in range(N_PX):
        rows = jnp.concatenate([second_ref[kk, i * 8 : (i + 1) * 8, :] for kk in range(16)], axis=0)
        high, low = two(rows)
        out_ref[i * 64 : (i + 1) * 64, :] = dot(back, jnp.concatenate([high, low], axis=1), 1, 1) + dot(
            back_lo, high, 1, 1
        )


def z_back_kernel(spec_ref, recv_ref, wave_hi_ref, wave_lo_ref, mix_hi_ref, mix_lo_ref, out_ref):
    lines = jnp.concatenate([spec_ref[pl.ds(b, 128, stride=4), :] for b in range(CYP)], axis=1)
    high, low = two(lines)
    both = jnp.concatenate([high, low], axis=0)
    residue = lane_residue((256, 512))
    acc = jnp.zeros((256, 512), F32)
    for r in range(9):
        rows = slice(r * 256, (r + 1) * 256)
        block = dot(wave_hi_ref[rows, :], both) + dot(wave_lo_ref[rows, :], high)
        acc = jnp.where(residue == r, block, acc)
    high, low = two(jnp.concatenate([acc[:128], acc[128:]], axis=1))
    field = dot(high, mix_hi_ref[...], 1, 1) + dot(low, mix_hi_ref[...], 1, 1) + dot(high, mix_lo_ref[...], 1, 1)
    parts = jnp.concatenate(three(field), axis=0)
    rows = dot(slot_hots(recv_ref), parts, 1, 1)
    rows = rows[:, :128] + rows[:, 128:256] + rows[:, 256:]
    for s in range(CAP):
        out_ref[pl.ds(s, 128, stride=4), :] = rows[s * 128 : (s + 1) * 128]


def unpack_kernel(back_ref, place_ref, out_ref):
    row, col = iota((256, 256), 0), iota((256, 256), 1)
    place = jnp.broadcast_to(place_ref[...], (256, 256))
    place = jnp.sum(jnp.where(row == col, place, 0.0), axis=1, keepdims=True).astype(jnp.int32)
    hots = jnp.where(iota((256, 512), 1) == place, 1.0, 0.0).astype(BF)
    parts = jnp.concatenate(three(back_ref[...]), axis=1)
    rows = dot(hots, parts)
    out_ref[...] = rows[:, :128] + rows[:, 128:256] + rows[:, 256:]


def green_kernel(green_ref, out_ref):
    for k2 in range(16):
        turned = green_ref[:, k2, :].T
        for i in range(N_PX):
            out_ref[i, k2 * 16 : (k2 + 1) * 16, :] = turned[i * 16 : (i + 1) * 16]


def call(kernel, shape, scratch=(), dtype=F32):
    return pl.pallas_call(
        kernel,
        out_shape=jax.tree.map(lambda s: jax.ShapeDtypeStruct(s, dtype), shape, is_leaf=lambda s: isinstance(s, tuple)),
        scratch_shapes=list(scratch),
        compiler_params=PARAMS,
        name=kernel.__name__,
    )


def all_to_all(x, axes):
    return lax.all_to_all(x, axes, split_axis=0, concat_axis=0, tiled=True)


def local(charge, dest, local_ids, green_hat):
    wave, mix = z_tables()
    wave_hi, wave_lo = split_table(wave.reshape(9 * 128, 256))
    mix_hi, mix_lo = split_table(mix)
    back = wave.reshape(9, 128, 2, 128).transpose(0, 2, 3, 1).reshape(9 * 256, 128)
    back_hi, back_lo = split_table(back)
    back_hi = np.concatenate([back_hi, back_hi], axis=1)
    plane = plane_table()
    plane_hi, plane_lo = split_table(plane)
    plane_fwd = np.concatenate([plane_hi, plane_hi, plane_lo], axis=0)
    plane_back = np.concatenate([plane_hi, plane_hi], axis=1)

    turned = call(green_kernel, (8, 256, 128))(green_hat)
    green = all_to_all(turned, "px").reshape(2048, 128)

    send, place = call(pack_kernel, [(640, 128), (1, 256)])(
        charge, dest.reshape(1, 256), local_ids.reshape(1, 256)
    )
    recv = all_to_all(send.reshape(N_DEV, 5, 128), BOTH).reshape(640, 128)
    lines = call(z_forward_kernel, (512, 128))(recv, wave_hi, wave_lo, mix_hi, mix_lo)
    planes = all_to_all(lines.reshape(N_DEV, 4, 128), BOTH).reshape(512, 128)
    planes = call(
        plane_kernel,
        (512, 128),
        [pltpu.VMEM((16, 64, 128), F32), pltpu.VMEM((16, 64, 128), F32)],
    )(planes, green, plane_fwd, plane_back, plane_lo)
    lines = all_to_all(planes.reshape(N_DEV, 4, 128), BOTH).reshape(512, 128)
    rows = call(z_back_kernel, (512, 128))(lines, recv, back_hi, back_lo, mix_hi, mix_lo)
    rows = all_to_all(rows.reshape(N_DEV, 4, 128), BOTH).reshape(512, 128)
    return call(unpack_kernel, (256, 128))(rows, place)


def solution(mesh):
    return jax.shard_map(
        local,
        mesh=mesh,
        in_specs=(
            P(BOTH, None),
            P(BOTH, None),
            P(BOTH),
            P(None, "px", "pz"),
        ),
        out_specs=P(BOTH, None),
        check_vma=False,
    )
```

time: 1050 us -> 104 us (0.10)
  waiting for transfers between devices: 725 us -> 9.41 us
  matrix products: 156 us -> 0 us
  local copies, waits for them, and re-layouts: 47.1 us -> 4.67 us
  blocking collectives: 94.5 us -> 73.5 us
  between operations: 13.9 us -> 0.15 us
  other arithmetic: 12.1 us -> 0 us
  Pallas kernels: 0 us -> 11.6 us
    reduce_scatter x1 -> x0, waiting for transfers between devices: 646 us -> none  [local(): lax.psum_scatter(dense, ('px', 'pz'), scatter_dimension=0, tiled=True)]
    dot_general x20 -> x0, matrix products: 156 us -> none  [the longest x1 36.1 us: solve_field(): jnp.einsum('xyz,zk->xyk', field, sine, precision=lax.Precision.HIGHEST)]
    all_gather x1 -> x0, waiting for transfers between devices: 79.6 us -> none  [local(): whole = lax.all_gather(phi_blocks, ('px', 'pz'), axis=0, tiled=True)]
    all_to_all x4, blocking collectives: 94.5 us -> 73.5 us  [all_to_all(): return lax.all_to_all(x, axes, split_axis=0, concat_axis=0, tiled=True)]
    unnamed x4 -> x26, local copies, waits for them, and re-layouts: 23.3 us -> 3.54 us
    pallas_call x0 -> x6, Pallas kernels: none -> 11.6 us  [the longest x1 3.84 us: local(): call(plane_kernel, (512, 128), [pltpu.VMEM((16, 64, 128), F32), pltpu.VME...]
  transfers between devices with their start and end apart: 2 -> 1, of which waited for: 2 -> 1; matrix products, arithmetic and copies ran while one was open for 0% -> 0% of each run, Pallas kernels for 0% -> 1%
where the time goes in v1:
time: 104 us
  blocking collectives  73.5 us (71%)
  Pallas kernels  11.6 us (11%)
  waiting for transfers between devices  9.41 us (9%)
  starting transfers between devices  4.73 us (5%)
  local copies, waits for them, and re-layouts  4.67 us (4%)
    all_to_all x4, blocking collectives, all_to_all(): return lax.all_to_all(x, axes, split_axis=0, concat_axis=0, tiled=True)  73.5 us
    all_to_all x1, waiting for transfers between devices, all_to_all(): return lax.all_to_all(x, axes, split_axis=0, concat_axis=0, tiled=True)  9.41 us
    all_to_all x1, starting transfers between devices, all_to_all(): return lax.all_to_all(x, axes, split_axis=0, concat_axis=0, tiled=True)  4.73 us
    pallas_call x1, Pallas kernels, local(): call(plane_kernel, (512, 128), [pltpu.VMEM((16, 64, 128), F32), pltpu.VME...  3.84 us
    unnamed x26, local copies, waits for them, and re-layouts  3.54 us
    pallas_call x1, Pallas kernels, local(): call(z_back_kernel, (512, 128))  2.89 us
    pallas_call x1, Pallas kernels, local(): call(z_forward_kernel, (512, 128))(recv, wave_hi, wave_lo, mix_hi, mix_lo)  2.77 us
  transfers between devices with their start and end apart: 1, of which 1 were waited for; matrix products, arithmetic and copies ran while one was open for 0% of the time, Pallas kernels for 1%

profile of v1, /device:TPU:1, one launch (start us, length us, event | category | flops | bytes accessed | tf_op | source)
XLA Modules:
  0.0 104.0 jit_solution(6200948736819777386)
XLA Ops:
  0.0 0.0 copy-start.7
  0.0 0.9 copy-done.7
  0.9 0.0 copy-start.11
  0.9 0.7 copy-done.11
  1.6 0.0 copy-start.12
  1.6 0.7 copy-done.12
  2.3 0.4 pack_kernel.1
  2.7 0.0 copy-start
  2.7 0.0 copy-start.1
  2.7 0.0 copy-start.5
  2.7 0.0 copy-start.6
  2.7 0.1 reshape.35
  2.8 24.7 %all_to_all.25 = f32[128,5,128]{2,1,0:T(8,128)} all-to-all(f32[128,5,128]{2,1,0:T(8,128)S(1)} %reshape.35), channel_id=1, replica_groups=mesh['px'=8,'pz'=16] {'px','pz'}, dimensions={0} | all-to-all | bytes 655360 | tf_op jit(solution)/shard_map/all_to_all | solution.py:213
  27.5 1.1 %reshape.36.recv_ref = f32[640,128]{1,0:T(8,128)S(1)} reshape(f32[128,5,128]{2,1,0:T(8,128)} %all_to_all.25) | data formatting | bytes 655360 | tf_op jit(solution)/shard_map/reshape | solution.py:234
  28.6 0.0 copy-done
  28.6 0.0 copy-done.1
  28.7 0.0 copy-done.5
  28.7 0.0 copy-done.6
  28.7 2.8 %z_forward_kernel.1 = f32[512,128]{1,0:T(8,128)} custom-call(f32[640,128]{1,0:T(8,128)S(1)} %reshape.36.recv_ref, bf16[1152,256]{1,0:T(8,128)(2,1)S(1)} %copy-done.6, bf16[1152,256]{1,0:T(8,128)(2,1)S(1)} %copy-done.5, bf16[256,1024]{1,0:T(8,128)(2,1)S(1)} %copy-done.1, bf16[256,1024]{1,0:T(8,128)(2,1)S(1)} %copy-done), custom_call_target="tpu_custom_call" | custom-call | tf_op jit(solution)/shard_map/z_forward_kernel/pallas_call | solution.py:235
  31.4 4.7 %all-to-all-start.1 = ((f32[128,4,128]{2,1,0:T(4,128)}), f32[128,4,128]{2,1,0:T(4,128)S(1)}, u32[]{:S(2)}, u32[]{:S(2)}) async-start(f32[128,4,128]{2,1,0:T(4,128)} %bitcast.2), calls=%async_computation.1 | async-start | bytes 524288 | tf_op jit(solution)/shard_map/all_to_all | solution.py:213
  36.2 0.0 copy-start.3
  36.2 1.2 %copy-done.3 = f32[128,16,128]{2,1,0:T(8,128)S(1)} copy-done((f32[128,16,128]{2,1,0:T(8,128)S(1)}, f32[128,16,128]{2,1,0:T(8,128)}, u32[]{:S(2)}) %copy-start.3) | copy-done | bytes 1048600
  37.4 0.6 green_kernel.1
  38.0 0.0 copy-start.8
  38.0 0.0 copy-start.9
  38.1 0.0 copy-start.10
  38.1 9.4 %all-to-all-done.1 = f32[128,4,128]{2,1,0:T(4,128)S(1)} async-done(((f32[128,4,128]{2,1,0:T(4,128)}), f32[128,4,128]{2,1,0:T(4,128)S(1)}, u32[]{:S(2)}, u32[]{:S(2)}) %all-to-all-start.1) | async-done | bytes 262176 | tf_op jit(solution)/shard_map/all_to_all | solution.py:213
  47.5 18.3 %all_to_all.26 = f32[8,256,128]{2,1,0:T(8,128)S(1)} all-to-all(f32[8,256,128]{2,1,0:T(8,128)S(1)} %green_kernel.1), channel_id=1, replica_groups=mesh['px'=8,'pz'=16] {'px'}, dimensions={0} | all-to-all | bytes 2097152 | tf_op jit(solution)/shard_map/all_to_all | solution.py:213
  65.7 0.0 copy-start.2
  65.7 0.0 copy-start.4
  65.7 0.0 copy-done.8
  65.7 0.0 copy-done.9
  65.8 0.0 copy-done.10
  65.8 3.8 %plane_kernel.1 = f32[512,128]{1,0:T(8,128)S(1)} custom-call(f32[512,128]{1,0:T(8,128)S(1)} %bitcast.12, f32[2048,128]{1,0:T(8,128)S(1)} %bitcast.9, bf16[192,128]{1,0:T(8,128)(2,1)S(1)} %copy-done.8, bf16[64,256]{1,0:T(8,128)(2,1)S(1)} %copy-done.9, bf16[64,128]{1,0:T(8,128)(2,1)S(1)} %copy-done.10), custom_call_target="tpu_custom_call" | custom-call | tf_op jit(solution)/shard_map/plane_kernel/pallas_call | solution.py:237
  69.6 15.3 %all_to_all.27 = f32[128,4,128]{2,1,0:T(4,128)S(1)} all-to-all(f32[128,4,128]{2,1,0:T(4,128)S(1)} %bitcast.13), channel_id=1, replica_groups=mesh['px'=8,'pz'=16] {'px','pz'}, dimensions={0} | all-to-all | bytes 524288 | tf_op jit(solution)/shard_map/all_to_all | solution.py:213
  84.9 0.0 copy-done.2
  84.9 0.0 copy-done.4
  84.9 2.9 %z_back_kernel.1 = f32[512,128]{1,0:T(8,128)S(1)} custom-call(f32[512,128]{1,0:T(8,128)S(1)} %bitcast.10, f32[640,128]{1,0:T(8,128)S(1)} %reshape.36.recv_ref, bf16[2304,256]{1,0:T(8,128)(2,1)S(1)} %copy-done.2, bf16[2304,128]{1,0:T(8,128)(2,1)S(1)} %copy-done.4, bf16[256,1024]{1,0:T(8,128)(2,1)S(1)} %copy-done.1, bf16[256,1024]{1,0:T(8,128)(2,1)S(1)} %copy-done), custom_call_target="tpu_custom_call" | custom-call | tf_op jit(solution)/shard_map/z_back_kernel/pallas_call | solution.py:243
  87.8 15.2 %all_to_all.28 = f32[128,4,128]{2,1,0:T(4,128)S(1)} all-to-all(f32[128,4,128]{2,1,0:T(4,128)S(1)} %bitcast.11), channel_id=1, replica_groups=mesh['px'=8,'pz'=16] {'px','pz'}, dimensions={0} | all-to-all | bytes 524288 | tf_op jit(solution)/shard_map/all_to_all | solution.py:213
  103.0 1.0 unpack_kernel.1
Async XLA Ops:
  0.0 0.9 copy-start.7
  0.9 0.7 copy-start.11
  1.6 0.7 copy-start.12
  2.7 25.9 %copy-start = (bf16[256,1024]{1,0:T(8,128)(2,1)S(1)}, bf16[256,1024]{1,0:T(8,128)(2,1)}, u32[]{:S(2)}) copy-start(bf16[256,1024]{1,0:T(8,128)(2,1)} %constant.21.clone.mix_lo_ref) | copy-start | bytes 1572868
  2.7 25.9 %copy-start.1 = (bf16[256,1024]{1,0:T(8,128)(2,1)S(1)}, bf16[256,1024]{1,0:T(8,128)(2,1)}, u32[]{:S(2)}) copy-start(bf16[256,1024]{1,0:T(8,128)(2,1)} %constant.20.clone.mix_hi_ref) | copy-start | bytes 1572868
  2.7 25.9 %copy-start.5 = (bf16[1152,256]{1,0:T(8,128)(2,1)S(1)}, bf16[1152,256]{1,0:T(8,128)(2,1)}, u32[]{:S(2)}) copy-start(bf16[1152,256]{1,0:T(8,128)(2,1)} %constant.19.clone.wave_lo_ref) | copy-start | bytes 1769476
  2.7 25.9 %copy-start.6 = (bf16[1152,256]{1,0:T(8,128)(2,1)S(1)}, bf16[1152,256]{1,0:T(8,128)(2,1)}, u32[]{:S(2)}) copy-start(bf16[1152,256]{1,0:T(8,128)(2,1)} %constant.18.clone.wave_hi_ref) | copy-start | bytes 1769476
  31.4 16.0 %all-to-all-start.1 = ((f32[128,4,128]{2,1,0:T(4,128)}), f32[128,4,128]{2,1,0:T(4,128)S(1)}, u32[]{:S(2)}, u32[]{:S(2)}) async-start(f32[128,4,128]{2,1,0:T(4,128)} %bitcast.2), calls=%async_computation.1 | async-start | bytes 524288 | tf_op jit(solution)/shard_map/all_to_all | solution.py:213
  36.2 1.2 %copy-start.3 = (f32[128,16,128]{2,1,0:T(8,128)S(1)}, f32[128,16,128]{2,1,0:T(8,128)}, u32[]{:S(2)}) copy-start(f32[128,16,128]{2,1,0:T(8,128)} %green_ref.1) | copy-start | bytes 3145732
  38.0 27.7 %copy-start.8 = (bf16[192,128]{1,0:T(8,128)(2,1)S(1)}, bf16[192,128]{1,0:T(8,128)(2,1)}, u32[]{:S(2)}) copy-start(bf16[192,128]{1,0:T(8,128)(2,1)} %constant.22.clone.fwd_ref) | copy-start | bytes 147460
  38.0 27.7 %copy-start.9 = (bf16[64,256]{1,0:T(8,128)(2,1)S(1)}, bf16[64,256]{1,0:T(8,128)(2,1)}, u32[]{:S(2)}) copy-start(bf16[64,256]{1,0:T(8,128)(2,1)} %constant.23.clone.back_ref) | copy-start | bytes 98308
  38.1 27.7 %copy-start.10 = (bf16[64,128]{1,0:T(8,128)(2,1)S(1)}, bf16[64,128]{1,0:T(8,128)(2,1)}, u32[]{:S(2)}) copy-start(bf16[64,128]{1,0:T(8,128)(2,1)} %constant.24.clone.back_lo_ref) | copy-start | bytes 49156
  65.7 19.2 %copy-start.2 = (bf16[2304,256]{1,0:T(8,128)(2,1)S(1)}, bf16[2304,256]{1,0:T(8,128)(2,1)}, u32[]{:S(2)}) copy-start(bf16[2304,256]{1,0:T(8,128)(2,1)} %constant.25.clone.wave_hi_ref) | copy-start | bytes 3538948
  65.7 19.2 %copy-start.4 = (bf16[2304,128]{1,0:T(8,128)(2,1)S(1)}, bf16[2304,128]{1,0:T(8,128)(2,1)}, u32[]{:S(2)}) copy-start(bf16[2304,128]{1,0:T(8,128)(2,1)} %constant.26.clone.wave_lo_ref) | copy-start | bytes 1769476

commit v2 on v1

--- a/solution.py
+++ b/solution.py
@@ -18,7 +18,8 @@
 BF = jnp.bfloat16
 F32 = jnp.float32
 VMEM = pl.BlockSpec(memory_space=pltpu.VMEM)
-PARAMS = pltpu.CompilerParams(vmem_limit_bytes=48 << 20)
+HBM = pl.BlockSpec(memory_space=pltpu.HBM)
+PARAMS = pltpu.CompilerParams(vmem_limit_bytes=16 << 20)
 
 
 def split_table(table):
@@ -60,6 +61,21 @@
     return (np.cos(angle) + np.sin(angle)) / np.sqrt(128.0)
 
 
+def pair_table(half):
+    k = 64 * half + np.arange(64)
+    cell = np.arange(64)[:, None]
+    cosine = np.cos(2.0 * np.pi * (cell * k[None, :] % 128) / 128.0) * np.sqrt(2.0)
+    sine = np.sin(2.0 * np.pi * (cell * k[None, :] % 128) / 128.0) * np.sqrt(2.0)
+    cosine[:, 0] = np.cos(np.pi * half * np.arange(64))
+    sine[:, 0] = np.cos(np.pi * (1 - half) * np.arange(64))
+    return np.concatenate([cosine, sine], axis=1) / np.sqrt(128.0)
+
+
+def stacked(table):
+    high, low = split_table(table)
+    return np.concatenate([high, high, low], axis=0), np.concatenate([high, high, low], axis=1)
+
+
 def iota(shape, axis):
     return lax.broadcasted_iota(jnp.int32, shape, axis)
 
@@ -80,7 +96,23 @@
     return lax.dot_general(a, b, (((a_axis,), (b_axis,)), ((), ())), preferred_element_type=F32)
 
 
-def pack_kernel(charge_ref, dest_ref, ids_ref, send_ref, place_ref):
+def pack_kernel(
+    charge_any, dest_any, ids_any, green_any, send_ref, place_ref, charge_ref, dest_ref, ids_ref, plane_ref, sems
+):
+    moves = [
+        pltpu.make_async_copy(source, target, sems.at[n])
+        for n, (source, target) in enumerate(
+            [
+                (dest_any, dest_ref),
+                (ids_any, ids_ref),
+                (charge_any, charge_ref),
+                (green_any.at[:, 0, :], plane_ref),
+            ]
+        )
+    ]
+    for move in moves:
+        move.start()
+    moves[0].wait()
     dest = jnp.broadcast_to(dest_ref[...], (256, 256))
     row, col = iota((256, 256), 0), iota((256, 256), 1)
     dest_f = dest.astype(F32)
@@ -90,15 +122,18 @@
     place_ref[...] = dest_f[0:1] * CAP + rank
     here = iota((128, 256), 0) == dest[:128]
     rank = jnp.broadcast_to(rank, (128, 256))
+    moves[1].wait()
     ids = jnp.broadcast_to(ids_ref[...], (128, 256)).astype(F32)
     lane = iota((128, 128), 1)
-    named = jnp.zeros((128, 128), F32)
+    moves[3].wait()
+    named = plane_ref[...]
     hots = []
     for slot in range(CAP):
         chosen = here & (rank == slot)
         hots.append(jnp.where(chosen, 1.0, 0.0).astype(BF))
         number = jnp.sum(jnp.where(chosen, ids + 1.0, 0.0), axis=1, keepdims=True) - 1.0
-        named = jnp.where(lane == slot, number, named)
+        named = jnp.where(lane == 9 + slot, number, named)
+    moves[2].wait()
     parts = jnp.concatenate(three(charge_ref[...]), axis=1)
     moved = dot(jnp.concatenate(hots, axis=0), parts)
     moved = moved[:, :128] + moved[:, 128:256] + moved[:, 256:]
@@ -112,7 +147,7 @@
     block = ((lane % 8) * 4 + (lane // 8) % 4) * 8 + lane // 32
     block = block.astype(F32)
     names = recv_ref[pl.ds(4, 128, stride=5), :]
-    hots = [jnp.where(names[:, s : s + 1] == block, 1.0, 0.0).astype(BF) for s in range(CAP)]
+    hots = [jnp.where(names[:, 9 + s : 10 + s] == block, 1.0, 0.0).astype(BF) for s in range(CAP)]
     return jnp.concatenate(hots, axis=0)
 
 
@@ -121,16 +156,25 @@
     return jnp.where(kk == 0, 0, jnp.where(kk == 1, 8, kk // 2))
 
 
-def z_forward_kernel(recv_ref, wave_hi_ref, wave_lo_ref, mix_hi_ref, mix_lo_ref, out_ref):
+def z_forward_kernel(recv_ref, *refs):
+    tables, out_ref, copies, sems = refs[:4], refs[4], refs[5:9], refs[9]
+    moves = [pltpu.make_async_copy(tables[n], copies[n], sems.at[n]) for n in range(4)]
+    for move in moves:
+        move.start()
+    mix_hi_ref, mix_lo_ref, wave_hi_ref, wave_lo_ref = copies
     hots = slot_hots(recv_ref)
     rows = jnp.concatenate([recv_ref[pl.ds(s, 128, stride=5), :] for s in range(CAP)], axis=0)
     parts = jnp.concatenate(three(rows), axis=1)
     field = dot(parts, hots, 0, 0)
     field = field[:128] + field[128:256] + field[256:]
     high, low = two(field)
+    moves[0].wait()
+    moves[1].wait()
     mixed = dot(high, mix_hi_ref[...]) + dot(low, mix_hi_ref[...]) + dot(high, mix_lo_ref[...])
     mixed = jnp.concatenate([mixed[:, :512], mixed[:, 512:]], axis=0)
     high, low = two(mixed)
+    moves[2].wait()
+    moves[3].wait()
     residue = lane_residue((128, 512))
     out = jnp.zeros((128, 512), F32)
     for r in range(9):
@@ -138,28 +182,54 @@
         block = dot(wave_hi_ref[rows, :], high) + dot(wave_hi_ref[rows, :], low) + dot(wave_lo_ref[rows, :], high)
         out = jnp.where(residue == r, block, out)
     for b in range(CYP):
-        out_ref[pl.ds(b, 128, stride=4), :] = out[:, b * 128 : (b + 1) * 128]
-
-
-def plane_kernel(spec_ref, green_ref, fwd_ref, back_ref, back_lo_ref, out_ref, first_ref, second_ref):
-    fwd = fwd_ref[...]
-    back, back_lo = back_ref[...], back_lo_ref[...]
+        out_ref[pl.ds(b, 128, stride=5), :] = out[:, b * 128 : (b + 1) * 128]
+    ends = recv_ref[pl.ds(4, 128, stride=5), :]
+    relayed = []
     for i in range(N_PX):
-        high, low = two(spec_ref[i * 64 : (i + 1) * 64, :])
-        turned = dot(jnp.concatenate([high, low, high], axis=0), fwd, 0, 0)
+        source = 64 if i < 4 else 0
+        rows = ends[source : source + 16]
+        relayed.append(pltpu.roll(rows, 128 - 16 * i, 1) if i else rows)
+    out_ref[pl.ds(4, 128, stride=5), :] = jnp.concatenate(relayed, axis=0)
+
+
+def plane_kernel(spec_ref, *refs):
+    pieces, refs = refs[:4], refs[4:]
+    x_fwd_ref, x_back_ref, y_fwd_ref, y_back_ref, out_ref, green_ref, first_ref, second_ref, sems = refs
+    me = lax.axis_index("px")
+    half, place = me // 4, me % 4
+    moves = []
+    for n in range(4):
+        source = jnp.bitwise_xor(place, n)
+        start = pl.multiple_of(source * 16, 16)
+        moves.append(pltpu.make_async_copy(pieces[n], green_ref.at[:, pl.ds(start, 16), :], sems.at[n]))
+    for move in moves:
+        move.start()
+    ends = spec_ref[pl.ds(4, 128, stride=5), :].T
+    y_fwd, y_back, y_low = y_fwd_ref[half], y_back_ref[half, :, :256], y_back_ref[half, :, 256:]
+    x_fwd, x_back, x_low = x_fwd_ref[...], x_back_ref[:, :256], x_back_ref[:, 256:]
+    for i in range(N_PX):
+        rows = [spec_ref[pl.ds(i * 80 + b, 16, stride=5), :] for b in range(CYP)]
+        high, low = two(jnp.concatenate(rows, axis=0))
+        turned = dot(jnp.concatenate([high, low, high], axis=0), y_fwd, 0, 0)
         for kk in range(16):
             first_ref[kk, i * 8 : (i + 1) * 8, :] = turned[kk * 8 : (kk + 1) * 8]
+    for move in moves:
+        move.wait()
+    top = iota((64, 128), 0) == 0
     for kk in range(16):
         high, low = two(first_ref[kk])
-        full = dot(jnp.concatenate([high, low, high], axis=0), fwd, 0, 0)
-        full = full * green_ref[pl.ds(RESIDUE[kk], 128, stride=16), :]
+        full = dot(jnp.concatenate([high, low, high], axis=0), x_fwd, 0, 0)
+        r = RESIDUE[kk]
+        green = green_ref[r]
+        other = jnp.where(top, ends[r : r + 1, :], green)
+        full = jnp.concatenate([full[:64] * green, full[64:] * other], axis=0)
         high, low = two(full)
-        second_ref[kk] = dot(back, jnp.concatenate([high, low], axis=1), 1, 1) + dot(back_lo, high, 1, 1)
+        second_ref[kk] = dot(x_back, jnp.concatenate([high, low], axis=1), 1, 1) + dot(x_low, high, 1, 1)
     for i in range(N_PX):
         rows = jnp.concatenate([second_ref[kk, i * 8 : (i + 1) * 8, :] for kk in range(16)], axis=0)
         high, low = two(rows)
-        out_ref[i * 64 : (i + 1) * 64, :] = dot(back, jnp.concatenate([high, low], axis=1), 1, 1) + dot(
-            back_lo, high, 1, 1
+        out_ref[i * 64 : (i + 1) * 64, :] = dot(y_back, jnp.concatenate([high, low], axis=1), 1, 1) + dot(
+            y_low, high, 1, 1
         )
 
 
@@ -192,16 +262,30 @@
     out_ref[...] = rows[:, :128] + rows[:, 128:256] + rows[:, 256:]
 
 
-def green_kernel(green_ref, out_ref):
+def green_kernel(green_any, *refs):
+    out_refs, (green_ref, turned_ref, piece_ref, sems) = refs[:4], refs[4:]
+    me = lax.axis_index("px")
+    move = pltpu.make_async_copy(green_any, green_ref, sems.at[0])
+    move.start()
+    starts = [
+        pl.multiple_of((me - me % 4 + jnp.bitwise_xor(me % 4, n)) * 16, 16) for n in range(4)
+    ]
+    move.wait()
     for k2 in range(16):
-        turned = green_ref[:, k2, :].T
-        for i in range(N_PX):
-            out_ref[i, k2 * 16 : (k2 + 1) * 16, :] = turned[i * 16 : (i + 1) * 16]
-
-
-def call(kernel, shape, scratch=(), dtype=F32):
+        turned_ref[...] = green_ref[:, k2, :].T
+        for n in range(4):
+            piece_ref[n, pl.ds(k2, 9, stride=16), :] = turned_ref[pl.ds(starts[n], 9), :]
+    moves = [pltpu.make_async_copy(piece_ref.at[n], out_refs[n], sems.at[n]) for n in range(4)]
+    for move in moves:
+        move.start()
+    for move in moves:
+        move.wait()
+
+
+def call(kernel, shape, scratch=(), dtype=F32, **specs):
     return pl.pallas_call(
         kernel,
+        **specs,
         out_shape=jax.tree.map(lambda s: jax.ShapeDtypeStruct(s, dtype), shape, is_leaf=lambda s: isinstance(s, tuple)),
         scratch_shapes=list(scratch),
         compiler_params=PARAMS,
@@ -220,25 +304,67 @@
     back = wave.reshape(9, 128, 2, 128).transpose(0, 2, 3, 1).reshape(9 * 256, 128)
     back_hi, back_lo = split_table(back)
     back_hi = np.concatenate([back_hi, back_hi], axis=1)
-    plane = plane_table()
-    plane_hi, plane_lo = split_table(plane)
-    plane_fwd = np.concatenate([plane_hi, plane_hi, plane_lo], axis=0)
-    plane_back = np.concatenate([plane_hi, plane_hi], axis=1)
-
-    turned = call(green_kernel, (8, 256, 128))(green_hat)
-    green = all_to_all(turned, "px").reshape(2048, 128)
-
-    send, place = call(pack_kernel, [(640, 128), (1, 256)])(
-        charge, dest.reshape(1, 256), local_ids.reshape(1, 256)
+    x_fwd, x_back = stacked(plane_table())
+    order = np.arange(64).reshape(N_PZ, CYP).T.reshape(64)
+    y_fwd, y_back = (np.stack(tables) for tables in zip(stacked(pair_table(0)), stacked(pair_table(1))))
+    y_fwd = y_fwd.reshape(2, 3, 64, 128)[:, :, order].reshape(2, 192, 128)
+
+    charge, dest, local_ids, green_hat = (
+        pltpu.with_memory_space_constraint(x, pltpu.HBM)
+        for x in (charge, dest.reshape(1, 256), local_ids.reshape(1, 256), green_hat)
     )
-    recv = all_to_all(send.reshape(N_DEV, 5, 128), BOTH).reshape(640, 128)
-    lines = call(z_forward_kernel, (512, 128))(recv, wave_hi, wave_lo, mix_hi, mix_lo)
-    planes = all_to_all(lines.reshape(N_DEV, 4, 128), BOTH).reshape(512, 128)
+    send, place = call(
+        pack_kernel,
+        [(640, 128), (1, 256)],
+        [
+            pltpu.VMEM((256, 128), F32),
+            pltpu.VMEM((1, 256), jnp.int32),
+            pltpu.VMEM((1, 256), jnp.int32),
+            pltpu.VMEM((128, 128), F32),
+            pltpu.SemaphoreType.DMA((4,)),
+        ],
+        in_specs=[HBM] * 4,
+    )(charge, dest, local_ids, green_hat)
+    recv = all_to_all(send.reshape(N_DEV, 1, 640), BOTH).reshape(640, 128)
+    pieces = call(
+        green_kernel,
+        [(144, 128)] * 4,
+        [
+            pltpu.VMEM((128, 16, 128), F32),
+            pltpu.VMEM((128, 128), F32),
+            pltpu.VMEM((4, 144, 128), F32),
+            pltpu.SemaphoreType.DMA((4,)),
+        ],
+        in_specs=[HBM],
+        out_specs=[HBM] * 4,
+    )(green_hat)
+    green = [pieces[0]]
+    for n in range(1, 4):
+        pairs = [(i, i // 4 * 4 + ((i % 4) ^ n)) for i in range(N_PX)]
+        green.append(lax.ppermute(pieces[n], "px", pairs))
+    green = [
+        pltpu.with_memory_space_constraint(piece.reshape(9, 16, 128), pltpu.HBM) for piece in green
+    ]
+    recv, green = lax.optimization_barrier((recv, green))
+    tables = [pltpu.with_memory_space_constraint(jnp.asarray(x), pltpu.HBM) for x in (mix_hi, mix_lo, wave_hi, wave_lo)]
+    lines = call(
+        z_forward_kernel,
+        (640, 128),
+        [pltpu.VMEM(x.shape, BF) for x in tables] + [pltpu.SemaphoreType.DMA((4,))],
+        in_specs=[VMEM] + [HBM] * 4,
+    )(recv, *tables)
+    planes = all_to_all(lines.reshape(N_DEV, 1, 640), BOTH).reshape(640, 128)
     planes = call(
         plane_kernel,
         (512, 128),
-        [pltpu.VMEM((16, 64, 128), F32), pltpu.VMEM((16, 64, 128), F32)],
-    )(planes, green, plane_fwd, plane_back, plane_lo)
+        [
+            pltpu.VMEM((9, 64, 128), F32),
+            pltpu.VMEM((16, 64, 128), F32),
+            pltpu.VMEM((16, 64, 128), F32),
+            pltpu.SemaphoreType.DMA((4,)),
+        ],
+        in_specs=[VMEM] + [HBM] * 4 + [VMEM] * 4,
+    )(planes, *green, x_fwd, x_back, y_fwd, y_back)
     lines = all_to_all(planes.reshape(N_DEV, 4, 128), BOTH).reshape(512, 128)
     rows = call(z_back_kernel, (512, 128))(lines, recv, back_hi, back_lo, mix_hi, mix_lo)
     rows = all_to_all(rows.reshape(N_DEV, 4, 128), BOTH).reshape(512, 128)

time: 104 us -> 87 us (0.84)
  blocking collectives: 73.5 us -> 49.5 us
  starting transfers between devices: 4.73 us -> 14.2 us
  Pallas kernels: 11.6 us -> 16.3 us
  local copies, waits for them, and re-layouts: 4.67 us -> 0.69 us
  waiting for transfers between devices: 9.41 us -> 5.74 us
    all_to_all x4 -> x3, blocking collectives: 73.5 us -> 49.5 us  [all_to_all(): return lax.all_to_all(x, axes, split_axis=0, concat_axis=0, tiled=True)]
    all_to_all x1, waiting for transfers between devices: 9.41 us -> 0.01 us  [all_to_all(): return lax.all_to_all(x, axes, split_axis=0, concat_axis=0, tiled=True)]
    all_to_all x1, starting transfers between devices: 4.73 us -> 11.5 us  [all_to_all(): return lax.all_to_all(x, axes, split_axis=0, concat_axis=0, tiled=True)]
    ppermute x0 -> x3, waiting for transfers between devices: none -> 5.74 us  [local(): green.append(lax.ppermute(pieces[n], 'px', pairs))]
    pallas_call x4, Pallas kernels: 7.65 us -> 12.5 us  [the longest x1 4.78 us: local(): call(plane_kernel, (512, 128), [pltpu.VMEM((9, 64, 128), F32), pltpu.VMEM...]
    unnamed x26 -> x24, local copies, waits for them, and re-layouts: 3.54 us -> 0.69 us
    ppermute x0 -> x3, starting transfers between devices: none -> 2.7 us  [local(): green.append(lax.ppermute(pieces[n], 'px', pairs))]
    reshape x2 -> x0, local copies, waits for them, and re-layouts: 1.14 us -> none  [local(): recv = all_to_all(send.reshape(N_DEV, 5, 128), BOTH).reshape(640, 128)]
  transfers between devices with their start and end apart: 1 -> 4, of which waited for: 1 -> 2; matrix products, arithmetic and copies ran while one was open for 0% -> 0% of each run, Pallas kernels for 1% -> 3%
where the time goes in v2:
time: 87 us; the launch traced here: 86.7 us
  blocking collectives  49.5 us (57%)
  Pallas kernels  16.3 us (19%)
  starting transfers between devices  14.2 us (16%)
  waiting for transfers between devices  5.74 us (7%)
    all_to_all x3, blocking collectives, all_to_all(): return lax.all_to_all(x, axes, split_axis=0, concat_axis=0, tiled=True)  49.5 us
    all_to_all x1, starting transfers between devices, all_to_all(): return lax.all_to_all(x, axes, split_axis=0, concat_axis=0, tiled=True)  11.5 us
    ppermute x3, waiting for transfers between devices, local(): green.append(lax.ppermute(pieces[n], 'px', pairs))  5.74 us
    pallas_call x1, Pallas kernels, local(): call(plane_kernel, (512, 128), [pltpu.VMEM((9, 64, 128), F32), pltpu.VMEM...  4.78 us
    pallas_call x1, Pallas kernels, local(): call(z_forward_kernel, (640, 128), [pltpu.VMEM(x.shape, BF) for x in tabl...  3.12 us
    pallas_call x1, Pallas kernels, local(): call(z_back_kernel, (512, 128))  2.85 us
    ppermute x3, starting transfers between devices, local(): green.append(lax.ppermute(pieces[n], 'px', pairs))  2.7 us
    pallas_call x1, Pallas kernels, local(): call(green_kernel, [(144, 128)] * 4, [pltpu.VMEM((128, 16, 128), F32), pl...  2.4 us
  transfers between devices with their start and end apart: 4, of which 2 were waited for; matrix products, arithmetic and copies ran while one was open for 0% of the time, Pallas kernels for 3%

profile of v2, /device:TPU:1, one launch (start us, length us, event | category | flops | bytes accessed | tf_op | source)
XLA Modules:
  0.0 86.7 jit_solution(17585822671439757458)
XLA Ops:
  0.0 2.2 %pack_kernel.1 = (f32[640,128]{1,0:T(8,128)}, f32[1,256]{1,0:T(1,128)S(1)}) custom-call(f32[256,128]{1,0:T(8,128)} %charge_any.1, s32[1,256]{1,0:T(1,128)} %bitcast.26, s32[1,256]{1,0:T(1,128)} %bitcast.27, f32[128,16,128]{2,1,0:T(8,128)} %green_any.3), custom_call_target="tpu_custom_call" | custom-call | tf_op jit(solution)/shard_map/pack_kernel/pallas_call | solution.py:316
  2.2 11.5 %all-to-all-start = ((f32[128,1,640]{2,1,0:T(1,128)}), f32[128,1,640]{2,1,0:T(1,128)S(1)}, u32[]{:S(2)}, u32[]{:S(2)}) async-start(f32[128,1,640]{2,1,0:T(1,128)} %bitcast.2), calls=%async_computation | async-start | bytes 655360 | tf_op jit(solution)/shard_map/all_to_all | solution.py:297
  13.7 2.4 %green_kernel.1 = (f32[144,128]{1,0:T(8,128)S(1)}, f32[144,128]{1,0:T(8,128)S(1)}, f32[144,128]{1,0:T(8,128)S(1)}, f32[144,128]{1,0:T(8,128)S(1)}) custom-call(f32[128,16,128]{2,1,0:T(8,128)} %green_any.3), custom_call_target="tpu_custom_call" | custom-call | tf_op jit(solution)/shard_map/green_kernel/pallas_call | solution.py:329
  16.1 0.0 copy-start.6
  16.1 0.6 copy-done.6
  16.7 1.1 %collective-permute-start = (f32[144,128]{1,0:T(8,128)S(1)}, f32[144,128]{1,0:T(8,128)S(1)}, u32[]{:S(2)}, u32[]{:S(2)}) collective-permute-start(f32[144,128]{1,0:T(8,128)S(1)} %get-tuple-element.18), channel_id=1, source_target_pairs={{0,16},{16,0},{32,48},{48,32},{64,80},{80,64},{96,112},{112,96},{1... | collective-permute-start | bytes 221192 | tf_op jit(solution)/shard_map/ppermute | solution.py:344
  17.8 0.8 collective-permute-start.1
  18.6 0.8 collective-permute-start.2
  19.4 0.0 collective-permute-done
  19.4 0.0 copy-start.9
  19.4 3.8 %collective-permute-done.1 = f32[144,128]{1,0:T(8,128)S(1)} collective-permute-done((f32[144,128]{1,0:T(8,128)S(1)}, f32[144,128]{1,0:T(8,128)S(1)}, u32[]{:S(2)}, u32[]{:S(2)}) %collective-permute-start.1) | collective-permute-done | bytes 73760 | tf_op jit(solution)/shard_map/ppermute | solution.py:344
  23.2 0.0 copy-start.10
  23.2 1.9 %collective-permute-done.2 = f32[144,128]{1,0:T(8,128)S(1)} collective-permute-done((f32[144,128]{1,0:T(8,128)S(1)}, f32[144,128]{1,0:T(8,128)S(1)}, u32[]{:S(2)}, u32[]{:S(2)}) %collective-permute-start.2) | collective-permute-done | bytes 73760 | tf_op jit(solution)/shard_map/ppermute | solution.py:344
  25.2 0.0 copy-start.11
  25.2 0.0 all-to-all-done
  25.2 0.0 copy-start.4
  25.2 0.0 copy-start.5
  25.2 0.0 copy-start.7
  25.2 0.0 copy-start.8
  25.2 0.0 copy-start.3
  25.2 3.1 %z_forward_kernel.1 = f32[640,128]{1,0:T(8,128)S(1)} custom-call(f32[640,128]{1,0:T(8,128)S(1)} %bitcast.14, bf16[256,1024]{1,0:T(8,128)(2,1)} %constant.20.clone.refs_0_.mix_hi_ref, bf16[256,1024]{1,0:T(8,128)(2,1)} %constant.21.clone.refs_1_.mix_lo_ref, bf16[1152,256]{1,0:T(8,128)(2,1)} %constant.22.clone.refs_2_, bf16[1152,256]{1,0:T(8,128)(2,1)} %constant.23.clone.refs_3_), custom_call_target="tpu_custom_call" | custom-call | tf_op jit(solution)/shard_map/z_forward_kernel/pallas_call | solution.py:350
  28.4 0.0 copy-done.9
  28.4 0.0 copy-done.10
  28.4 0.0 copy-done.11
  28.4 0.0 copy-start
  28.4 0.0 copy-start.1
  28.4 0.0 copy-start.2
  28.4 18.6 %all_to_all.20 = f32[128,1,640]{2,1,0:T(1,128)S(1)} all-to-all(f32[128,1,640]{2,1,0:T(1,128)S(1)} %bitcast.17), channel_id=1, replica_groups=mesh['px'=8,'pz'=16] {'px','pz'}, dimensions={0} | all-to-all | bytes 655360 | tf_op jit(solution)/shard_map/all_to_all | solution.py:297
  47.1 0.0 copy-done.4
  47.1 0.0 copy-done.5
  47.1 0.0 copy-done.7
  47.1 0.0 copy-done.8
  47.1 4.8 %plane_kernel.1 = f32[512,128]{1,0:T(8,128)S(1)} custom-call(f32[640,128]{1,0:T(8,128)S(1)} %bitcast.16, f32[9,16,128]{2,1,0:T(8,128)} %bitcast.22, f32[9,16,128]{2,1,0:T(8,128)} %bitcast.23, f32[9,16,128]{2,1,0:T(8,128)} %bitcast.24, f32[9,16,128]{2,1,0:T(8,128)} %bitcast.25, bf16[192,128]{1,0:T(8,128)(2,1)S(1)} %copy-done.8, ...), custom_call_target="tpu_custom_call" | custom-call | tf_op jit(solution)/shard_map/plane_kernel/pallas_call | solution.py:357
  51.9 15.7 %all_to_all.21 = f32[128,4,128]{2,1,0:T(4,128)S(1)} all-to-all(f32[128,4,128]{2,1,0:T(4,128)S(1)} %bitcast.21), channel_id=1, replica_groups=mesh['px'=8,'pz'=16] {'px','pz'}, dimensions={0} | all-to-all | bytes 524288 | tf_op jit(solution)/shard_map/all_to_all | solution.py:297
  67.5 0.0 copy-done.3
  67.5 0.0 copy-done
  67.5 0.0 copy-done.1
  67.6 0.0 copy-done.2
  67.6 2.8 %z_back_kernel.1 = f32[512,128]{1,0:T(8,128)S(1)} custom-call(f32[512,128]{1,0:T(8,128)S(1)} %bitcast.18, f32[640,128]{1,0:T(8,128)S(1)} %bitcast.15, bf16[2304,256]{1,0:T(8,128)(2,1)S(1)} %copy-done.2, bf16[2304,128]{1,0:T(8,128)(2,1)S(1)} %copy-done.3, bf16[256,1024]{1,0:T(8,128)(2,1)S(1)} %copy-done.1, bf16[256,1024]{1,0:T(8,128)(2,1)S(1)} %copy-done), custom_call_target="tpu_custom_call" | custom-call | tf_op jit(solution)/shard_map/z_back_kernel/pallas_call | solution.py:369
  70.4 15.2 %all_to_all.22 = f32[128,4,128]{2,1,0:T(4,128)S(1)} all-to-all(f32[128,4,128]{2,1,0:T(4,128)S(1)} %bitcast.19), channel_id=1, replica_groups=mesh['px'=8,'pz'=16] {'px','pz'}, dimensions={0} | all-to-all | bytes 524288 | tf_op jit(solution)/shard_map/all_to_all | solution.py:297
  85.6 1.0 %unpack_kernel.1 = f32[256,128]{1,0:T(8,128)} custom-call(f32[512,128]{1,0:T(8,128)S(1)} %bitcast.20, f32[1,256]{1,0:T(1,128)S(1)} %get-tuple-element.26.place_ref), custom_call_target="tpu_custom_call" | custom-call | tf_op jit(solution)/shard_map/unpack_kernel/pallas_call | solution.py:371
Async XLA Ops:
  2.2 23.0 %all-to-all-start = ((f32[128,1,640]{2,1,0:T(1,128)}), f32[128,1,640]{2,1,0:T(1,128)S(1)}, u32[]{:S(2)}, u32[]{:S(2)}) async-start(f32[128,1,640]{2,1,0:T(1,128)} %bitcast.2), calls=%async_computation | async-start | bytes 655360 | tf_op jit(solution)/shard_map/all_to_all | solution.py:297
  16.1 0.6 copy-start.6
  16.7 2.7 %collective-permute-start = (f32[144,128]{1,0:T(8,128)S(1)}, f32[144,128]{1,0:T(8,128)S(1)}, u32[]{:S(2)}, u32[]{:S(2)}) collective-permute-start(f32[144,128]{1,0:T(8,128)S(1)} %get-tuple-element.18), channel_id=1, source_target_pairs={{0,16},{16,0},{32,48},{48,32},{64,80},{80,64},{96,112},{112,96},{1... | collective-permute-start | bytes 221192 | tf_op jit(solution)/shard_map/ppermute | solution.py:344
  17.8 5.4 %collective-permute-start.1 = (f32[144,128]{1,0:T(8,128)S(1)}, f32[144,128]{1,0:T(8,128)S(1)}, u32[]{:S(2)}, u32[]{:S(2)}) collective-permute-start(f32[144,128]{1,0:T(8,128)S(1)} %get-tuple-element.19), channel_id=1, source_target_pairs={{0,32},{16,48},{32,0},{48,16},{64,96},{80,112},{96,64},{112,80},{1... | collective-permute-start | bytes 221192 | tf_op jit(solution)/shard_map/ppermute | solution.py:344
  18.6 6.6 %collective-permute-start.2 = (f32[144,128]{1,0:T(8,128)S(1)}, f32[144,128]{1,0:T(8,128)S(1)}, u32[]{:S(2)}, u32[]{:S(2)}) collective-permute-start(f32[144,128]{1,0:T(8,128)S(1)} %get-tuple-element.20), channel_id=1, source_target_pairs={{0,48},{16,32},{32,16},{48,0},{64,112},{80,96},{96,80},{112,64},{1... | collective-permute-start | bytes 221192 | tf_op jit(solution)/shard_map/ppermute | solution.py:344
  19.4 8.9 %copy-start.9 = (f32[144,128]{1,0:T(8,128)}, f32[144,128]{1,0:T(8,128)S(1)}, u32[]{:S(2)}) copy-start(f32[144,128]{1,0:T(8,128)S(1)} %collective-permute-done) | copy-start | bytes 221188
  23.2 5.1 %copy-start.10 = (f32[144,128]{1,0:T(8,128)}, f32[144,128]{1,0:T(8,128)S(1)}, u32[]{:S(2)}) copy-start(f32[144,128]{1,0:T(8,128)S(1)} %collective-permute-done.1) | copy-start | bytes 221188
  25.2 3.2 %copy-start.11 = (f32[144,128]{1,0:T(8,128)}, f32[144,128]{1,0:T(8,128)S(1)}, u32[]{:S(2)}) copy-start(f32[144,128]{1,0:T(8,128)S(1)} %collective-permute-done.2) | copy-start | bytes 221188
  25.2 21.9 %copy-start.4 = (bf16[2,64,384]{2,1,0:T(8,128)(2,1)S(1)}, bf16[2,64,384]{2,1,0:T(8,128)(2,1)}, u32[]{:S(2)}) copy-start(bf16[2,64,384]{2,1,0:T(8,128)(2,1)} %constant.27.clone.refs_7_) | copy-start | bytes 294916
  25.2 21.9 %copy-start.5 = (bf16[2,192,128]{2,1,0:T(8,128)(2,1)S(1)}, bf16[2,192,128]{2,1,0:T(8,128)(2,1)}, u32[]{:S(2)}) copy-start(bf16[2,192,128]{2,1,0:T(8,128)(2,1)} %constant.26.clone.refs_6_) | copy-start | bytes 294916
  25.2 21.9 %copy-start.7 = (bf16[64,384]{1,0:T(8,128)(2,1)S(1)}, bf16[64,384]{1,0:T(8,128)(2,1)}, u32[]{:S(2)}) copy-start(bf16[64,384]{1,0:T(8,128)(2,1)} %constant.25.clone.refs_5_) | copy-start | bytes 147460
  25.2 21.9 %copy-start.8 = (bf16[192,128]{1,0:T(8,128)(2,1)S(1)}, bf16[192,128]{1,0:T(8,128)(2,1)}, u32[]{:S(2)}) copy-start(bf16[192,128]{1,0:T(8,128)(2,1)} %constant.24.clone.refs_4_) | copy-start | bytes 147460
  25.2 42.3 %copy-start.3 = (bf16[2304,128]{1,0:T(8,128)(2,1)S(1)}, bf16[2304,128]{1,0:T(8,128)(2,1)}, u32[]{:S(2)}) copy-start(bf16[2304,128]{1,0:T(8,128)(2,1)} %constant.29.clone.wave_lo_ref) | copy-start | bytes 1769476
  28.4 39.2 %copy-start = (bf16[256,1024]{1,0:T(8,128)(2,1)S(1)}, bf16[256,1024]{1,0:T(8,128)(2,1)}, u32[]{:S(2)}) copy-start(bf16[256,1024]{1,0:T(8,128)(2,1)} %constant.21.clone.refs_1_.mix_lo_ref) | copy-start | bytes 1572868
  28.4 39.2 %copy-start.1 = (bf16[256,1024]{1,0:T(8,128)(2,1)S(1)}, bf16[256,1024]{1,0:T(8,128)(2,1)}, u32[]{:S(2)}) copy-start(bf16[256,1024]{1,0:T(8,128)(2,1)} %constant.20.clone.refs_0_.mix_hi_ref) | copy-start | bytes 1572868
  28.4 39.1 %copy-start.2 = (bf16[2304,256]{1,0:T(8,128)(2,1)S(1)}, bf16[2304,256]{1,0:T(8,128)(2,1)}, u32[]{:S(2)}) copy-start(bf16[2304,256]{1,0:T(8,128)(2,1)} %constant.28.clone.wave_hi_ref) | copy-start | bytes 3538948

commit v3 on v2

--- a/solution.py
+++ b/solution.py
@@ -142,48 +142,37 @@
     send_ref[pl.ds(4, 128, stride=5), :] = named
 
 
-def slot_hots(recv_ref):
-    lane = iota((128, 256), 1)
-    block = ((lane % 8) * 4 + (lane // 8) % 4) * 8 + lane // 32
-    block = block.astype(F32)
-    names = recv_ref[pl.ds(4, 128, stride=5), :]
-    hots = [jnp.where(names[:, 9 + s : 10 + s] == block, 1.0, 0.0).astype(BF) for s in range(CAP)]
-    return jnp.concatenate(hots, axis=0)
-
-
-def lane_residue(shape):
-    kk = (iota(shape, 1) // 8) % 16
-    return jnp.where(kk == 0, 0, jnp.where(kk == 1, 8, kk // 2))
-
-
-def z_forward_kernel(recv_ref, *refs):
-    tables, out_ref, copies, sems = refs[:4], refs[4], refs[5:9], refs[9]
-    moves = [pltpu.make_async_copy(tables[n], copies[n], sems.at[n]) for n in range(4)]
-    for move in moves:
-        move.start()
-    mix_hi_ref, mix_lo_ref, wave_hi_ref, wave_lo_ref = copies
-    hots = slot_hots(recv_ref)
+def block_name(index):
+    return (((index % 8) * 4 + (index // 8) % 4) * 8 + index // 32).astype(F32)
+
+
+def slot_rows(r):
+    first, count = (0, 8) if r == 0 else (8, 8) if r == 8 else (16 * r, 16)
+    return [slice(b * 128 + first, b * 128 + first + count) for b in range(CYP)], count
+
+
+def z_forward_kernel(recv_ref, mix_ref, wave_ref, out_ref, turned_ref):
+    ends = recv_ref[pl.ds(4, 128, stride=5), :]
+    names = ends.T
+    block = block_name(iota((256, 128), 0))
+    hots = [jnp.where(block == names[9 + s : 10 + s, :], 1.0, 0.0).astype(BF) for s in range(CAP)]
     rows = jnp.concatenate([recv_ref[pl.ds(s, 128, stride=5), :] for s in range(CAP)], axis=0)
-    parts = jnp.concatenate(three(rows), axis=1)
-    field = dot(parts, hots, 0, 0)
-    field = field[:128] + field[128:256] + field[256:]
+    field = dot(jnp.concatenate(hots, axis=1), jnp.concatenate(three(rows), axis=1))
+    field = field[:, :128] + field[:, 128:256] + field[:, 256:]
     high, low = two(field)
-    moves[0].wait()
-    moves[1].wait()
-    mixed = dot(high, mix_hi_ref[...]) + dot(low, mix_hi_ref[...]) + dot(high, mix_lo_ref[...])
-    mixed = jnp.concatenate([mixed[:, :512], mixed[:, 512:]], axis=0)
-    high, low = two(mixed)
-    moves[2].wait()
-    moves[3].wait()
-    residue = lane_residue((128, 512))
-    out = jnp.zeros((128, 512), F32)
+    mixed = dot(mix_ref[:1024], jnp.concatenate([high, low], axis=1))
+    mixed = mixed[:, :128] + mixed[:, 128:] + dot(mix_ref[1024:], high)
+    mixed = jnp.concatenate([mixed[:512], mixed[512:]], axis=1)
     for r in range(9):
-        rows = slice(r * 128, (r + 1) * 128)
-        block = dot(wave_hi_ref[rows, :], high) + dot(wave_hi_ref[rows, :], low) + dot(wave_lo_ref[rows, :], high)
-        out = jnp.where(residue == r, block, out)
+        places, count = slot_rows(r)
+        high, low = two(jnp.concatenate([mixed[place] for place in places], axis=0))
+        block = dot(jnp.concatenate([high, low], axis=0), wave_ref[r * 256 : (r + 1) * 256, :])
+        size = 4 * count
+        block = block[:size, :128] + block[:size, 128:] + block[size:, :128]
+        for b, place in enumerate(places):
+            turned_ref[place, :] = block[b * count : (b + 1) * count]
     for b in range(CYP):
-        out_ref[pl.ds(b, 128, stride=5), :] = out[:, b * 128 : (b + 1) * 128]
-    ends = recv_ref[pl.ds(4, 128, stride=5), :]
+        out_ref[pl.ds(b, 128, stride=5), :] = turned_ref[b * 128 : (b + 1) * 128, :].T
     relayed = []
     for i in range(N_PX):
         source = 64 if i < 4 else 0
@@ -194,16 +183,13 @@
 
 def plane_kernel(spec_ref, *refs):
     pieces, refs = refs[:4], refs[4:]
-    x_fwd_ref, x_back_ref, y_fwd_ref, y_back_ref, out_ref, green_ref, first_ref, second_ref, sems = refs
+    x_fwd_ref, x_back_ref, y_fwd_ref, y_back_ref, out_ref, green_ref, first_ref, second_ref = refs
     me = lax.axis_index("px")
     half, place = me // 4, me % 4
-    moves = []
     for n in range(4):
-        source = jnp.bitwise_xor(place, n)
-        start = pl.multiple_of(source * 16, 16)
-        moves.append(pltpu.make_async_copy(pieces[n], green_ref.at[:, pl.ds(start, 16), :], sems.at[n]))
-    for move in moves:
-        move.start()
+        start = pl.multiple_of(jnp.bitwise_xor(place, n) * 16, 16)
+        for r in range(9):
+            green_ref[r, pl.ds(start, 16), :] = pieces[n][r * 16 : (r + 1) * 16, :]
     ends = spec_ref[pl.ds(4, 128, stride=5), :].T
     y_fwd, y_back, y_low = y_fwd_ref[half], y_back_ref[half, :, :256], y_back_ref[half, :, 256:]
     x_fwd, x_back, x_low = x_fwd_ref[...], x_back_ref[:, :256], x_back_ref[:, 256:]
@@ -213,8 +199,6 @@
         turned = dot(jnp.concatenate([high, low, high], axis=0), y_fwd, 0, 0)
         for kk in range(16):
             first_ref[kk, i * 8 : (i + 1) * 8, :] = turned[kk * 8 : (kk + 1) * 8]
-    for move in moves:
-        move.wait()
     top = iota((64, 128), 0) == 0
     for kk in range(16):
         high, low = two(first_ref[kk])
@@ -233,20 +217,27 @@
         )
 
 
-def z_back_kernel(spec_ref, recv_ref, wave_hi_ref, wave_lo_ref, mix_hi_ref, mix_lo_ref, out_ref):
-    lines = jnp.concatenate([spec_ref[pl.ds(b, 128, stride=4), :] for b in range(CYP)], axis=1)
-    high, low = two(lines)
-    both = jnp.concatenate([high, low], axis=0)
-    residue = lane_residue((256, 512))
-    acc = jnp.zeros((256, 512), F32)
+def z_back_kernel(spec_ref, recv_ref, wave_hi_ref, wave_lo_ref, mix_hi_ref, mix_lo_ref, out_ref, turned_ref, line_ref):
+    for b in range(CYP):
+        turned_ref[b * 128 : (b + 1) * 128, :] = spec_ref[pl.ds(b, 128, stride=4), :].T
     for r in range(9):
-        rows = slice(r * 256, (r + 1) * 256)
-        block = dot(wave_hi_ref[rows, :], both) + dot(wave_lo_ref[rows, :], high)
-        acc = jnp.where(residue == r, block, acc)
-    high, low = two(jnp.concatenate([acc[:128], acc[128:]], axis=1))
-    field = dot(high, mix_hi_ref[...], 1, 1) + dot(low, mix_hi_ref[...], 1, 1) + dot(high, mix_lo_ref[...], 1, 1)
-    parts = jnp.concatenate(three(field), axis=0)
-    rows = dot(slot_hots(recv_ref), parts, 1, 1)
+        places, count = slot_rows(r)
+        high, low = two(jnp.concatenate([turned_ref[place, :] for place in places], axis=0))
+        rows = slice(r * 128, (r + 1) * 128)
+        size = 4 * count
+        block = dot(jnp.concatenate([high, low], axis=0), wave_hi_ref[rows, :])
+        block = block[:size] + block[size:] + dot(high, wave_lo_ref[rows, :])
+        for b, place in enumerate(places):
+            part = block[b * count : (b + 1) * count]
+            line_ref[place, :] = part[:, :128]
+            line_ref[slice(place.start + 512, place.stop + 512), :] = part[:, 128:]
+    high, low = two(line_ref[...])
+    field = dot(mix_hi_ref[...], jnp.concatenate([high, low], axis=1))
+    field = field[:, :128] + field[:, 128:] + dot(mix_lo_ref[...], high)
+    block = block_name(iota((128, 256), 1))
+    names = recv_ref[pl.ds(4, 128, stride=5), :]
+    hots = [jnp.where(names[:, 9 + s : 10 + s] == block, 1.0, 0.0).astype(BF) for s in range(CAP)]
+    rows = dot(jnp.concatenate(hots, axis=0), jnp.concatenate(three(field), axis=1))
     rows = rows[:, :128] + rows[:, 128:256] + rows[:, 256:]
     for s in range(CAP):
         out_ref[pl.ds(s, 128, stride=4), :] = rows[s * 128 : (s + 1) * 128]
@@ -263,22 +254,25 @@
 
 
 def green_kernel(green_any, *refs):
-    out_refs, (green_ref, turned_ref, piece_ref, sems) = refs[:4], refs[4:]
+    tables, out_refs, copies, (green_ref, turned_ref, piece_ref, sems) = refs[:6], refs[6:10], refs[10:16], refs[16:]
     me = lax.axis_index("px")
-    move = pltpu.make_async_copy(green_any, green_ref, sems.at[0])
-    move.start()
+    moves = [pltpu.make_async_copy(green_any, green_ref, sems.at[0])]
+    for n in range(6):
+        moves.append(pltpu.make_async_copy(tables[n], copies[n], sems.at[n + 1]))
+    for move in moves:
+        move.start()
     starts = [
         pl.multiple_of((me - me % 4 + jnp.bitwise_xor(me % 4, n)) * 16, 16) for n in range(4)
     ]
-    move.wait()
+    moves[0].wait()
     for k2 in range(16):
         turned_ref[...] = green_ref[:, k2, :].T
         for n in range(4):
             piece_ref[n, pl.ds(k2, 9, stride=16), :] = turned_ref[pl.ds(starts[n], 9), :]
-    moves = [pltpu.make_async_copy(piece_ref.at[n], out_refs[n], sems.at[n]) for n in range(4)]
-    for move in moves:
+    stores = [pltpu.make_async_copy(piece_ref.at[n], out_refs[n], sems.at[n + 7]) for n in range(4)]
+    for move in stores:
         move.start()
-    for move in moves:
+    for move in moves[1:] + stores:
         move.wait()
 
 
@@ -286,7 +280,11 @@
     return pl.pallas_call(
         kernel,
         **specs,
-        out_shape=jax.tree.map(lambda s: jax.ShapeDtypeStruct(s, dtype), shape, is_leaf=lambda s: isinstance(s, tuple)),
+        out_shape=jax.tree.map(
+            lambda s: jax.ShapeDtypeStruct(s, dtype) if isinstance(s, tuple) else s,
+            shape,
+            is_leaf=lambda s: isinstance(s, tuple),
+        ),
         scratch_shapes=list(scratch),
         compiler_params=PARAMS,
         name=kernel.__name__,
@@ -299,11 +297,10 @@
 
 def local(charge, dest, local_ids, green_hat):
     wave, mix = z_tables()
+    mix_hi, mix_lo = split_table(mix)
+    mix_both = np.concatenate([mix_hi.T, mix_lo.T], axis=0)
     wave_hi, wave_lo = split_table(wave.reshape(9 * 128, 256))
-    mix_hi, mix_lo = split_table(mix)
-    back = wave.reshape(9, 128, 2, 128).transpose(0, 2, 3, 1).reshape(9 * 256, 128)
-    back_hi, back_lo = split_table(back)
-    back_hi = np.concatenate([back_hi, back_hi], axis=1)
+    wave_both = np.concatenate(split_table(wave.transpose(0, 2, 1).reshape(9 * 256, 128)), axis=1)
     x_fwd, x_back = stacked(plane_table())
     order = np.arange(64).reshape(N_PZ, CYP).T.reshape(64)
     y_fwd, y_back = (np.stack(tables) for tables in zip(stacked(pair_table(0)), stacked(pair_table(1))))
@@ -326,33 +323,27 @@
         in_specs=[HBM] * 4,
     )(charge, dest, local_ids, green_hat)
     recv = all_to_all(send.reshape(N_DEV, 1, 640), BOTH).reshape(640, 128)
-    pieces = call(
+    tables = [
+        pltpu.with_memory_space_constraint(jnp.asarray(x), pltpu.HBM)
+        for x in (mix_both, wave_both, x_fwd, x_back, y_fwd, y_back)
+    ]
+    *pieces, mix_both, wave_both, x_fwd, x_back, y_fwd, y_back = call(
         green_kernel,
-        [(144, 128)] * 4,
+        [pltpu.HBM((144, 128), F32)] * 4 + [jax.ShapeDtypeStruct(x.shape, BF) for x in tables],
         [
             pltpu.VMEM((128, 16, 128), F32),
             pltpu.VMEM((128, 128), F32),
             pltpu.VMEM((4, 144, 128), F32),
-            pltpu.SemaphoreType.DMA((4,)),
+            pltpu.SemaphoreType.DMA((11,)),
         ],
-        in_specs=[HBM],
-        out_specs=[HBM] * 4,
-    )(green_hat)
+        in_specs=[HBM] * 7,
+        out_specs=[HBM] * 4 + [VMEM] * 6,
+    )(green_hat, *tables)
     green = [pieces[0]]
     for n in range(1, 4):
         pairs = [(i, i // 4 * 4 + ((i % 4) ^ n)) for i in range(N_PX)]
         green.append(lax.ppermute(pieces[n], "px", pairs))
-    green = [
-        pltpu.with_memory_space_constraint(piece.reshape(9, 16, 128), pltpu.HBM) for piece in green
-    ]
-    recv, green = lax.optimization_barrier((recv, green))
-    tables = [pltpu.with_memory_space_constraint(jnp.asarray(x), pltpu.HBM) for x in (mix_hi, mix_lo, wave_hi, wave_lo)]
-    lines = call(
-        z_forward_kernel,
-        (640, 128),
-        [pltpu.VMEM(x.shape, BF) for x in tables] + [pltpu.SemaphoreType.DMA((4,))],
-        in_specs=[VMEM] + [HBM] * 4,
-    )(recv, *tables)
+    lines = call(z_forward_kernel, (640, 128), [pltpu.VMEM((512, 128), F32)])(recv, mix_both, wave_both)
     planes = all_to_all(lines.reshape(N_DEV, 1, 640), BOTH).reshape(640, 128)
     planes = call(
         plane_kernel,
@@ -361,12 +352,12 @@
             pltpu.VMEM((9, 64, 128), F32),
             pltpu.VMEM((16, 64, 128), F32),
             pltpu.VMEM((16, 64, 128), F32),
-            pltpu.SemaphoreType.DMA((4,)),
         ],
-        in_specs=[VMEM] + [HBM] * 4 + [VMEM] * 4,
     )(planes, *green, x_fwd, x_back, y_fwd, y_back)
     lines = all_to_all(planes.reshape(N_DEV, 4, 128), BOTH).reshape(512, 128)
-    rows = call(z_back_kernel, (512, 128))(lines, recv, back_hi, back_lo, mix_hi, mix_lo)
+    rows = call(z_back_kernel, (512, 128), [pltpu.VMEM((512, 128), F32), pltpu.VMEM((1024, 128), F32)])(
+        lines, recv, wave_hi, wave_lo, mix_hi, mix_lo
+    )
     rows = all_to_all(rows.reshape(N_DEV, 4, 128), BOTH).reshape(512, 128)
     return call(unpack_kernel, (256, 128))(rows, place)
 

time: 87 us -> 82.6 us (0.949)
  blocking collectives: 49.5 us -> 33.1 us
  waiting for transfers between devices: 5.74 us -> 17.1 us
  starting transfers between devices: 14.2 us -> 19.3 us
  Pallas kernels: 16.3 us -> 12.8 us
    all_to_all x3 -> x2, blocking collectives: 49.5 us -> 33.1 us  [all_to_all(): return lax.all_to_all(x, axes, split_axis=0, concat_axis=0, tiled=True)]
    all_to_all x1 -> x2, waiting for transfers between devices: 0.01 us -> 9.64 us  [all_to_all(): return lax.all_to_all(x, axes, split_axis=0, concat_axis=0, tiled=True)]
    all_to_all x1 -> x2, starting transfers between devices: 11.5 us -> 16.3 us  [all_to_all(): return lax.all_to_all(x, axes, split_axis=0, concat_axis=0, tiled=True)]
    pallas_call x3, Pallas kernels: 8.36 us -> 5.82 us  [the longest x1 2.79 us: local(): call(green_kernel, [pltpu.HBM((144, 128), F32)] * 4 + [jax.ShapeDtypeStru...]
    ppermute x3, waiting for transfers between devices: 5.74 us -> 7.41 us  [local(): green.append(lax.ppermute(pieces[n], 'px', pairs))]
    pallas_call x1, Pallas kernels: 4.78 us -> 3.82 us  [local(): call(plane_kernel, (512, 128), [pltpu.VMEM((9, 64, 128), F32), pltpu.VMEM...]
  transfers between devices with their start and end apart: 4 -> 5, of which waited for: 2 -> 4; matrix products, arithmetic and copies ran while one was open for 0% -> 0% of each run, Pallas kernels for 3% -> 3%
where the time goes in v3:
time: 82.6 us; the launch traced here: 82.4 us
  blocking collectives  33.1 us (40%)
  starting transfers between devices  19.3 us (23%)
  waiting for transfers between devices  17.1 us (21%)
  Pallas kernels  12.8 us (15%)
    all_to_all x2, blocking collectives, all_to_all(): return lax.all_to_all(x, axes, split_axis=0, concat_axis=0, tiled=True)  33.1 us
    all_to_all x2, starting transfers between devices, all_to_all(): return lax.all_to_all(x, axes, split_axis=0, concat_axis=0, tiled=True)  16.3 us
    all_to_all x2, waiting for transfers between devices, all_to_all(): return lax.all_to_all(x, axes, split_axis=0, concat_axis=0, tiled=True)  9.64 us
    ppermute x3, waiting for transfers between devices, local(): green.append(lax.ppermute(pieces[n], 'px', pairs))  7.41 us
    pallas_call x1, Pallas kernels, local(): call(plane_kernel, (512, 128), [pltpu.VMEM((9, 64, 128), F32), pltpu.VMEM...  3.82 us
    ppermute x3, starting transfers between devices, local(): green.append(lax.ppermute(pieces[n], 'px', pairs))  3.01 us
    pallas_call x1, Pallas kernels, local(): call(green_kernel, [pltpu.HBM((144, 128), F32)] * 4 + [jax.ShapeDtypeStru...  2.79 us
    pallas_call x1, Pallas kernels, local(): call(pack_kernel, [(640, 128), (1, 256)], [pltpu.VMEM((256, 128), F32), p...  2.16 us
  transfers between devices with their start and end apart: 5, of which 4 were waited for; matrix products, arithmetic and copies ran while one was open for 0% of the time, Pallas kernels for 3%

profile of v3, /device:TPU:1, one launch (start us, length us, event | category | flops | bytes accessed | tf_op | source)
XLA Modules:
  0.0 82.4 jit_solution(15303751313277117348)
XLA Ops:
  0.0 2.2 %pack_kernel.1 = (f32[640,128]{1,0:T(8,128)}, f32[1,256]{1,0:T(1,128)S(1)}) custom-call(f32[256,128]{1,0:T(8,128)} %charge_any.1, s32[1,256]{1,0:T(1,128)} %bitcast.17, s32[1,256]{1,0:T(1,128)} %bitcast.18, f32[128,16,128]{2,1,0:T(8,128)} %green_any.3), custom_call_target="tpu_custom_call" | custom-call | tf_op jit(solution)/shard_map/pack_kernel/pallas_call | solution.py:313
  2.2 11.5 %all-to-all-start = ((f32[128,1,640]{2,1,0:T(1,128)}), f32[128,1,640]{2,1,0:T(1,128)S(1)}, u32[]{:S(2)}, u32[]{:S(2)}) async-start(f32[128,1,640]{2,1,0:T(1,128)} %bitcast.2), calls=%async_computation | async-start | bytes 655360 | tf_op jit(solution)/shard_map/all_to_all | solution.py:295
  13.7 2.8 %green_kernel.1 = (f32[144,128]{1,0:T(8,128)}, f32[144,128]{1,0:T(8,128)}, f32[144,128]{1,0:T(8,128)}, f32[144,128]{1,0:T(8,128)}, bf16[2048,256]{1,0:T(8,128)(2...) custom-call(f32[128,16,128]{2,1,0:T(8,128)} %green_any.3, ...), custom_call_target="tpu_custom_call" | custom-call | tf_op jit(solution)/shard_map/green_kernel/pallas_call | solution.py:330
  16.5 8.6 %all-to-all-done = f32[128,1,640]{2,1,0:T(1,128)S(1)} async-done(((f32[128,1,640]{2,1,0:T(1,128)}), f32[128,1,640]{2,1,0:T(1,128)S(1)}, u32[]{:S(2)}, u32[]{:S(2)}) %all-to-all-start) | async-done | bytes 327712 | tf_op jit(solution)/shard_map/all_to_all | solution.py:295
  25.0 0.0 copy-start.5
  25.1 0.0 copy-start.4
  25.1 1.9 %z_forward_kernel.1 = f32[640,128]{1,0:T(8,128)} custom-call(f32[640,128]{1,0:T(8,128)S(1)} %bitcast.10, bf16[2048,256]{1,0:T(8,128)(2,1)S(1)} %get-tuple-element.18.mix_ref, bf16[2304,256]{1,0:T(8,128)(2,1)S(1)} %get-tuple-element.19.wave_ref), custom_call_target="tpu_custom_call" | custom-call | tf_op jit(solution)/shard_map/z_forward_kernel/pallas_call | solution.py:346
  26.9 0.0 copy-start
  26.9 0.0 copy-start.1
  26.9 0.0 copy-start.2
  26.9 0.0 copy-start.3
  26.9 4.8 %all-to-all-start.1 = ((f32[128,1,640]{2,1,0:T(1,128)}), f32[128,1,640]{2,1,0:T(1,128)S(1)}, u32[]{:S(2)}, u32[]{:S(2)}) async-start(f32[128,1,640]{2,1,0:T(1,128)} %bitcast.4), calls=%async_computation.1 | async-start | bytes 655360 | tf_op jit(solution)/shard_map/all_to_all | solution.py:295
  31.8 1.3 %collective-permute-start = (f32[144,128]{1,0:T(8,128)}, f32[144,128]{1,0:T(8,128)S(1)}, u32[]{:S(2)}, u32[]{:S(2)}) collective-permute-start(f32[144,128]{1,0:T(8,128)} %get-tuple-element.21), channel_id=1, source_target_pairs={{0,16},{16,0},{32,48},{48,32},{64,80},{80,64},{96,112},{112,96},{1... | collective-permute-start | bytes 221192 | tf_op jit(solution)/shard_map/ppermute | solution.py:345
  33.0 0.8 collective-permute-start.1
  33.8 0.0 copy-done.5
  33.8 0.9 %collective-permute-start.2 = (f32[144,128]{1,0:T(8,128)S(1)}, f32[144,128]{1,0:T(8,128)S(1)}, u32[]{:S(2)}, u32[]{:S(2)}) collective-permute-start(f32[144,128]{1,0:T(8,128)S(1)} %copy-done.5), channel_id=1, source_target_pairs={{0,48},{16,32},{32,16},{48,0},{64,112},{80,96},{96,80},{112,64},{1... | collective-permute-start | bytes 221192 | tf_op jit(solution)/shard_map/ppermute | solution.py:345
  34.8 0.0 collective-permute-done.refs_1_
  34.8 4.1 %collective-permute-done.1.refs_2_ = f32[144,128]{1,0:T(8,128)S(1)} collective-permute-done((f32[144,128]{1,0:T(8,128)}, f32[144,128]{1,0:T(8,128)S(1)}, u32[]{:S(2)}, u32[]{:S(2)}) %collective-permute-start.1) | collective-permute-done | bytes 73760 | tf_op jit(solution)/shard_map/ppermute | solution.py:345
  38.9 3.3 %collective-permute-done.2.refs_3_ = f32[144,128]{1,0:T(8,128)S(1)} collective-permute-done((f32[144,128]{1,0:T(8,128)S(1)}, f32[144,128]{1,0:T(8,128)S(1)}, u32[]{:S(2)}, u32[]{:S(2)}) %collective-permute-start.2) | collective-permute-done | bytes 73760 | tf_op jit(solution)/shard_map/ppermute | solution.py:345
  42.2 1.1 %all-to-all-done.1 = f32[128,1,640]{2,1,0:T(1,128)S(1)} async-done(((f32[128,1,640]{2,1,0:T(1,128)}), f32[128,1,640]{2,1,0:T(1,128)S(1)}, u32[]{:S(2)}, u32[]{:S(2)}) %all-to-all-start.1) | async-done | bytes 327712 | tf_op jit(solution)/shard_map/all_to_all | solution.py:295
  43.3 0.0 copy-done.4
  43.3 3.8 %plane_kernel.1 = f32[512,128]{1,0:T(8,128)S(1)} custom-call(f32[640,128]{1,0:T(8,128)S(1)} %bitcast.12, f32[144,128]{1,0:T(8,128)S(1)} %copy-done.4, f32[144,128]{1,0:T(8,128)S(1)} %collective-permute-done.refs_1_, f32[144,128]{1,0:T(8,128)S(1)} %collective-permute-done.1.refs_2_, f32[144,128]{1,0:T(8,128)S(1)} %collective-permute-done.2.refs_3_, ...), custom_call_target="tpu_custom_call" | custom-call | tf_op jit(solution)/shard_map/plane_kernel/pallas_call | solution.py:348
  47.1 17.8 %all_to_all.20 = f32[128,4,128]{2,1,0:T(4,128)S(1)} all-to-all(f32[128,4,128]{2,1,0:T(4,128)S(1)} %bitcast.16), channel_id=1, replica_groups=mesh['px'=8,'pz'=16] {'px','pz'}, dimensions={0} | all-to-all | bytes 524288 | tf_op jit(solution)/shard_map/all_to_all | solution.py:295
  64.9 0.0 copy-done
  64.9 0.0 copy-done.1
  64.9 0.0 copy-done.2
  64.9 0.0 copy-done.3
  65.0 1.2 %z_back_kernel.1 = f32[512,128]{1,0:T(8,128)S(1)} custom-call(f32[512,128]{1,0:T(8,128)S(1)} %bitcast.13, f32[640,128]{1,0:T(8,128)S(1)} %bitcast.11, bf16[1152,256]{1,0:T(8,128)(2,1)S(1)} %copy-done.1, bf16[1152,256]{1,0:T(8,128)(2,1)S(1)} %copy-done, bf16[256,1024]{1,0:T(8,128)(2,1)S(1)} %copy-done.3, bf16[256,1024]{1,0:T(8,128)(2,1)S(1)} %copy-done.2), custom_call_target="tpu_custom_call" | custom-call | tf_op jit(solution)/shard_map/z_back_kernel/pallas_call | solution.py:358
  66.1 15.2 %all_to_all.21 = f32[128,4,128]{2,1,0:T(4,128)S(1)} all-to-all(f32[128,4,128]{2,1,0:T(4,128)S(1)} %bitcast.14), channel_id=1, replica_groups=mesh['px'=8,'pz'=16] {'px','pz'}, dimensions={0} | all-to-all | bytes 524288 | tf_op jit(solution)/shard_map/all_to_all | solution.py:295
  81.3 1.0 %unpack_kernel.1 = f32[256,128]{1,0:T(8,128)} custom-call(f32[512,128]{1,0:T(8,128)S(1)} %bitcast.15, f32[1,256]{1,0:T(1,128)S(1)} %get-tuple-element.28.place_ref), custom_call_target="tpu_custom_call" | custom-call | tf_op jit(solution)/shard_map/unpack_kernel/pallas_call | solution.py:362
Async XLA Ops:
  2.2 22.9 %all-to-all-start = ((f32[128,1,640]{2,1,0:T(1,128)}), f32[128,1,640]{2,1,0:T(1,128)S(1)}, u32[]{:S(2)}, u32[]{:S(2)}) async-start(f32[128,1,640]{2,1,0:T(1,128)} %bitcast.2), calls=%async_computation | async-start | bytes 655360 | tf_op jit(solution)/shard_map/all_to_all | solution.py:295
  25.0 8.8 %copy-start.5 = (f32[144,128]{1,0:T(8,128)S(1)}, f32[144,128]{1,0:T(8,128)}, u32[]{:S(2)}) copy-start(f32[144,128]{1,0:T(8,128)} %get-tuple-element.23) | copy-start | bytes 221188
  25.1 18.2 %copy-start.4 = (f32[144,128]{1,0:T(8,128)S(1)}, f32[144,128]{1,0:T(8,128)}, u32[]{:S(2)}) copy-start(f32[144,128]{1,0:T(8,128)} %get-tuple-element.20.refs_0_) | copy-start | bytes 221188
  26.9 38.0 %copy-start = (bf16[1152,256]{1,0:T(8,128)(2,1)S(1)}, bf16[1152,256]{1,0:T(8,128)(2,1)}, u32[]{:S(2)}) copy-start(bf16[1152,256]{1,0:T(8,128)(2,1)} %constant.27.clone.wave_lo_ref) | copy-start | bytes 1769476
  26.9 38.0 %copy-start.1 = (bf16[1152,256]{1,0:T(8,128)(2,1)S(1)}, bf16[1152,256]{1,0:T(8,128)(2,1)}, u32[]{:S(2)}) copy-start(bf16[1152,256]{1,0:T(8,128)(2,1)} %constant.26.clone.wave_hi_ref) | copy-start | bytes 1769476
  26.9 38.0 %copy-start.2 = (bf16[256,1024]{1,0:T(8,128)(2,1)S(1)}, bf16[256,1024]{1,0:T(8,128)(2,1)}, u32[]{:S(2)}) copy-start(bf16[256,1024]{1,0:T(8,128)(2,1)} %constant.29.clone.mix_lo_ref) | copy-start | bytes 1572868
  26.9 38.0 %copy-start.3 = (bf16[256,1024]{1,0:T(8,128)(2,1)S(1)}, bf16[256,1024]{1,0:T(8,128)(2,1)}, u32[]{:S(2)}) copy-start(bf16[256,1024]{1,0:T(8,128)(2,1)} %constant.28.clone.mix_hi_ref) | copy-start | bytes 1572868
  26.9 16.3 %all-to-all-start.1 = ((f32[128,1,640]{2,1,0:T(1,128)}), f32[128,1,640]{2,1,0:T(1,128)S(1)}, u32[]{:S(2)}, u32[]{:S(2)}) async-start(f32[128,1,640]{2,1,0:T(1,128)} %bitcast.4), calls=%async_computation.1 | async-start | bytes 655360 | tf_op jit(solution)/shard_map/all_to_all | solution.py:295
  31.8 3.0 %collective-permute-start = (f32[144,128]{1,0:T(8,128)}, f32[144,128]{1,0:T(8,128)S(1)}, u32[]{:S(2)}, u32[]{:S(2)}) collective-permute-start(f32[144,128]{1,0:T(8,128)} %get-tuple-element.21), channel_id=1, source_target_pairs={{0,16},{16,0},{32,48},{48,32},{64,80},{80,64},{96,112},{112,96},{1... | collective-permute-start | bytes 221192 | tf_op jit(solution)/shard_map/ppermute | solution.py:345
  33.0 5.8 %collective-permute-start.1 = (f32[144,128]{1,0:T(8,128)}, f32[144,128]{1,0:T(8,128)S(1)}, u32[]{:S(2)}, u32[]{:S(2)}) collective-permute-start(f32[144,128]{1,0:T(8,128)} %get-tuple-element.22), channel_id=1, source_target_pairs={{0,32},{16,48},{32,0},{48,16},{64,96},{80,112},{96,64},{112,80},{1... | collective-permute-start | bytes 221192 | tf_op jit(solution)/shard_map/ppermute | solution.py:345
  33.8 8.3 %collective-permute-start.2 = (f32[144,128]{1,0:T(8,128)S(1)}, f32[144,128]{1,0:T(8,128)S(1)}, u32[]{:S(2)}, u32[]{:S(2)}) collective-permute-start(f32[144,128]{1,0:T(8,128)S(1)} %copy-done.5), channel_id=1, source_target_pairs={{0,48},{16,32},{32,16},{48,0},{64,112},{80,96},{96,80},{112,64},{1... | collective-permute-start | bytes 221192 | tf_op jit(solution)/shard_map/ppermute | solution.py:345

commit v4 on v3

--- a/solution.py
+++ b/solution.py
@@ -54,11 +54,6 @@
                     mix[c, b, a, 0, b, kk, a] = cosine_part * scale
                     mix[c, b, a, 1, b, kk, a] = sine_part * scale
     return wave, mix.reshape(256, 1024)
-
-
-def plane_table():
-    angle = 2.0 * np.pi * (np.arange(64)[:, None] * np.arange(128)[None, :] % 128) / 128.0
-    return (np.cos(angle) + np.sin(angle)) / np.sqrt(128.0)
 
 
 def pair_table(half):
@@ -186,11 +181,18 @@
     x_fwd_ref, x_back_ref, y_fwd_ref, y_back_ref, out_ref, green_ref, first_ref, second_ref = refs
     me = lax.axis_index("px")
     half, place = me // 4, me % 4
+    left, middle = iota((16, 128), 1) < 64, iota((16, 128), 1) == 64
     for n in range(4):
         start = pl.multiple_of(jnp.bitwise_xor(place, n) * 16, 16)
+        last = pieces[n][64:80, :]
         for r in range(9):
-            green_ref[r, pl.ds(start, 16), :] = pieces[n][r * 16 : (r + 1) * 16, :]
-    ends = spec_ref[pl.ds(4, 128, stride=5), :].T
+            pair = pieces[n][r // 2 * 16 : (r // 2 + 1) * 16, :]
+            swapped = pltpu.roll(pair, 64, 1)
+            both = jnp.where(left, swapped, pair) if r % 2 else jnp.where(left, pair, swapped)
+            both = jnp.where(middle, last[:, 64 + r : 65 + r], both)
+            green_ref[r, pl.ds(start, 16), :] = both
+    ends = spec_ref[pl.ds(4, 128, stride=5), :].T[:16]
+    ends = jnp.where(left | middle, ends, pltpu.roll(ends, 64, 1))
     y_fwd, y_back, y_low = y_fwd_ref[half], y_back_ref[half, :, :256], y_back_ref[half, :, 256:]
     x_fwd, x_back, x_low = x_fwd_ref[...], x_back_ref[:, :256], x_back_ref[:, 256:]
     for i in range(N_PX):
@@ -264,11 +266,18 @@
     starts = [
         pl.multiple_of((me - me % 4 + jnp.bitwise_xor(me % 4, n)) * 16, 16) for n in range(4)
     ]
+    left = iota((16, 128), 1) < 64
     moves[0].wait()
     for k2 in range(16):
         turned_ref[...] = green_ref[:, k2, :].T
         for n in range(4):
-            piece_ref[n, pl.ds(k2, 9, stride=16), :] = turned_ref[pl.ds(starts[n], 9), :]
+            even = turned_ref[pl.ds(starts[n], 4, stride=2), :]
+            odd = pltpu.roll(turned_ref[pl.ds(starts[n] + 1, 4, stride=2), :], 64, 1)
+            piece_ref[n, pl.ds(k2, 4, stride=16), :] = jnp.where(left[:4], even, odd)
+            piece_ref[n, pl.ds(k2 + 64, 1), :] = turned_ref[pl.ds(starts[n] + 8, 1), :]
+    for n in range(4):
+        ends = pltpu.roll(green_ref[64], 192 - starts[n], 1)
+        piece_ref[n, 64:80, :] = jnp.where(left, piece_ref[n, 64:80, :], ends)
     stores = [pltpu.make_async_copy(piece_ref.at[n], out_refs[n], sems.at[n + 7]) for n in range(4)]
     for move in stores:
         move.start()
@@ -301,7 +310,7 @@
     mix_both = np.concatenate([mix_hi.T, mix_lo.T], axis=0)
     wave_hi, wave_lo = split_table(wave.reshape(9 * 128, 256))
     wave_both = np.concatenate(split_table(wave.transpose(0, 2, 1).reshape(9 * 256, 128)), axis=1)
-    x_fwd, x_back = stacked(plane_table())
+    x_fwd, x_back = stacked(pair_table(0))
     order = np.arange(64).reshape(N_PZ, CYP).T.reshape(64)
     y_fwd, y_back = (np.stack(tables) for tables in zip(stacked(pair_table(0)), stacked(pair_table(1))))
     y_fwd = y_fwd.reshape(2, 3, 64, 128)[:, :, order].reshape(2, 192, 128)
@@ -329,11 +338,11 @@
     ]
     *pieces, mix_both, wave_both, x_fwd, x_back, y_fwd, y_back = call(
         green_kernel,
-        [pltpu.HBM((144, 128), F32)] * 4 + [jax.ShapeDtypeStruct(x.shape, BF) for x in tables],
+        [pltpu.HBM((80, 128), F32)] * 4 + [jax.ShapeDtypeStruct(x.shape, BF) for x in tables],
         [
             pltpu.VMEM((128, 16, 128), F32),
             pltpu.VMEM((128, 128), F32),
-            pltpu.VMEM((4, 144, 128), F32),
+            pltpu.VMEM((4, 80, 128), F32),
             pltpu.SemaphoreType.DMA((11,)),
         ],
         in_specs=[HBM] * 7,

time: 82.6 us -> 81.3 us (0.984)
  blocking collectives: 33.1 us -> 31.7 us
    ppermute x3, waiting for transfers between devices: 7.41 us -> 5.16 us  [local(): green.append(lax.ppermute(pieces[n], 'px', pairs))]
    all_to_all x2, waiting for transfers between devices: 9.64 us -> 11.9 us  [all_to_all(): return lax.all_to_all(x, axes, split_axis=0, concat_axis=0, tiled=True)]
    all_to_all x2, blocking collectives: 33.1 us -> 31.7 us  [all_to_all(): return lax.all_to_all(x, axes, split_axis=0, concat_axis=0, tiled=True)]
where the time goes in v4:
time: 81.3 us; the launch traced here: 81.1 us
  blocking collectives  31.7 us (39%)
  starting transfers between devices  19.3 us (24%)
  waiting for transfers between devices  17 us (21%)
  Pallas kernels  12.9 us (16%)
    all_to_all x2, blocking collectives, all_to_all(): return lax.all_to_all(x, axes, split_axis=0, concat_axis=0, tiled=True)  31.7 us
    all_to_all x2, starting transfers between devices, all_to_all(): return lax.all_to_all(x, axes, split_axis=0, concat_axis=0, tiled=True)  16.3 us
    all_to_all x2, waiting for transfers between devices, all_to_all(): return lax.all_to_all(x, axes, split_axis=0, concat_axis=0, tiled=True)  11.9 us
    ppermute x3, waiting for transfers between devices, local(): green.append(lax.ppermute(pieces[n], 'px', pairs))  5.16 us
    pallas_call x1, Pallas kernels, local(): call(plane_kernel, (512, 128), [pltpu.VMEM((9, 64, 128), F32), pltpu.VMEM...  3.9 us
    ppermute x3, starting transfers between devices, local(): green.append(lax.ppermute(pieces[n], 'px', pairs))  3.02 us
    pallas_call x1, Pallas kernels, local(): call(green_kernel, [pltpu.HBM((80, 128), F32)] * 4 + [jax.ShapeDtypeStruc...  2.77 us
    pallas_call x1, Pallas kernels, local(): call(pack_kernel, [(640, 128), (1, 256)], [pltpu.VMEM((256, 128), F32), p...  2.16 us
  transfers between devices with their start and end apart: 5, of which 4 were waited for; matrix products, arithmetic and copies ran while one was open for 0% of the time, Pallas kernels for 3%

profile of v4, /device:TPU:1, one launch (start us, length us, event | category | flops | bytes accessed | tf_op | source)
XLA Modules:
  0.0 81.1 jit_solution(12053089118152382112)
XLA Ops:
  0.0 2.2 %pack_kernel.1 = (f32[640,128]{1,0:T(8,128)}, f32[1,256]{1,0:T(1,128)S(1)}) custom-call(f32[256,128]{1,0:T(8,128)} %charge_any.1, s32[1,256]{1,0:T(1,128)} %bitcast.17, s32[1,256]{1,0:T(1,128)} %bitcast.18, f32[128,16,128]{2,1,0:T(8,128)} %green_any.3), custom_call_target="tpu_custom_call" | custom-call | tf_op jit(solution)/shard_map/pack_kernel/pallas_call | solution.py:322
  2.2 11.5 %all-to-all-start = ((f32[128,1,640]{2,1,0:T(1,128)}), f32[128,1,640]{2,1,0:T(1,128)S(1)}, u32[]{:S(2)}, u32[]{:S(2)}) async-start(f32[128,1,640]{2,1,0:T(1,128)} %bitcast.2), calls=%async_computation | async-start | bytes 655360 | tf_op jit(solution)/shard_map/all_to_all | solution.py:304
  13.7 2.8 %green_kernel.1 = (f32[80,128]{1,0:T(8,128)}, f32[80,128]{1,0:T(8,128)}, f32[80,128]{1,0:T(8,128)}, f32[80,128]{1,0:T(8,128)}, bf16[2048,256]{1,0:T(8,128)(2,1)S...) custom-call(f32[128,16,128]{2,1,0:T(8,128)} %green_any.3, ...), custom_call_target="tpu_custom_call" | custom-call | tf_op jit(solution)/shard_map/green_kernel/pallas_call | solution.py:339
  16.5 8.6 %all-to-all-done = f32[128,1,640]{2,1,0:T(1,128)S(1)} async-done(((f32[128,1,640]{2,1,0:T(1,128)}), f32[128,1,640]{2,1,0:T(1,128)S(1)}, u32[]{:S(2)}, u32[]{:S(2)}) %all-to-all-start) | async-done | bytes 327712 | tf_op jit(solution)/shard_map/all_to_all | solution.py:304
  25.0 0.0 copy-start.7
  25.1 0.0 copy-start.6
  25.1 0.0 copy-start.5
  25.1 0.0 copy-start.4
  25.1 1.9 %z_forward_kernel.1 = f32[640,128]{1,0:T(8,128)} custom-call(f32[640,128]{1,0:T(8,128)S(1)} %bitcast.10, bf16[2048,256]{1,0:T(8,128)(2,1)S(1)} %get-tuple-element.18.mix_ref, bf16[2304,256]{1,0:T(8,128)(2,1)S(1)} %get-tuple-element.19.wave_ref), custom_call_target="tpu_custom_call" | custom-call | tf_op jit(solution)/shard_map/z_forward_kernel/pallas_call | solution.py:355
  26.9 0.0 copy-start
  26.9 0.0 copy-start.1
  26.9 0.0 copy-start.2
  26.9 0.0 copy-start.3
  26.9 4.8 %all-to-all-start.1 = ((f32[128,1,640]{2,1,0:T(1,128)}), f32[128,1,640]{2,1,0:T(1,128)S(1)}, u32[]{:S(2)}, u32[]{:S(2)}) async-start(f32[128,1,640]{2,1,0:T(1,128)} %bitcast.4), calls=%async_computation.1 | async-start | bytes 655360 | tf_op jit(solution)/shard_map/all_to_all | solution.py:304
  31.8 0.0 copy-done.7
  31.8 1.3 %collective-permute-start = (f32[80,128]{1,0:T(8,128)S(1)}, f32[80,128]{1,0:T(8,128)S(1)}, u32[]{:S(2)}, u32[]{:S(2)}) collective-permute-start(f32[80,128]{1,0:T(8,128)S(1)} %copy-done.7), channel_id=1, source_target_pairs={{0,16},{16,0},{32,48},{48,32},{64,80},{80,64},{96,112},{112,96},{1... | collective-permute-start | bytes 122888 | tf_op jit(solution)/shard_map/ppermute | solution.py:354
  33.1 0.0 copy-done.6
  33.1 0.8 collective-permute-start.1
  33.9 0.0 copy-done.5
  33.9 0.9 %collective-permute-start.2 = (f32[80,128]{1,0:T(8,128)S(1)}, f32[80,128]{1,0:T(8,128)S(1)}, u32[]{:S(2)}, u32[]{:S(2)}) collective-permute-start(f32[80,128]{1,0:T(8,128)S(1)} %copy-done.5), channel_id=1, source_target_pairs={{0,48},{16,32},{32,16},{48,0},{64,112},{80,96},{96,80},{112,64},{1... | collective-permute-start | bytes 122888 | tf_op jit(solution)/shard_map/ppermute | solution.py:354
  34.8 0.0 collective-permute-done.refs_1_
  34.8 2.1 %collective-permute-done.1.refs_2_ = f32[80,128]{1,0:T(8,128)S(1)} collective-permute-done((f32[80,128]{1,0:T(8,128)S(1)}, f32[80,128]{1,0:T(8,128)S(1)}, u32[]{:S(2)}, u32[]{:S(2)}) %collective-permute-start.1) | collective-permute-done | bytes 40992 | tf_op jit(solution)/shard_map/ppermute | solution.py:354
  36.9 3.0 %collective-permute-done.2.refs_3_ = f32[80,128]{1,0:T(8,128)S(1)} collective-permute-done((f32[80,128]{1,0:T(8,128)S(1)}, f32[80,128]{1,0:T(8,128)S(1)}, u32[]{:S(2)}, u32[]{:S(2)}) %collective-permute-start.2) | collective-permute-done | bytes 40992 | tf_op jit(solution)/shard_map/ppermute | solution.py:354
  40.0 3.3 %all-to-all-done.1 = f32[128,1,640]{2,1,0:T(1,128)S(1)} async-done(((f32[128,1,640]{2,1,0:T(1,128)}), f32[128,1,640]{2,1,0:T(1,128)S(1)}, u32[]{:S(2)}, u32[]{:S(2)}) %all-to-all-start.1) | async-done | bytes 327712 | tf_op jit(solution)/shard_map/all_to_all | solution.py:304
  43.3 0.0 copy-done.4
  43.3 3.9 %plane_kernel.1 = f32[512,128]{1,0:T(8,128)S(1)} custom-call(f32[640,128]{1,0:T(8,128)S(1)} %bitcast.12, f32[80,128]{1,0:T(8,128)S(1)} %copy-done.4, f32[80,128]{1,0:T(8,128)S(1)} %collective-permute-done.refs_1_, f32[80,128]{1,0:T(8,128)S(1)} %collective-permute-done.1.refs_2_, f32[80,128]{1,0:T(8,128)S(1)} %collective-permute-done.2.refs_3_, ...), custom_call_target="tpu_custom_call" | custom-call | tf_op jit(solution)/shard_map/plane_kernel/pallas_call | solution.py:357
  47.2 16.5 %all_to_all.20 = f32[128,4,128]{2,1,0:T(4,128)S(1)} all-to-all(f32[128,4,128]{2,1,0:T(4,128)S(1)} %bitcast.16), channel_id=1, replica_groups=mesh['px'=8,'pz'=16] {'px','pz'}, dimensions={0} | all-to-all | bytes 524288 | tf_op jit(solution)/shard_map/all_to_all | solution.py:304
  63.6 0.0 copy-done
  63.6 0.0 copy-done.1
  63.6 0.0 copy-done.2
  63.6 0.0 copy-done.3
  63.7 1.2 %z_back_kernel.1 = f32[512,128]{1,0:T(8,128)S(1)} custom-call(f32[512,128]{1,0:T(8,128)S(1)} %bitcast.13, f32[640,128]{1,0:T(8,128)S(1)} %bitcast.11, bf16[1152,256]{1,0:T(8,128)(2,1)S(1)} %copy-done.1, bf16[1152,256]{1,0:T(8,128)(2,1)S(1)} %copy-done, bf16[256,1024]{1,0:T(8,128)(2,1)S(1)} %copy-done.3, bf16[256,1024]{1,0:T(8,128)(2,1)S(1)} %copy-done.2), custom_call_target="tpu_custom_call" | custom-call | tf_op jit(solution)/shard_map/z_back_kernel/pallas_call | solution.py:367
  64.8 15.2 %all_to_all.21 = f32[128,4,128]{2,1,0:T(4,128)S(1)} all-to-all(f32[128,4,128]{2,1,0:T(4,128)S(1)} %bitcast.14), channel_id=1, replica_groups=mesh['px'=8,'pz'=16] {'px','pz'}, dimensions={0} | all-to-all | bytes 524288 | tf_op jit(solution)/shard_map/all_to_all | solution.py:304
  80.0 1.0 %unpack_kernel.1 = f32[256,128]{1,0:T(8,128)} custom-call(f32[512,128]{1,0:T(8,128)S(1)} %bitcast.15, f32[1,256]{1,0:T(1,128)S(1)} %get-tuple-element.28.place_ref), custom_call_target="tpu_custom_call" | custom-call | tf_op jit(solution)/shard_map/unpack_kernel/pallas_call | solution.py:371
Async XLA Ops:
  2.2 22.9 %all-to-all-start = ((f32[128,1,640]{2,1,0:T(1,128)}), f32[128,1,640]{2,1,0:T(1,128)S(1)}, u32[]{:S(2)}, u32[]{:S(2)}) async-start(f32[128,1,640]{2,1,0:T(1,128)} %bitcast.2), calls=%async_computation | async-start | bytes 655360 | tf_op jit(solution)/shard_map/all_to_all | solution.py:304
  25.0 6.7 %copy-start.7 = (f32[80,128]{1,0:T(8,128)S(1)}, f32[80,128]{1,0:T(8,128)}, u32[]{:S(2)}) copy-start(f32[80,128]{1,0:T(8,128)} %get-tuple-element.21) | copy-start | bytes 122884
  25.1 8.0 %copy-start.6 = (f32[80,128]{1,0:T(8,128)S(1)}, f32[80,128]{1,0:T(8,128)}, u32[]{:S(2)}) copy-start(f32[80,128]{1,0:T(8,128)} %get-tuple-element.22) | copy-start | bytes 122884
  25.1 8.8 %copy-start.5 = (f32[80,128]{1,0:T(8,128)S(1)}, f32[80,128]{1,0:T(8,128)}, u32[]{:S(2)}) copy-start(f32[80,128]{1,0:T(8,128)} %get-tuple-element.23) | copy-start | bytes 122884
  25.1 18.2 %copy-start.4 = (f32[80,128]{1,0:T(8,128)S(1)}, f32[80,128]{1,0:T(8,128)}, u32[]{:S(2)}) copy-start(f32[80,128]{1,0:T(8,128)} %get-tuple-element.20.refs_0_) | copy-start | bytes 122884
  26.9 36.7 %copy-start = (bf16[1152,256]{1,0:T(8,128)(2,1)S(1)}, bf16[1152,256]{1,0:T(8,128)(2,1)}, u32[]{:S(2)}) copy-start(bf16[1152,256]{1,0:T(8,128)(2,1)} %constant.27.clone.wave_lo_ref) | copy-start | bytes 1769476
  26.9 36.7 %copy-start.1 = (bf16[1152,256]{1,0:T(8,128)(2,1)S(1)}, bf16[1152,256]{1,0:T(8,128)(2,1)}, u32[]{:S(2)}) copy-start(bf16[1152,256]{1,0:T(8,128)(2,1)} %constant.26.clone.wave_hi_ref) | copy-start | bytes 1769476
  26.9 36.7 %copy-start.2 = (bf16[256,1024]{1,0:T(8,128)(2,1)S(1)}, bf16[256,1024]{1,0:T(8,128)(2,1)}, u32[]{:S(2)}) copy-start(bf16[256,1024]{1,0:T(8,128)(2,1)} %constant.29.clone.mix_lo_ref) | copy-start | bytes 1572868
  26.9 36.7 %copy-start.3 = (bf16[256,1024]{1,0:T(8,128)(2,1)S(1)}, bf16[256,1024]{1,0:T(8,128)(2,1)}, u32[]{:S(2)}) copy-start(bf16[256,1024]{1,0:T(8,128)(2,1)} %constant.28.clone.mix_hi_ref) | copy-start | bytes 1572868
  26.9 16.3 %all-to-all-start.1 = ((f32[128,1,640]{2,1,0:T(1,128)}), f32[128,1,640]{2,1,0:T(1,128)S(1)}, u32[]{:S(2)}, u32[]{:S(2)}) async-start(f32[128,1,640]{2,1,0:T(1,128)} %bitcast.4), calls=%async_computation.1 | async-start | bytes 655360 | tf_op jit(solution)/shard_map/all_to_all | solution.py:304
  31.8 3.0 %collective-permute-start = (f32[80,128]{1,0:T(8,128)S(1)}, f32[80,128]{1,0:T(8,128)S(1)}, u32[]{:S(2)}, u32[]{:S(2)}) collective-permute-start(f32[80,128]{1,0:T(8,128)S(1)} %copy-done.7), channel_id=1, source_target_pairs={{0,16},{16,0},{32,48},{48,32},{64,80},{80,64},{96,112},{112,96},{1... | collective-permute-start | bytes 122888 | tf_op jit(solution)/shard_map/ppermute | solution.py:354
  33.1 3.9 %collective-permute-start.1 = (f32[80,128]{1,0:T(8,128)S(1)}, f32[80,128]{1,0:T(8,128)S(1)}, u32[]{:S(2)}, u32[]{:S(2)}) collective-permute-start(f32[80,128]{1,0:T(8,128)S(1)} %copy-done.6), channel_id=1, source_target_pairs={{0,32},{16,48},{32,0},{48,16},{64,96},{80,112},{96,64},{112,80},{1... | collective-permute-start | bytes 122888 | tf_op jit(solution)/shard_map/ppermute | solution.py:354
  33.9 6.1 %collective-permute-start.2 = (f32[80,128]{1,0:T(8,128)S(1)}, f32[80,128]{1,0:T(8,128)S(1)}, u32[]{:S(2)}, u32[]{:S(2)}) collective-permute-start(f32[80,128]{1,0:T(8,128)S(1)} %copy-done.5), channel_id=1, source_target_pairs={{0,48},{16,32},{32,16},{48,0},{64,112},{80,96},{96,80},{112,64},{1... | collective-permute-start | bytes 122888 | tf_op jit(solution)/shard_map/ppermute | solution.py:354

commit v5 on v4

--- a/solution.py
+++ b/solution.py
@@ -68,7 +68,10 @@
 
 def stacked(table):
     high, low = split_table(table)
-    return np.concatenate([high, high, low], axis=0), np.concatenate([high, high, low], axis=1)
+    none = np.zeros_like(low)
+    fwd = np.block([[high, low], [high, none]])
+    back = np.block([[high.T, low.T], [high.T, none.T]])
+    return fwd, back
 
 
 def iota(shape, axis):
@@ -87,12 +90,21 @@
     return high, middle, (rest - middle.astype(F32)).astype(BF)
 
 
+def turned_pair(x):
+    high = x.astype(BF).astype(F32)
+    return jnp.concatenate([high, x - high], axis=0).T.astype(BF)
+
+
+def halves(x, size):
+    return x[:, :size] + x[:, size:]
+
+
 def dot(a, b, a_axis=1, b_axis=0):
     return lax.dot_general(a, b, (((a_axis,), (b_axis,)), ((), ())), preferred_element_type=F32)
 
 
 def pack_kernel(
-    charge_any, dest_any, ids_any, green_any, send_ref, place_ref, charge_ref, dest_ref, ids_ref, plane_ref, sems
+    charge_any, dest_any, ids_any, green_any, send_ref, place_ref, green_ref, charge_ref, dest_ref, ids_ref, sems
 ):
     moves = [
         pltpu.make_async_copy(source, target, sems.at[n])
@@ -101,7 +113,7 @@
                 (dest_any, dest_ref),
                 (ids_any, ids_ref),
                 (charge_any, charge_ref),
-                (green_any.at[:, 0, :], plane_ref),
+                (green_any, green_ref),
             ]
         )
     ]
@@ -121,7 +133,7 @@
     ids = jnp.broadcast_to(ids_ref[...], (128, 256)).astype(F32)
     lane = iota((128, 128), 1)
     moves[3].wait()
-    named = plane_ref[...]
+    named = green_ref[:, 0, :]
     hots = []
     for slot in range(CAP):
         chosen = here & (rank == slot)
@@ -178,7 +190,7 @@
 
 def plane_kernel(spec_ref, *refs):
     pieces, refs = refs[:4], refs[4:]
-    x_fwd_ref, x_back_ref, y_fwd_ref, y_back_ref, out_ref, green_ref, first_ref, second_ref = refs
+    x_fwd_ref, x_back_ref, y_fwd_ref, y_back_ref, out_ref, green_ref, first_ref, second_ref, line_ref = refs
     me = lax.axis_index("px")
     half, place = me // 4, me % 4
     left, middle = iota((16, 128), 1) < 64, iota((16, 128), 1) == 64
@@ -193,30 +205,35 @@
             green_ref[r, pl.ds(start, 16), :] = both
     ends = spec_ref[pl.ds(4, 128, stride=5), :].T[:16]
     ends = jnp.where(left | middle, ends, pltpu.roll(ends, 64, 1))
-    y_fwd, y_back, y_low = y_fwd_ref[half], y_back_ref[half, :, :256], y_back_ref[half, :, 256:]
-    x_fwd, x_back, x_low = x_fwd_ref[...], x_back_ref[:, :256], x_back_ref[:, 256:]
+    y_fwd, y_back, x_fwd, x_back = y_fwd_ref[half], y_back_ref[half], x_fwd_ref[...], x_back_ref[...]
     for i in range(N_PX):
-        rows = [spec_ref[pl.ds(i * 80 + b, 16, stride=5), :] for b in range(CYP)]
-        high, low = two(jnp.concatenate(rows, axis=0))
-        turned = dot(jnp.concatenate([high, low, high], axis=0), y_fwd, 0, 0)
+        rows = jnp.concatenate([spec_ref[pl.ds(i * 80 + b, 16, stride=5), :] for b in range(CYP)], axis=0)
+        line_ref[i * 128 : (i + 1) * 128, :] = turned_pair(rows)
+    turned = halves(dot(line_ref[...], y_fwd), 128)
+    for i in range(N_PX):
         for kk in range(16):
-            first_ref[kk, i * 8 : (i + 1) * 8, :] = turned[kk * 8 : (kk + 1) * 8]
+            row = i * 128 + kk * 8
+            first_ref[kk, i * 8 : (i + 1) * 8, :] = turned[row : row + 8]
     top = iota((64, 128), 0) == 0
-    for kk in range(16):
-        high, low = two(first_ref[kk])
-        full = dot(jnp.concatenate([high, low, high], axis=0), x_fwd, 0, 0)
-        r = RESIDUE[kk]
-        green = green_ref[r]
-        other = jnp.where(top, ends[r : r + 1, :], green)
-        full = jnp.concatenate([full[:64] * green, full[64:] * other], axis=0)
-        high, low = two(full)
-        second_ref[kk] = dot(x_back, jnp.concatenate([high, low], axis=1), 1, 1) + dot(x_low, high, 1, 1)
+    for group in range(4):
+        rows = jnp.concatenate([turned_pair(first_ref[group * 4 + n]) for n in range(4)], axis=0)
+        full = halves(dot(rows, x_fwd), 128)
+        scaled = []
+        for n in range(4):
+            r = RESIDUE[group * 4 + n]
+            green = green_ref[r]
+            other = jnp.where(top, ends[r : r + 1, :], green)
+            scaled += [full[n * 128 : n * 128 + 64] * green, full[n * 128 + 64 : (n + 1) * 128] * other]
+        high, low = two(jnp.concatenate(scaled, axis=0))
+        cells = dot(jnp.concatenate([high, low], axis=1), x_back)
+        for n in range(4):
+            pair = cells[n * 128 : (n + 1) * 128].T
+            second_ref[group * 4 + n] = pair[:64] + pair[64:]
     for i in range(N_PX):
         rows = jnp.concatenate([second_ref[kk, i * 8 : (i + 1) * 8, :] for kk in range(16)], axis=0)
         high, low = two(rows)
-        out_ref[i * 64 : (i + 1) * 64, :] = dot(y_back, jnp.concatenate([high, low], axis=1), 1, 1) + dot(
-            y_low, high, 1, 1
-        )
+        pair = dot(y_back, jnp.concatenate([high, low], axis=1), 0, 1)
+        out_ref[i * 64 : (i + 1) * 64, :] = pair[:64] + pair[64:]
 
 
 def z_back_kernel(spec_ref, recv_ref, wave_hi_ref, wave_lo_ref, mix_hi_ref, mix_lo_ref, out_ref, turned_ref, line_ref):
@@ -255,19 +272,13 @@
     out_ref[...] = rows[:, :128] + rows[:, 128:256] + rows[:, 256:]
 
 
-def green_kernel(green_any, *refs):
-    tables, out_refs, copies, (green_ref, turned_ref, piece_ref, sems) = refs[:6], refs[6:10], refs[10:16], refs[16:]
+def green_kernel(green_ref, *refs):
+    out_refs, (turned_ref, piece_ref, sems) = refs[:4], refs[4:]
     me = lax.axis_index("px")
-    moves = [pltpu.make_async_copy(green_any, green_ref, sems.at[0])]
-    for n in range(6):
-        moves.append(pltpu.make_async_copy(tables[n], copies[n], sems.at[n + 1]))
-    for move in moves:
-        move.start()
     starts = [
         pl.multiple_of((me - me % 4 + jnp.bitwise_xor(me % 4, n)) * 16, 16) for n in range(4)
     ]
     left = iota((16, 128), 1) < 64
-    moves[0].wait()
     for k2 in range(16):
         turned_ref[...] = green_ref[:, k2, :].T
         for n in range(4):
@@ -278,10 +289,19 @@
     for n in range(4):
         ends = pltpu.roll(green_ref[64], 192 - starts[n], 1)
         piece_ref[n, 64:80, :] = jnp.where(left, piece_ref[n, 64:80, :], ends)
-    stores = [pltpu.make_async_copy(piece_ref.at[n], out_refs[n], sems.at[n + 7]) for n in range(4)]
+    stores = [pltpu.make_async_copy(piece_ref.at[n], out_refs[n], sems.at[n]) for n in range(4)]
     for move in stores:
         move.start()
-    for move in moves[1:] + stores:
+    for move in stores:
+        move.wait()
+
+
+def table_kernel(*refs):
+    tables, copies, sems = refs[:6], refs[6:12], refs[12]
+    moves = [pltpu.make_async_copy(tables[n], copies[n], sems.at[n]) for n in range(6)]
+    for move in moves:
+        move.start()
+    for move in moves:
         move.wait()
 
 
@@ -313,20 +333,19 @@
     x_fwd, x_back = stacked(pair_table(0))
     order = np.arange(64).reshape(N_PZ, CYP).T.reshape(64)
     y_fwd, y_back = (np.stack(tables) for tables in zip(stacked(pair_table(0)), stacked(pair_table(1))))
-    y_fwd = y_fwd.reshape(2, 3, 64, 128)[:, :, order].reshape(2, 192, 128)
+    y_fwd = y_fwd.reshape(2, 2, 64, 256)[:, :, order].reshape(2, 128, 256)
 
     charge, dest, local_ids, green_hat = (
         pltpu.with_memory_space_constraint(x, pltpu.HBM)
         for x in (charge, dest.reshape(1, 256), local_ids.reshape(1, 256), green_hat)
     )
-    send, place = call(
+    send, place, green_hat = call(
         pack_kernel,
-        [(640, 128), (1, 256)],
+        [(640, 128), (1, 256), (128, 16, 128)],
         [
             pltpu.VMEM((256, 128), F32),
             pltpu.VMEM((1, 256), jnp.int32),
             pltpu.VMEM((1, 256), jnp.int32),
-            pltpu.VMEM((128, 128), F32),
             pltpu.SemaphoreType.DMA((4,)),
         ],
         in_specs=[HBM] * 4,
@@ -336,22 +355,23 @@
         pltpu.with_memory_space_constraint(jnp.asarray(x), pltpu.HBM)
         for x in (mix_both, wave_both, x_fwd, x_back, y_fwd, y_back)
     ]
-    *pieces, mix_both, wave_both, x_fwd, x_back, y_fwd, y_back = call(
+    pieces = call(
         green_kernel,
-        [pltpu.HBM((80, 128), F32)] * 4 + [jax.ShapeDtypeStruct(x.shape, BF) for x in tables],
-        [
-            pltpu.VMEM((128, 16, 128), F32),
-            pltpu.VMEM((128, 128), F32),
-            pltpu.VMEM((4, 80, 128), F32),
-            pltpu.SemaphoreType.DMA((11,)),
-        ],
-        in_specs=[HBM] * 7,
-        out_specs=[HBM] * 4 + [VMEM] * 6,
-    )(green_hat, *tables)
+        [pltpu.HBM((80, 128), F32)] * 4,
+        [pltpu.VMEM((128, 128), F32), pltpu.VMEM((4, 80, 128), F32), pltpu.SemaphoreType.DMA((4,))],
+        out_specs=[HBM] * 4,
+    )(green_hat)
+    mix_both, wave_both, x_fwd, x_back, y_fwd, y_back = call(
+        table_kernel,
+        [jax.ShapeDtypeStruct(x.shape, BF) for x in tables],
+        [pltpu.SemaphoreType.DMA((6,))],
+        in_specs=[HBM] * 6,
+    )(*tables)
     green = [pieces[0]]
     for n in range(1, 4):
         pairs = [(i, i // 4 * 4 + ((i % 4) ^ n)) for i in range(N_PX)]
         green.append(lax.ppermute(pieces[n], "px", pairs))
+    recv, green = lax.optimization_barrier((recv, green))
     lines = call(z_forward_kernel, (640, 128), [pltpu.VMEM((512, 128), F32)])(recv, mix_both, wave_both)
     planes = all_to_all(lines.reshape(N_DEV, 1, 640), BOTH).reshape(640, 128)
     planes = call(
@@ -361,6 +381,7 @@
             pltpu.VMEM((9, 64, 128), F32),
             pltpu.VMEM((16, 64, 128), F32),
             pltpu.VMEM((16, 64, 128), F32),
+            pltpu.VMEM((1024, 128), BF),
         ],
     )(planes, *green, x_fwd, x_back, y_fwd, y_back)
     lines = all_to_all(planes.reshape(N_DEV, 4, 128), BOTH).reshape(512, 128)

time: 81.3 us -> 78.2 us (0.962)
  blocking collectives: 31.7 us -> 47.5 us
  waiting for transfers between devices: 17 us -> 5.29 us
  starting transfers between devices: 19.3 us -> 14.4 us
  Pallas kernels: 12.9 us -> 10.7 us
    all_to_all x2 -> x3, blocking collectives: 31.7 us -> 47.5 us  [all_to_all(): return lax.all_to_all(x, axes, split_axis=0, concat_axis=0, tiled=True)]
    all_to_all x2 -> x1, waiting for transfers between devices: 11.9 us -> 2.02 us  [all_to_all(): return lax.all_to_all(x, axes, split_axis=0, concat_axis=0, tiled=True)]
    all_to_all x2 -> x1, starting transfers between devices: 16.3 us -> 11.5 us  [all_to_all(): return lax.all_to_all(x, axes, split_axis=0, concat_axis=0, tiled=True)]
    pallas_call x1, Pallas kernels: 3.9 us -> 1.65 us  [local(): call(plane_kernel, (512, 128), [pltpu.VMEM((9, 64, 128), F32), pltpu.VMEM...]
    ppermute x3, waiting for transfers between devices: 5.16 us -> 3.28 us  [local(): green.append(lax.ppermute(pieces[n], 'px', pairs))]
    pallas_call x2 -> x3, Pallas kernels: 4.93 us -> 5.73 us  [the longest x1 2.56 us: local(): call(pack_kernel, [(640, 128), (1, 256), (128, 16, 128)], [pltpu.VMEM((25...]
  transfers between devices with their start and end apart: 5 -> 4, of which waited for: 4 -> 3; matrix products, arithmetic and copies ran while one was open for 0% -> 0% of each run, Pallas kernels for 3% -> 4%
where the time goes in v5:
time: 78.2 us; the launch traced here: 77.9 us
  blocking collectives  47.5 us (61%)
  starting transfers between devices  14.4 us (18%)
  Pallas kernels  10.7 us (14%)
  waiting for transfers between devices  5.29 us (7%)
    all_to_all x3, blocking collectives, all_to_all(): return lax.all_to_all(x, axes, split_axis=0, concat_axis=0, tiled=True)  47.5 us
    all_to_all x1, starting transfers between devices, all_to_all(): return lax.all_to_all(x, axes, split_axis=0, concat_axis=0, tiled=True)  11.5 us
    ppermute x3, waiting for transfers between devices, local(): green.append(lax.ppermute(pieces[n], 'px', pairs))  3.28 us
    ppermute x3, starting transfers between devices, local(): green.append(lax.ppermute(pieces[n], 'px', pairs))  2.87 us
    pallas_call x1, Pallas kernels, local(): call(pack_kernel, [(640, 128), (1, 256), (128, 16, 128)], [pltpu.VMEM((25...  2.56 us
    all_to_all x1, waiting for transfers between devices, all_to_all(): return lax.all_to_all(x, axes, split_axis=0, concat_axis=0, tiled=True)  2.02 us
    pallas_call x1, Pallas kernels, local(): call(table_kernel, [jax.ShapeDtypeStruct(x.shape, BF) for x in tables], [...  1.7 us
    pallas_call x1, Pallas kernels, local(): call(plane_kernel, (512, 128), [pltpu.VMEM((9, 64, 128), F32), pltpu.VMEM...  1.65 us
  transfers between devices with their start and end apart: 4, of which 3 were waited for; matrix products, arithmetic and copies ran while one was open for 0% of the time, Pallas kernels for 4%

profile of v5, /device:TPU:1, one launch (start us, length us, event | category | flops | bytes accessed | tf_op | source)
XLA Modules:
  0.0 77.9 jit_solution(1812069325264814752)
XLA Ops:
  0.0 2.6 %pack_kernel.1 = (f32[640,128]{1,0:T(8,128)}, f32[1,256]{1,0:T(1,128)S(1)}, f32[128,16,128]{2,1,0:T(8,128)S(1)}) custom-call(f32[256,128]{1,0:T(8,128)} %charge_any.1, s32[1,256]{1,0:T(1,128)} %bitcast.18, s32[1,256]{1,0:T(1,128)} %bitcast.19, f32[128,16,128]{2,1,0:T(8,128)} %green_any.1), custom_call_target="tpu_custom_call" | custom-call | tf_op jit(solution)/shard_map/pack_kernel/pallas_call | solution.py:342
  2.6 11.5 %all-to-all-start = ((f32[128,1,640]{2,1,0:T(1,128)}), f32[128,1,640]{2,1,0:T(1,128)S(1)}, u32[]{:S(2)}, u32[]{:S(2)}) async-start(f32[128,1,640]{2,1,0:T(1,128)} %bitcast.2), calls=%async_computation | async-start | bytes 655360 | tf_op jit(solution)/shard_map/all_to_all | solution.py:324
  14.1 1.5 %green_kernel.1 = (f32[80,128]{1,0:T(8,128)}, f32[80,128]{1,0:T(8,128)}, f32[80,128]{1,0:T(8,128)}, f32[80,128]{1,0:T(8,128)}) custom-call(f32[128,16,128]{2,1,0:T(8,128)S(1)} %get-tuple-element.24.green_ref), custom_call_target="tpu_custom_call" | custom-call | tf_op jit(solution)/shard_map/green_kernel/pallas_call | solution.py:358
  15.6 1.1 %collective-permute-start = (f32[80,128]{1,0:T(8,128)}, f32[80,128]{1,0:T(8,128)S(1)}, u32[]{:S(2)}, u32[]{:S(2)}) collective-permute-start(f32[80,128]{1,0:T(8,128)} %get-tuple-element.26), channel_id=1, source_target_pairs={{0,16},{16,0},{32,48},{48,32},{64,80},{80,64},{96,112},{112,96},{1... | collective-permute-start | bytes 122888 | tf_op jit(solution)/shard_map/ppermute | solution.py:373
  16.7 0.8 %collective-permute-start.1 = (f32[80,128]{1,0:T(8,128)}, f32[80,128]{1,0:T(8,128)S(1)}, u32[]{:S(2)}, u32[]{:S(2)}) collective-permute-start(f32[80,128]{1,0:T(8,128)} %get-tuple-element.27), channel_id=1, source_target_pairs={{0,32},{16,48},{32,0},{48,16},{64,96},{80,112},{96,64},{112,80},{1... | collective-permute-start | bytes 122888 | tf_op jit(solution)/shard_map/ppermute | solution.py:373
  17.5 0.9 %collective-permute-start.2 = (f32[80,128]{1,0:T(8,128)}, f32[80,128]{1,0:T(8,128)S(1)}, u32[]{:S(2)}, u32[]{:S(2)}) collective-permute-start(f32[80,128]{1,0:T(8,128)} %get-tuple-element.28), channel_id=1, source_target_pairs={{0,48},{16,32},{32,16},{48,0},{64,112},{80,96},{96,80},{112,64},{1... | collective-permute-start | bytes 122888 | tf_op jit(solution)/shard_map/ppermute | solution.py:373
  18.4 1.7 %table_kernel.1 = (bf16[2048,256]{1,0:T(8,128)(2,1)S(1)}, bf16[2304,256]{1,0:T(8,128)(2,1)S(1)}, bf16[128,256]{1,0:T(8,128)(2,1)S(1)}, bf16[256,128]{1,0:T(8,128...) custom-call(bf16[2048,256]{1,0:T(8,128)(2,1)} %constant.20.clone.refs_0_, ...), custom_call_target="tpu_custom_call" | custom-call | tf_op jit(solution)/shard_map/table_kernel/pallas_call | solution.py:364
  20.1 0.0 collective-permute-done.refs_1_
  20.1 1.4 %collective-permute-done.1.refs_2_ = f32[80,128]{1,0:T(8,128)S(1)} collective-permute-done((f32[80,128]{1,0:T(8,128)}, f32[80,128]{1,0:T(8,128)S(1)}, u32[]{:S(2)}, u32[]{:S(2)}) %collective-permute-start.1) | collective-permute-done | bytes 40992 | tf_op jit(solution)/shard_map/ppermute | solution.py:373
  21.6 1.8 %collective-permute-done.2.refs_3_ = f32[80,128]{1,0:T(8,128)S(1)} collective-permute-done((f32[80,128]{1,0:T(8,128)}, f32[80,128]{1,0:T(8,128)S(1)}, u32[]{:S(2)}, u32[]{:S(2)}) %collective-permute-start.2) | collective-permute-done | bytes 40992 | tf_op jit(solution)/shard_map/ppermute | solution.py:373
  23.4 2.0 %all-to-all-done = f32[128,1,640]{2,1,0:T(1,128)S(1)} async-done(((f32[128,1,640]{2,1,0:T(1,128)}), f32[128,1,640]{2,1,0:T(1,128)S(1)}, u32[]{:S(2)}, u32[]{:S(2)}) %all-to-all-start) | async-done | bytes 327712 | tf_op jit(solution)/shard_map/all_to_all | solution.py:324
  25.4 0.0 copy-start.4
  25.4 1.1 %z_forward_kernel.1 = f32[640,128]{1,0:T(8,128)S(1)} custom-call(f32[640,128]{1,0:T(8,128)S(1)} %bitcast.10, bf16[2048,256]{1,0:T(8,128)(2,1)S(1)} %get-tuple-element.30.mix_ref, bf16[2304,256]{1,0:T(8,128)(2,1)S(1)} %get-tuple-element.31.wave_ref), custom_call_target="tpu_custom_call" | custom-call | tf_op jit(solution)/shard_map/z_forward_kernel/pallas_call | solution.py:375
  26.6 0.0 copy-start
  26.6 0.0 copy-start.1
  26.6 0.0 copy-start.2
  26.6 0.0 copy-start.3
  26.6 16.6 %all_to_all.20 = f32[128,1,640]{2,1,0:T(1,128)S(1)} all-to-all(f32[128,1,640]{2,1,0:T(1,128)S(1)} %bitcast.13), channel_id=1, replica_groups=mesh['px'=8,'pz'=16] {'px','pz'}, dimensions={0} | all-to-all | bytes 655360 | tf_op jit(solution)/shard_map/all_to_all | solution.py:324
  43.2 0.0 copy-done.4
  43.2 1.6 %plane_kernel.1 = f32[512,128]{1,0:T(8,128)S(1)} custom-call(f32[640,128]{1,0:T(8,128)S(1)} %bitcast.12, f32[80,128]{1,0:T(8,128)S(1)} %copy-done.4, f32[80,128]{1,0:T(8,128)S(1)} %collective-permute-done.refs_1_, f32[80,128]{1,0:T(8,128)S(1)} %collective-permute-done.1.refs_2_, f32[80,128]{1,0:T(8,128)S(1)} %collective-permute-done.2.refs_3_, ...), custom_call_target="tpu_custom_call" | custom-call | tf_op jit(solution)/shard_map/plane_kernel/pallas_call | solution.py:377
  44.8 15.7 %all_to_all.21 = f32[128,4,128]{2,1,0:T(4,128)S(1)} all-to-all(f32[128,4,128]{2,1,0:T(4,128)S(1)} %bitcast.17), channel_id=1, replica_groups=mesh['px'=8,'pz'=16] {'px','pz'}, dimensions={0} | all-to-all | bytes 524288 | tf_op jit(solution)/shard_map/all_to_all | solution.py:324
  60.5 0.0 copy-done
  60.5 0.0 copy-done.1
  60.5 0.0 copy-done.2
  60.5 0.0 copy-done.3
  60.5 1.2 %z_back_kernel.1 = f32[512,128]{1,0:T(8,128)S(1)} custom-call(f32[512,128]{1,0:T(8,128)S(1)} %bitcast.14, f32[640,128]{1,0:T(8,128)S(1)} %bitcast.11, bf16[1152,256]{1,0:T(8,128)(2,1)S(1)} %copy-done.1, bf16[1152,256]{1,0:T(8,128)(2,1)S(1)} %copy-done, bf16[256,1024]{1,0:T(8,128)(2,1)S(1)} %copy-done.3, bf16[256,1024]{1,0:T(8,128)(2,1)S(1)} %copy-done.2), custom_call_target="tpu_custom_call" | custom-call | tf_op jit(solution)/shard_map/z_back_kernel/pallas_call | solution.py:388
  61.7 15.2 %all_to_all.22 = f32[128,4,128]{2,1,0:T(4,128)S(1)} all-to-all(f32[128,4,128]{2,1,0:T(4,128)S(1)} %bitcast.15), channel_id=1, replica_groups=mesh['px'=8,'pz'=16] {'px','pz'}, dimensions={0} | all-to-all | bytes 524288 | tf_op jit(solution)/shard_map/all_to_all | solution.py:324
  76.9 1.0 %unpack_kernel.1 = f32[256,128]{1,0:T(8,128)} custom-call(f32[512,128]{1,0:T(8,128)S(1)} %bitcast.16, f32[1,256]{1,0:T(1,128)S(1)} %get-tuple-element.40.place_ref), custom_call_target="tpu_custom_call" | custom-call | tf_op jit(solution)/shard_map/unpack_kernel/pallas_call | solution.py:392
Async XLA Ops:
  2.6 22.9 %all-to-all-start = ((f32[128,1,640]{2,1,0:T(1,128)}), f32[128,1,640]{2,1,0:T(1,128)S(1)}, u32[]{:S(2)}, u32[]{:S(2)}) async-start(f32[128,1,640]{2,1,0:T(1,128)} %bitcast.2), calls=%async_computation | async-start | bytes 655360 | tf_op jit(solution)/shard_map/all_to_all | solution.py:324
  15.6 4.6 %collective-permute-start = (f32[80,128]{1,0:T(8,128)}, f32[80,128]{1,0:T(8,128)S(1)}, u32[]{:S(2)}, u32[]{:S(2)}) collective-permute-start(f32[80,128]{1,0:T(8,128)} %get-tuple-element.26), channel_id=1, source_target_pairs={{0,16},{16,0},{32,48},{48,32},{64,80},{80,64},{96,112},{112,96},{1... | collective-permute-start | bytes 122888 | tf_op jit(solution)/shard_map/ppermute | solution.py:373
  16.7 4.9 %collective-permute-start.1 = (f32[80,128]{1,0:T(8,128)}, f32[80,128]{1,0:T(8,128)S(1)}, u32[]{:S(2)}, u32[]{:S(2)}) collective-permute-start(f32[80,128]{1,0:T(8,128)} %get-tuple-element.27), channel_id=1, source_target_pairs={{0,32},{16,48},{32,0},{48,16},{64,96},{80,112},{96,64},{112,80},{1... | collective-permute-start | bytes 122888 | tf_op jit(solution)/shard_map/ppermute | solution.py:373
  17.5 5.9 %collective-permute-start.2 = (f32[80,128]{1,0:T(8,128)}, f32[80,128]{1,0:T(8,128)S(1)}, u32[]{:S(2)}, u32[]{:S(2)}) collective-permute-start(f32[80,128]{1,0:T(8,128)} %get-tuple-element.28), channel_id=1, source_target_pairs={{0,48},{16,32},{32,16},{48,0},{64,112},{80,96},{96,80},{112,64},{1... | collective-permute-start | bytes 122888 | tf_op jit(solution)/shard_map/ppermute | solution.py:373
  25.4 17.8 %copy-start.4 = (f32[80,128]{1,0:T(8,128)S(1)}, f32[80,128]{1,0:T(8,128)}, u32[]{:S(2)}) copy-start(f32[80,128]{1,0:T(8,128)} %get-tuple-element.32.refs_0_) | copy-start | bytes 122884
  26.6 33.9 %copy-start = (bf16[1152,256]{1,0:T(8,128)(2,1)S(1)}, bf16[1152,256]{1,0:T(8,128)(2,1)}, u32[]{:S(2)}) copy-start(bf16[1152,256]{1,0:T(8,128)(2,1)} %constant.27.clone.wave_lo_ref) | copy-start | bytes 1769476
  26.6 33.9 %copy-start.1 = (bf16[1152,256]{1,0:T(8,128)(2,1)S(1)}, bf16[1152,256]{1,0:T(8,128)(2,1)}, u32[]{:S(2)}) copy-start(bf16[1152,256]{1,0:T(8,128)(2,1)} %constant.26.clone.wave_hi_ref) | copy-start | bytes 1769476
  26.6 33.9 %copy-start.2 = (bf16[256,1024]{1,0:T(8,128)(2,1)S(1)}, bf16[256,1024]{1,0:T(8,128)(2,1)}, u32[]{:S(2)}) copy-start(bf16[256,1024]{1,0:T(8,128)(2,1)} %constant.29.clone.mix_lo_ref) | copy-start | bytes 1572868
  26.6 33.9 %copy-start.3 = (bf16[256,1024]{1,0:T(8,128)(2,1)S(1)}, bf16[256,1024]{1,0:T(8,128)(2,1)}, u32[]{:S(2)}) copy-start(bf16[256,1024]{1,0:T(8,128)(2,1)} %constant.28.clone.mix_hi_ref) | copy-start | bytes 1572868

commit v6 on v5

--- a/solution.py
+++ b/solution.py
@@ -113,7 +113,7 @@
                 (dest_any, dest_ref),
                 (ids_any, ids_ref),
                 (charge_any, charge_ref),
-                (green_any, green_ref),
+                (green_any.at[:72], green_ref),
             ]
         )
     ]
@@ -132,8 +132,7 @@
     moves[1].wait()
     ids = jnp.broadcast_to(ids_ref[...], (128, 256)).astype(F32)
     lane = iota((128, 128), 1)
-    moves[3].wait()
-    named = green_ref[:, 0, :]
+    named = jnp.zeros((128, 128), F32)
     hots = []
     for slot in range(CAP):
         chosen = here & (rank == slot)
@@ -146,7 +145,9 @@
     moved = moved[:, :128] + moved[:, 128:256] + moved[:, 256:]
     for slot in range(CAP):
         send_ref[pl.ds(slot, 128, stride=5), :] = moved[slot * 128 : (slot + 1) * 128]
-    send_ref[pl.ds(4, 128, stride=5), :] = named
+    moves[3].wait()
+    plane = jnp.concatenate([green_ref[:, 0, :], jnp.zeros((56, 128), F32)], axis=0)
+    send_ref[pl.ds(4, 128, stride=5), :] = jnp.where((lane >= 9) & (lane < 9 + CAP), named, plane)
 
 
 def block_name(index):
@@ -193,18 +194,19 @@
     x_fwd_ref, x_back_ref, y_fwd_ref, y_back_ref, out_ref, green_ref, first_ref, second_ref, line_ref = refs
     me = lax.axis_index("px")
     half, place = me // 4, me % 4
-    left, middle = iota((16, 128), 1) < 64, iota((16, 128), 1) == 64
+    left, middle = iota((8, 128), 1) < 64, iota((8, 128), 1) == 64
     for n in range(4):
         start = pl.multiple_of(jnp.bitwise_xor(place, n) * 16, 16)
-        last = pieces[n][64:80, :]
+        last = pieces[n][72:80, :]
         for r in range(9):
-            pair = pieces[n][r // 2 * 16 : (r // 2 + 1) * 16, :]
+            pair = pieces[n][r * 8 : (r + 1) * 8, :]
             swapped = pltpu.roll(pair, 64, 1)
-            both = jnp.where(left, swapped, pair) if r % 2 else jnp.where(left, pair, swapped)
-            both = jnp.where(middle, last[:, 64 + r : 65 + r], both)
-            green_ref[r, pl.ds(start, 16), :] = both
+            low = jnp.where(middle, last[:, r : r + 1], jnp.where(left, pair, swapped))
+            high = jnp.where(middle, last[:, 64 + r : 65 + r], jnp.where(left, swapped, pair))
+            green_ref[r, pl.ds(start, 16), :] = jnp.concatenate([low, high], axis=0)
     ends = spec_ref[pl.ds(4, 128, stride=5), :].T[:16]
-    ends = jnp.where(left | middle, ends, pltpu.roll(ends, 64, 1))
+    lane = iota((16, 128), 1)
+    ends = jnp.where(lane <= 64, ends, pltpu.roll(ends, 64, 1))
     y_fwd, y_back, x_fwd, x_back = y_fwd_ref[half], y_back_ref[half], x_fwd_ref[...], x_back_ref[...]
     for i in range(N_PX):
         rows = jnp.concatenate([spec_ref[pl.ds(i * 80 + b, 16, stride=5), :] for b in range(CYP)], axis=0)
@@ -278,17 +280,18 @@
     starts = [
         pl.multiple_of((me - me % 4 + jnp.bitwise_xor(me % 4, n)) * 16, 16) for n in range(4)
     ]
-    left = iota((16, 128), 1) < 64
-    for k2 in range(16):
-        turned_ref[...] = green_ref[:, k2, :].T
+    left = iota((8, 128), 1) < 64
+    for k2 in range(8):
+        both = jnp.concatenate([green_ref[:64, k2, :], green_ref[:64, k2 + 8, :]], axis=0)
+        turned_ref[...] = both.T
         for n in range(4):
-            even = turned_ref[pl.ds(starts[n], 4, stride=2), :]
-            odd = pltpu.roll(turned_ref[pl.ds(starts[n] + 1, 4, stride=2), :], 64, 1)
-            piece_ref[n, pl.ds(k2, 4, stride=16), :] = jnp.where(left[:4], even, odd)
-            piece_ref[n, pl.ds(k2 + 64, 1), :] = turned_ref[pl.ds(starts[n] + 8, 1), :]
+            piece_ref[n, pl.ds(k2, 8, stride=8), :] = turned_ref[pl.ds(starts[n], 8), :]
+            piece_ref[n, 64 + k2 : 65 + k2, :] = turned_ref[pl.ds(starts[n] + 8, 1), :]
+    middle = green_ref[64]
     for n in range(4):
-        ends = pltpu.roll(green_ref[64], 192 - starts[n], 1)
-        piece_ref[n, 64:80, :] = jnp.where(left, piece_ref[n, 64:80, :], ends)
+        low = pltpu.roll(middle[:8], 128 - starts[n], 1)
+        high = pltpu.roll(middle[8:], 192 - starts[n], 1)
+        piece_ref[n, 72:80, :] = jnp.where(left, low, high)
     stores = [pltpu.make_async_copy(piece_ref.at[n], out_refs[n], sems.at[n]) for n in range(4)]
     for move in stores:
         move.start()
@@ -341,7 +344,7 @@
     )
     send, place, green_hat = call(
         pack_kernel,
-        [(640, 128), (1, 256), (128, 16, 128)],
+        [(640, 128), (1, 256), (72, 16, 128)],
         [
             pltpu.VMEM((256, 128), F32),
             pltpu.VMEM((1, 256), jnp.int32),

time: 78.2 us -> 77.8 us (level)
  Pallas kernels: 10.7 us -> 9.89 us
where the time goes in v6:
time: 77.8 us; the launch traced here: 77.6 us
  blocking collectives  47.5 us (61%)
  starting transfers between devices  14.4 us (19%)
  Pallas kernels  9.89 us (13%)
  waiting for transfers between devices  5.68 us (7%)
    all_to_all x3, blocking collectives, all_to_all(): return lax.all_to_all(x, axes, split_axis=0, concat_axis=0, tiled=True)  47.5 us
    all_to_all x1, starting transfers between devices, all_to_all(): return lax.all_to_all(x, axes, split_axis=0, concat_axis=0, tiled=True)  11.5 us
    ppermute x3, waiting for transfers between devices, local(): green.append(lax.ppermute(pieces[n], 'px', pairs))  3.44 us
    ppermute x3, starting transfers between devices, local(): green.append(lax.ppermute(pieces[n], 'px', pairs))  2.87 us
    all_to_all x1, waiting for transfers between devices, all_to_all(): return lax.all_to_all(x, axes, split_axis=0, concat_axis=0, tiled=True)  2.24 us
    pallas_call x1, Pallas kernels, local(): call(pack_kernel, [(640, 128), (1, 256), (72, 16, 128)], [pltpu.VMEM((256...  2.08 us
    pallas_call x1, Pallas kernels, local(): call(plane_kernel, (512, 128), [pltpu.VMEM((9, 64, 128), F32), pltpu.VMEM...  1.73 us
    pallas_call x1, Pallas kernels, local(): call(table_kernel, [jax.ShapeDtypeStruct(x.shape, BF) for x in tables], [...  1.7 us
  transfers between devices with their start and end apart: 4, of which 3 were waited for; matrix products, arithmetic and copies ran while one was open for 0% of the time, Pallas kernels for 4%

profile of v6, /device:TPU:1, one launch (start us, length us, event | category | flops | bytes accessed | tf_op | source)
XLA Modules:
  0.0 77.6 jit_solution(15313245660007274015)
XLA Ops:
  0.0 2.1 %pack_kernel.1 = (f32[640,128]{1,0:T(8,128)}, f32[1,256]{1,0:T(1,128)S(1)}, f32[72,16,128]{2,1,0:T(8,128)S(1)}) custom-call(f32[256,128]{1,0:T(8,128)} %charge_any.1, s32[1,256]{1,0:T(1,128)} %bitcast.18, s32[1,256]{1,0:T(1,128)} %bitcast.19, f32[128,16,128]{2,1,0:T(8,128)} %green_any.1), custom_call_target="tpu_custom_call" | custom-call | tf_op jit(solution)/shard_map/pack_kernel/pallas_call | solution.py:345
  2.1 11.5 %all-to-all-start = ((f32[128,1,640]{2,1,0:T(1,128)}), f32[128,1,640]{2,1,0:T(1,128)S(1)}, u32[]{:S(2)}, u32[]{:S(2)}) async-start(f32[128,1,640]{2,1,0:T(1,128)} %bitcast.2), calls=%async_computation | async-start | bytes 655360 | tf_op jit(solution)/shard_map/all_to_all | solution.py:327
  13.6 1.1 %green_kernel.1 = (f32[80,128]{1,0:T(8,128)}, f32[80,128]{1,0:T(8,128)}, f32[80,128]{1,0:T(8,128)}, f32[80,128]{1,0:T(8,128)}) custom-call(f32[72,16,128]{2,1,0:T(8,128)S(1)} %get-tuple-element.24.green_ref), custom_call_target="tpu_custom_call" | custom-call | tf_op jit(solution)/shard_map/green_kernel/pallas_call | solution.py:361
  14.7 1.1 %collective-permute-start = (f32[80,128]{1,0:T(8,128)}, f32[80,128]{1,0:T(8,128)S(1)}, u32[]{:S(2)}, u32[]{:S(2)}) collective-permute-start(f32[80,128]{1,0:T(8,128)} %get-tuple-element.26), channel_id=1, source_target_pairs={{0,16},{16,0},{32,48},{48,32},{64,80},{80,64},{96,112},{112,96},{1... | collective-permute-start | bytes 122888 | tf_op jit(solution)/shard_map/ppermute | solution.py:376
  15.8 0.8 %collective-permute-start.1 = (f32[80,128]{1,0:T(8,128)}, f32[80,128]{1,0:T(8,128)S(1)}, u32[]{:S(2)}, u32[]{:S(2)}) collective-permute-start(f32[80,128]{1,0:T(8,128)} %get-tuple-element.27), channel_id=1, source_target_pairs={{0,32},{16,48},{32,0},{48,16},{64,96},{80,112},{96,64},{112,80},{1... | collective-permute-start | bytes 122888 | tf_op jit(solution)/shard_map/ppermute | solution.py:376
  16.6 0.9 %collective-permute-start.2 = (f32[80,128]{1,0:T(8,128)}, f32[80,128]{1,0:T(8,128)S(1)}, u32[]{:S(2)}, u32[]{:S(2)}) collective-permute-start(f32[80,128]{1,0:T(8,128)} %get-tuple-element.28), channel_id=1, source_target_pairs={{0,48},{16,32},{32,16},{48,0},{64,112},{80,96},{96,80},{112,64},{1... | collective-permute-start | bytes 122888 | tf_op jit(solution)/shard_map/ppermute | solution.py:376
  17.6 1.7 %table_kernel.1 = (bf16[2048,256]{1,0:T(8,128)(2,1)S(1)}, bf16[2304,256]{1,0:T(8,128)(2,1)S(1)}, bf16[128,256]{1,0:T(8,128)(2,1)S(1)}, bf16[256,128]{1,0:T(8,128...) custom-call(bf16[2048,256]{1,0:T(8,128)(2,1)} %constant.20.clone.refs_0_, ...), custom_call_target="tpu_custom_call" | custom-call | tf_op jit(solution)/shard_map/table_kernel/pallas_call | solution.py:367
  19.3 0.0 collective-permute-done.refs_1_
  19.3 1.1 %collective-permute-done.1.refs_2_ = f32[80,128]{1,0:T(8,128)S(1)} collective-permute-done((f32[80,128]{1,0:T(8,128)}, f32[80,128]{1,0:T(8,128)S(1)}, u32[]{:S(2)}, u32[]{:S(2)}) %collective-permute-start.1) | collective-permute-done | bytes 40992 | tf_op jit(solution)/shard_map/ppermute | solution.py:376
  20.4 2.4 %collective-permute-done.2.refs_3_ = f32[80,128]{1,0:T(8,128)S(1)} collective-permute-done((f32[80,128]{1,0:T(8,128)}, f32[80,128]{1,0:T(8,128)S(1)}, u32[]{:S(2)}, u32[]{:S(2)}) %collective-permute-start.2) | collective-permute-done | bytes 40992 | tf_op jit(solution)/shard_map/ppermute | solution.py:376
  22.7 2.2 %all-to-all-done = f32[128,1,640]{2,1,0:T(1,128)S(1)} async-done(((f32[128,1,640]{2,1,0:T(1,128)}), f32[128,1,640]{2,1,0:T(1,128)S(1)}, u32[]{:S(2)}, u32[]{:S(2)}) %all-to-all-start) | async-done | bytes 327712 | tf_op jit(solution)/shard_map/all_to_all | solution.py:327
  25.0 0.0 copy-start.4
  25.0 1.1 %z_forward_kernel.1 = f32[640,128]{1,0:T(8,128)S(1)} custom-call(f32[640,128]{1,0:T(8,128)S(1)} %bitcast.10, bf16[2048,256]{1,0:T(8,128)(2,1)S(1)} %get-tuple-element.30.mix_ref, bf16[2304,256]{1,0:T(8,128)(2,1)S(1)} %get-tuple-element.31.wave_ref), custom_call_target="tpu_custom_call" | custom-call | tf_op jit(solution)/shard_map/z_forward_kernel/pallas_call | solution.py:378
  26.1 0.0 copy-start
  26.1 0.0 copy-start.1
  26.1 0.0 copy-start.2
  26.1 0.0 copy-start.3
  26.1 16.6 %all_to_all.20 = f32[128,1,640]{2,1,0:T(1,128)S(1)} all-to-all(f32[128,1,640]{2,1,0:T(1,128)S(1)} %bitcast.13), channel_id=1, replica_groups=mesh['px'=8,'pz'=16] {'px','pz'}, dimensions={0} | all-to-all | bytes 655360 | tf_op jit(solution)/shard_map/all_to_all | solution.py:327
  42.7 0.0 copy-done.4
  42.8 1.7 %plane_kernel.1 = f32[512,128]{1,0:T(8,128)S(1)} custom-call(f32[640,128]{1,0:T(8,128)S(1)} %bitcast.12, f32[80,128]{1,0:T(8,128)S(1)} %copy-done.4, f32[80,128]{1,0:T(8,128)S(1)} %collective-permute-done.refs_1_, f32[80,128]{1,0:T(8,128)S(1)} %collective-permute-done.1.refs_2_, f32[80,128]{1,0:T(8,128)S(1)} %collective-permute-done.2.refs_3_, ...), custom_call_target="tpu_custom_call" | custom-call | tf_op jit(solution)/shard_map/plane_kernel/pallas_call | solution.py:380
  44.5 15.7 %all_to_all.21 = f32[128,4,128]{2,1,0:T(4,128)S(1)} all-to-all(f32[128,4,128]{2,1,0:T(4,128)S(1)} %bitcast.17), channel_id=1, replica_groups=mesh['px'=8,'pz'=16] {'px','pz'}, dimensions={0} | all-to-all | bytes 524288 | tf_op jit(solution)/shard_map/all_to_all | solution.py:327
  60.1 0.0 copy-done
  60.1 0.0 copy-done.1
  60.2 0.0 copy-done.2
  60.2 0.0 copy-done.3
  60.2 1.2 %z_back_kernel.1 = f32[512,128]{1,0:T(8,128)S(1)} custom-call(f32[512,128]{1,0:T(8,128)S(1)} %bitcast.14, f32[640,128]{1,0:T(8,128)S(1)} %bitcast.11, bf16[1152,256]{1,0:T(8,128)(2,1)S(1)} %copy-done.1, bf16[1152,256]{1,0:T(8,128)(2,1)S(1)} %copy-done, bf16[256,1024]{1,0:T(8,128)(2,1)S(1)} %copy-done.3, bf16[256,1024]{1,0:T(8,128)(2,1)S(1)} %copy-done.2), custom_call_target="tpu_custom_call" | custom-call | tf_op jit(solution)/shard_map/z_back_kernel/pallas_call | solution.py:391
  61.3 15.2 %all_to_all.22 = f32[128,4,128]{2,1,0:T(4,128)S(1)} all-to-all(f32[128,4,128]{2,1,0:T(4,128)S(1)} %bitcast.15), channel_id=1, replica_groups=mesh['px'=8,'pz'=16] {'px','pz'}, dimensions={0} | all-to-all | bytes 524288 | tf_op jit(solution)/shard_map/all_to_all | solution.py:327
  76.6 1.0 %unpack_kernel.1 = f32[256,128]{1,0:T(8,128)} custom-call(f32[512,128]{1,0:T(8,128)S(1)} %bitcast.16, f32[1,256]{1,0:T(1,128)S(1)} %get-tuple-element.40.place_ref), custom_call_target="tpu_custom_call" | custom-call | tf_op jit(solution)/shard_map/unpack_kernel/pallas_call | solution.py:395
Async XLA Ops:
  2.1 22.9 %all-to-all-start = ((f32[128,1,640]{2,1,0:T(1,128)}), f32[128,1,640]{2,1,0:T(1,128)S(1)}, u32[]{:S(2)}, u32[]{:S(2)}) async-start(f32[128,1,640]{2,1,0:T(1,128)} %bitcast.2), calls=%async_computation | async-start | bytes 655360 | tf_op jit(solution)/shard_map/all_to_all | solution.py:327
  14.7 4.6 %collective-permute-start = (f32[80,128]{1,0:T(8,128)}, f32[80,128]{1,0:T(8,128)S(1)}, u32[]{:S(2)}, u32[]{:S(2)}) collective-permute-start(f32[80,128]{1,0:T(8,128)} %get-tuple-element.26), channel_id=1, source_target_pairs={{0,16},{16,0},{32,48},{48,32},{64,80},{80,64},{96,112},{112,96},{1... | collective-permute-start | bytes 122888 | tf_op jit(solution)/shard_map/ppermute | solution.py:376
  15.8 4.5 %collective-permute-start.1 = (f32[80,128]{1,0:T(8,128)}, f32[80,128]{1,0:T(8,128)S(1)}, u32[]{:S(2)}, u32[]{:S(2)}) collective-permute-start(f32[80,128]{1,0:T(8,128)} %get-tuple-element.27), channel_id=1, source_target_pairs={{0,32},{16,48},{32,0},{48,16},{64,96},{80,112},{96,64},{112,80},{1... | collective-permute-start | bytes 122888 | tf_op jit(solution)/shard_map/ppermute | solution.py:376
  16.6 6.1 %collective-permute-start.2 = (f32[80,128]{1,0:T(8,128)}, f32[80,128]{1,0:T(8,128)S(1)}, u32[]{:S(2)}, u32[]{:S(2)}) collective-permute-start(f32[80,128]{1,0:T(8,128)} %get-tuple-element.28), channel_id=1, source_target_pairs={{0,48},{16,32},{32,16},{48,0},{64,112},{80,96},{96,80},{112,64},{1... | collective-permute-start | bytes 122888 | tf_op jit(solution)/shard_map/ppermute | solution.py:376
  25.0 17.8 %copy-start.4 = (f32[80,128]{1,0:T(8,128)S(1)}, f32[80,128]{1,0:T(8,128)}, u32[]{:S(2)}) copy-start(f32[80,128]{1,0:T(8,128)} %get-tuple-element.32.refs_0_) | copy-start | bytes 122884
  26.1 34.1 %copy-start = (bf16[1152,256]{1,0:T(8,128)(2,1)S(1)}, bf16[1152,256]{1,0:T(8,128)(2,1)}, u32[]{:S(2)}) copy-start(bf16[1152,256]{1,0:T(8,128)(2,1)} %constant.27.clone.wave_lo_ref) | copy-start | bytes 1769476
  26.1 34.1 %copy-start.1 = (bf16[1152,256]{1,0:T(8,128)(2,1)S(1)}, bf16[1152,256]{1,0:T(8,128)(2,1)}, u32[]{:S(2)}) copy-start(bf16[1152,256]{1,0:T(8,128)(2,1)} %constant.26.clone.wave_hi_ref) | copy-start | bytes 1769476
  26.1 34.0 %copy-start.2 = (bf16[256,1024]{1,0:T(8,128)(2,1)S(1)}, bf16[256,1024]{1,0:T(8,128)(2,1)}, u32[]{:S(2)}) copy-start(bf16[256,1024]{1,0:T(8,128)(2,1)} %constant.29.clone.mix_lo_ref) | copy-start | bytes 1572868
  26.1 34.0 %copy-start.3 = (bf16[256,1024]{1,0:T(8,128)(2,1)S(1)}, bf16[256,1024]{1,0:T(8,128)(2,1)}, u32[]{:S(2)}) copy-start(bf16[256,1024]{1,0:T(8,128)(2,1)} %constant.28.clone.mix_hi_ref) | copy-start | bytes 1572868

commit v7 on v6

--- a/solution.py
+++ b/solution.py
@@ -159,7 +159,7 @@
     return [slice(b * 128 + first, b * 128 + first + count) for b in range(CYP)], count
 
 
-def z_forward_kernel(recv_ref, mix_ref, wave_ref, out_ref, turned_ref):
+def scatter_kernel(recv_ref, mix_ref, mixed_ref):
     ends = recv_ref[pl.ds(4, 128, stride=5), :]
     names = ends.T
     block = block_name(iota((256, 128), 0))
@@ -170,7 +170,13 @@
     high, low = two(field)
     mixed = dot(mix_ref[:1024], jnp.concatenate([high, low], axis=1))
     mixed = mixed[:, :128] + mixed[:, 128:] + dot(mix_ref[1024:], high)
-    mixed = jnp.concatenate([mixed[:512], mixed[512:]], axis=1)
+    mixed_ref[:, :128] = mixed[:512]
+    mixed_ref[:, 128:] = mixed[512:]
+
+
+def z_forward_kernel(mixed_ref, recv_ref, wave_ref, out_ref, turned_ref):
+    ends = recv_ref[pl.ds(4, 128, stride=5), :]
+    mixed = mixed_ref[...]
     for r in range(9):
         places, count = slot_rows(r)
         high, low = two(jnp.concatenate([mixed[place] for place in places], axis=0))
@@ -374,8 +380,9 @@
     for n in range(1, 4):
         pairs = [(i, i // 4 * 4 + ((i % 4) ^ n)) for i in range(N_PX)]
         green.append(lax.ppermute(pieces[n], "px", pairs))
-    recv, green = lax.optimization_barrier((recv, green))
-    lines = call(z_forward_kernel, (640, 128), [pltpu.VMEM((512, 128), F32)])(recv, mix_both, wave_both)
+    mixed = call(scatter_kernel, (512, 256))(recv, mix_both)
+    mixed, green = lax.optimization_barrier((mixed, green))
+    lines = call(z_forward_kernel, (640, 128), [pltpu.VMEM((512, 128), F32)])(mixed, recv, wave_both)
     planes = all_to_all(lines.reshape(N_DEV, 1, 640), BOTH).reshape(640, 128)
     planes = call(
         plane_kernel,

time: 77.8 us -> 77.2 us (level)
    all_to_all x1, waiting for transfers between devices: 2.24 us -> 5.69 us  [all_to_all(): return lax.all_to_all(x, axes, split_axis=0, concat_axis=0, tiled=True)]
    ppermute x3, waiting for transfers between devices: 3.44 us -> 0.01 us  [local(): green.append(lax.ppermute(pieces[n], 'px', pairs))]
  transfers between devices with their start and end apart: 4 -> 4, of which waited for: 3 -> 1; matrix products, arithmetic and copies ran while one was open for 0% -> 0% of each run, Pallas kernels for 4% -> 5%
where the time goes in v7:
time: 77.2 us; the launch traced here: 77 us
  blocking collectives  46.8 us (61%)
  starting transfers between devices  14.4 us (19%)
  Pallas kernels  9.96 us (13%)
  waiting for transfers between devices  5.7 us (7%)
    all_to_all x3, blocking collectives, all_to_all(): return lax.all_to_all(x, axes, split_axis=0, concat_axis=0, tiled=True)  46.8 us
    all_to_all x1, starting transfers between devices, all_to_all(): return lax.all_to_all(x, axes, split_axis=0, concat_axis=0, tiled=True)  11.5 us
    all_to_all x1, waiting for transfers between devices, all_to_all(): return lax.all_to_all(x, axes, split_axis=0, concat_axis=0, tiled=True)  5.69 us
    ppermute x3, starting transfers between devices, local(): green.append(lax.ppermute(pieces[n], 'px', pairs))  2.87 us
    pallas_call x1, Pallas kernels, local(): call(pack_kernel, [(640, 128), (1, 256), (72, 16, 128)], [pltpu.VMEM((256...  2.08 us
    pallas_call x1, Pallas kernels, local(): call(plane_kernel, (512, 128), [pltpu.VMEM((9, 64, 128), F32), pltpu.VMEM...  1.72 us
    pallas_call x1, Pallas kernels, local(): call(table_kernel, [jax.ShapeDtypeStruct(x.shape, BF) for x in tables], [...  1.7 us
  transfers between devices with their start and end apart: 4, of which 1 were waited for; matrix products, arithmetic and copies ran while one was open for 0% of the time, Pallas kernels for 5%

profile of v7, /device:TPU:1, one launch (start us, length us, event | category | flops | bytes accessed | tf_op | source)
XLA Modules:
  0.0 77.0 jit_solution(592680333837357289)
XLA Ops:
  0.0 2.1 %pack_kernel.1 = (f32[640,128]{1,0:T(8,128)}, f32[1,256]{1,0:T(1,128)S(1)}, f32[72,16,128]{2,1,0:T(8,128)S(1)}) custom-call(f32[256,128]{1,0:T(8,128)} %charge_any.1, s32[1,256]{1,0:T(1,128)} %bitcast.19, s32[1,256]{1,0:T(1,128)} %bitcast.20, f32[128,16,128]{2,1,0:T(8,128)} %green_any.1), custom_call_target="tpu_custom_call" | custom-call | tf_op jit(solution)/shard_map/pack_kernel/pallas_call | solution.py:351
  2.1 11.5 %all-to-all-start = ((f32[128,1,640]{2,1,0:T(1,128)}), f32[128,1,640]{2,1,0:T(1,128)S(1)}, u32[]{:S(2)}, u32[]{:S(2)}) async-start(f32[128,1,640]{2,1,0:T(1,128)} %bitcast.2), calls=%async_computation | async-start | bytes 655360 | tf_op jit(solution)/shard_map/all_to_all | solution.py:333
  13.6 1.1 %green_kernel.1 = (f32[80,128]{1,0:T(8,128)}, f32[80,128]{1,0:T(8,128)}, f32[80,128]{1,0:T(8,128)}, f32[80,128]{1,0:T(8,128)}) custom-call(f32[72,16,128]{2,1,0:T(8,128)S(1)} %get-tuple-element.25.green_ref), custom_call_target="tpu_custom_call" | custom-call | tf_op jit(solution)/shard_map/green_kernel/pallas_call | solution.py:367
  14.7 1.1 %collective-permute-start = (f32[80,128]{1,0:T(8,128)}, f32[80,128]{1,0:T(8,128)S(1)}, u32[]{:S(2)}, u32[]{:S(2)}) collective-permute-start(f32[80,128]{1,0:T(8,128)} %get-tuple-element.27), channel_id=1, source_target_pairs={{0,16},{16,0},{32,48},{48,32},{64,80},{80,64},{96,112},{112,96},{1... | collective-permute-start | bytes 122888 | tf_op jit(solution)/shard_map/ppermute | solution.py:382
  15.8 0.8 %collective-permute-start.1 = (f32[80,128]{1,0:T(8,128)}, f32[80,128]{1,0:T(8,128)S(1)}, u32[]{:S(2)}, u32[]{:S(2)}) collective-permute-start(f32[80,128]{1,0:T(8,128)} %get-tuple-element.28), channel_id=1, source_target_pairs={{0,32},{16,48},{32,0},{48,16},{64,96},{80,112},{96,64},{112,80},{1... | collective-permute-start | bytes 122888 | tf_op jit(solution)/shard_map/ppermute | solution.py:382
  16.6 0.9 %collective-permute-start.2 = (f32[80,128]{1,0:T(8,128)}, f32[80,128]{1,0:T(8,128)S(1)}, u32[]{:S(2)}, u32[]{:S(2)}) collective-permute-start(f32[80,128]{1,0:T(8,128)} %get-tuple-element.29), channel_id=1, source_target_pairs={{0,48},{16,32},{32,16},{48,0},{64,112},{80,96},{96,80},{112,64},{1... | collective-permute-start | bytes 122888 | tf_op jit(solution)/shard_map/ppermute | solution.py:382
  17.6 1.7 %table_kernel.1 = (bf16[2048,256]{1,0:T(8,128)(2,1)S(1)}, bf16[2304,256]{1,0:T(8,128)(2,1)S(1)}, bf16[128,256]{1,0:T(8,128)(2,1)S(1)}, bf16[256,128]{1,0:T(8,128...) custom-call(bf16[2048,256]{1,0:T(8,128)(2,1)} %constant.20.clone.refs_0_, ...), custom_call_target="tpu_custom_call" | custom-call | tf_op jit(solution)/shard_map/table_kernel/pallas_call | solution.py:373
  19.3 5.7 %all-to-all-done = f32[128,1,640]{2,1,0:T(1,128)S(1)} async-done(((f32[128,1,640]{2,1,0:T(1,128)}), f32[128,1,640]{2,1,0:T(1,128)S(1)}, u32[]{:S(2)}, u32[]{:S(2)}) %all-to-all-start) | async-done | bytes 327712 | tf_op jit(solution)/shard_map/all_to_all | solution.py:333
  25.0 0.8 scatter_kernel.1.mixed_ref
  25.7 0.0 collective-permute-done.refs_1_
  25.7 0.0 collective-permute-done.1.refs_2_
  25.7 0.0 collective-permute-done.2.refs_3_
  25.7 0.0 copy-start.4
  25.8 0.5 z_forward_kernel.1
  26.2 0.0 copy-start
  26.2 0.0 copy-start.1
  26.2 0.0 copy-start.2
  26.2 0.0 copy-start.3
  26.3 15.9 %all_to_all.20 = f32[128,1,640]{2,1,0:T(1,128)S(1)} all-to-all(f32[128,1,640]{2,1,0:T(1,128)S(1)} %bitcast.13), channel_id=1, replica_groups=mesh['px'=8,'pz'=16] {'px','pz'}, dimensions={0} | all-to-all | bytes 655360 | tf_op jit(solution)/shard_map/all_to_all | solution.py:333
  42.1 0.0 copy-done.4
  42.1 1.7 %plane_kernel.1 = f32[512,128]{1,0:T(8,128)S(1)} custom-call(f32[640,128]{1,0:T(8,128)S(1)} %bitcast.14, f32[80,128]{1,0:T(8,128)S(1)} %copy-done.4, f32[80,128]{1,0:T(8,128)S(1)} %collective-permute-done.refs_1_, f32[80,128]{1,0:T(8,128)S(1)} %collective-permute-done.1.refs_2_, f32[80,128]{1,0:T(8,128)S(1)} %collective-permute-done.2.refs_3_, ...), custom_call_target="tpu_custom_call" | custom-call | tf_op jit(solution)/shard_map/plane_kernel/pallas_call | solution.py:387
  43.9 15.7 %all_to_all.21 = f32[128,4,128]{2,1,0:T(4,128)S(1)} all-to-all(f32[128,4,128]{2,1,0:T(4,128)S(1)} %bitcast.18), channel_id=1, replica_groups=mesh['px'=8,'pz'=16] {'px','pz'}, dimensions={0} | all-to-all | bytes 524288 | tf_op jit(solution)/shard_map/all_to_all | solution.py:333
  59.5 0.0 copy-done
  59.5 0.0 copy-done.1
  59.5 0.0 copy-done.2
  59.5 0.0 copy-done.3
  59.6 1.2 %z_back_kernel.1 = f32[512,128]{1,0:T(8,128)S(1)} custom-call(f32[512,128]{1,0:T(8,128)S(1)} %bitcast.15, f32[640,128]{1,0:T(8,128)S(1)} %bitcast.12, bf16[1152,256]{1,0:T(8,128)(2,1)S(1)} %copy-done.1, bf16[1152,256]{1,0:T(8,128)(2,1)S(1)} %copy-done, bf16[256,1024]{1,0:T(8,128)(2,1)S(1)} %copy-done.3, bf16[256,1024]{1,0:T(8,128)(2,1)S(1)} %copy-done.2), custom_call_target="tpu_custom_call" | custom-call | tf_op jit(solution)/shard_map/z_back_kernel/pallas_call | solution.py:398
  60.7 15.2 %all_to_all.22 = f32[128,4,128]{2,1,0:T(4,128)S(1)} all-to-all(f32[128,4,128]{2,1,0:T(4,128)S(1)} %bitcast.16), channel_id=1, replica_groups=mesh['px'=8,'pz'=16] {'px','pz'}, dimensions={0} | all-to-all | bytes 524288 | tf_op jit(solution)/shard_map/all_to_all | solution.py:333
  75.9 1.0 %unpack_kernel.1 = f32[256,128]{1,0:T(8,128)} custom-call(f32[512,128]{1,0:T(8,128)S(1)} %bitcast.17, f32[1,256]{1,0:T(1,128)S(1)} %get-tuple-element.40.place_ref), custom_call_target="tpu_custom_call" | custom-call | tf_op jit(solution)/shard_map/unpack_kernel/pallas_call | solution.py:402
Async XLA Ops:
  2.1 22.9 %all-to-all-start = ((f32[128,1,640]{2,1,0:T(1,128)}), f32[128,1,640]{2,1,0:T(1,128)S(1)}, u32[]{:S(2)}, u32[]{:S(2)}) async-start(f32[128,1,640]{2,1,0:T(1,128)} %bitcast.2), calls=%async_computation | async-start | bytes 655360 | tf_op jit(solution)/shard_map/all_to_all | solution.py:333
  14.7 11.0 %collective-permute-start = (f32[80,128]{1,0:T(8,128)}, f32[80,128]{1,0:T(8,128)S(1)}, u32[]{:S(2)}, u32[]{:S(2)}) collective-permute-start(f32[80,128]{1,0:T(8,128)} %get-tuple-element.27), channel_id=1, source_target_pairs={{0,16},{16,0},{32,48},{48,32},{64,80},{80,64},{96,112},{112,96},{1... | collective-permute-start | bytes 122888 | tf_op jit(solution)/shard_map/ppermute | solution.py:382
  15.8 9.9 %collective-permute-start.1 = (f32[80,128]{1,0:T(8,128)}, f32[80,128]{1,0:T(8,128)S(1)}, u32[]{:S(2)}, u32[]{:S(2)}) collective-permute-start(f32[80,128]{1,0:T(8,128)} %get-tuple-element.28), channel_id=1, source_target_pairs={{0,32},{16,48},{32,0},{48,16},{64,96},{80,112},{96,64},{112,80},{1... | collective-permute-start | bytes 122888 | tf_op jit(solution)/shard_map/ppermute | solution.py:382
  16.6 9.1 %collective-permute-start.2 = (f32[80,128]{1,0:T(8,128)}, f32[80,128]{1,0:T(8,128)S(1)}, u32[]{:S(2)}, u32[]{:S(2)}) collective-permute-start(f32[80,128]{1,0:T(8,128)} %get-tuple-element.29), channel_id=1, source_target_pairs={{0,48},{16,32},{32,16},{48,0},{64,112},{80,96},{96,80},{112,64},{1... | collective-permute-start | bytes 122888 | tf_op jit(solution)/shard_map/ppermute | solution.py:382
  25.7 16.4 %copy-start.4 = (f32[80,128]{1,0:T(8,128)S(1)}, f32[80,128]{1,0:T(8,128)}, u32[]{:S(2)}) copy-start(f32[80,128]{1,0:T(8,128)} %get-tuple-element.32.refs_0_) | copy-start | bytes 122884
  26.2 33.3 %copy-start = (bf16[1152,256]{1,0:T(8,128)(2,1)S(1)}, bf16[1152,256]{1,0:T(8,128)(2,1)}, u32[]{:S(2)}) copy-start(bf16[1152,256]{1,0:T(8,128)(2,1)} %constant.27.clone.wave_lo_ref) | copy-start | bytes 1769476
  26.2 33.3 %copy-start.1 = (bf16[1152,256]{1,0:T(8,128)(2,1)S(1)}, bf16[1152,256]{1,0:T(8,128)(2,1)}, u32[]{:S(2)}) copy-start(bf16[1152,256]{1,0:T(8,128)(2,1)} %constant.26.clone.wave_hi_ref) | copy-start | bytes 1769476
  26.2 33.3 %copy-start.2 = (bf16[256,1024]{1,0:T(8,128)(2,1)S(1)}, bf16[256,1024]{1,0:T(8,128)(2,1)}, u32[]{:S(2)}) copy-start(bf16[256,1024]{1,0:T(8,128)(2,1)} %constant.29.clone.mix_lo_ref) | copy-start | bytes 1572868
  26.2 33.3 %copy-start.3 = (bf16[256,1024]{1,0:T(8,128)(2,1)S(1)}, bf16[256,1024]{1,0:T(8,128)(2,1)}, u32[]{:S(2)}) copy-start(bf16[256,1024]{1,0:T(8,128)(2,1)} %constant.28.clone.mix_hi_ref) | copy-start | bytes 1572868

commit v8 on v6

--- a/solution.py
+++ b/solution.py
@@ -374,8 +374,8 @@
     for n in range(1, 4):
         pairs = [(i, i // 4 * 4 + ((i % 4) ^ n)) for i in range(N_PX)]
         green.append(lax.ppermute(pieces[n], "px", pairs))
-    recv, green = lax.optimization_barrier((recv, green))
     lines = call(z_forward_kernel, (640, 128), [pltpu.VMEM((512, 128), F32)])(recv, mix_both, wave_both)
+    lines, green = lax.optimization_barrier((lines, green))
     planes = all_to_all(lines.reshape(N_DEV, 1, 640), BOTH).reshape(640, 128)
     planes = call(
         plane_kernel,

time: 77.8 us -> 77.1 us (level)
    all_to_all x1, waiting for transfers between devices: 2.24 us -> 5.69 us  [all_to_all(): return lax.all_to_all(x, axes, split_axis=0, concat_axis=0, tiled=True)]
    ppermute x3, waiting for transfers between devices: 3.44 us -> 0.01 us  [local(): green.append(lax.ppermute(pieces[n], 'px', pairs))]
  transfers between devices with their start and end apart: 4 -> 4, of which waited for: 3 -> 1; matrix products, arithmetic and copies ran while one was open for 0% -> 0% of each run, Pallas kernels for 4% -> 5%
where the time goes in v8:
time: 77.1 us; the launch traced here: 76.9 us
  blocking collectives  46.8 us (61%)
  starting transfers between devices  14.4 us (19%)
  Pallas kernels  9.9 us (13%)
  waiting for transfers between devices  5.7 us (7%)
    all_to_all x3, blocking collectives, all_to_all(): return lax.all_to_all(x, axes, split_axis=0, concat_axis=0, tiled=True)  46.8 us
    all_to_all x1, starting transfers between devices, all_to_all(): return lax.all_to_all(x, axes, split_axis=0, concat_axis=0, tiled=True)  11.5 us
    all_to_all x1, waiting for transfers between devices, all_to_all(): return lax.all_to_all(x, axes, split_axis=0, concat_axis=0, tiled=True)  5.69 us
    ppermute x3, starting transfers between devices, local(): green.append(lax.ppermute(pieces[n], 'px', pairs))  2.87 us
    pallas_call x1, Pallas kernels, local(): call(pack_kernel, [(640, 128), (1, 256), (72, 16, 128)], [pltpu.VMEM((256...  2.08 us
    pallas_call x1, Pallas kernels, local(): call(plane_kernel, (512, 128), [pltpu.VMEM((9, 64, 128), F32), pltpu.VMEM...  1.73 us
    pallas_call x1, Pallas kernels, local(): call(table_kernel, [jax.ShapeDtypeStruct(x.shape, BF) for x in tables], [...  1.7 us
  transfers between devices with their start and end apart: 4, of which 1 were waited for; matrix products, arithmetic and copies ran while one was open for 0% of the time, Pallas kernels for 5%

profile of v8, /device:TPU:1, one launch (start us, length us, event | category | flops | bytes accessed | tf_op | source)
XLA Modules:
  0.0 76.9 jit_solution(18183130929720573943)
XLA Ops:
  0.0 2.1 %pack_kernel.1 = (f32[640,128]{1,0:T(8,128)}, f32[1,256]{1,0:T(1,128)S(1)}, f32[72,16,128]{2,1,0:T(8,128)S(1)}) custom-call(f32[256,128]{1,0:T(8,128)} %charge_any.1, s32[1,256]{1,0:T(1,128)} %bitcast.18, s32[1,256]{1,0:T(1,128)} %bitcast.19, f32[128,16,128]{2,1,0:T(8,128)} %green_any.1), custom_call_target="tpu_custom_call" | custom-call | tf_op jit(solution)/shard_map/pack_kernel/pallas_call | solution.py:345
  2.1 11.5 %all-to-all-start = ((f32[128,1,640]{2,1,0:T(1,128)}), f32[128,1,640]{2,1,0:T(1,128)S(1)}, u32[]{:S(2)}, u32[]{:S(2)}) async-start(f32[128,1,640]{2,1,0:T(1,128)} %bitcast.2), calls=%async_computation | async-start | bytes 655360 | tf_op jit(solution)/shard_map/all_to_all | solution.py:327
  13.6 1.1 %green_kernel.1 = (f32[80,128]{1,0:T(8,128)}, f32[80,128]{1,0:T(8,128)}, f32[80,128]{1,0:T(8,128)}, f32[80,128]{1,0:T(8,128)}) custom-call(f32[72,16,128]{2,1,0:T(8,128)S(1)} %get-tuple-element.26.green_ref), custom_call_target="tpu_custom_call" | custom-call | tf_op jit(solution)/shard_map/green_kernel/pallas_call | solution.py:361
  14.7 1.1 %collective-permute-start = (f32[80,128]{1,0:T(8,128)}, f32[80,128]{1,0:T(8,128)S(1)}, u32[]{:S(2)}, u32[]{:S(2)}) collective-permute-start(f32[80,128]{1,0:T(8,128)} %get-tuple-element.28), channel_id=1, source_target_pairs={{0,16},{16,0},{32,48},{48,32},{64,80},{80,64},{96,112},{112,96},{1... | collective-permute-start | bytes 122888 | tf_op jit(solution)/shard_map/ppermute | solution.py:376
  15.8 0.8 %collective-permute-start.1 = (f32[80,128]{1,0:T(8,128)}, f32[80,128]{1,0:T(8,128)S(1)}, u32[]{:S(2)}, u32[]{:S(2)}) collective-permute-start(f32[80,128]{1,0:T(8,128)} %get-tuple-element.29), channel_id=1, source_target_pairs={{0,32},{16,48},{32,0},{48,16},{64,96},{80,112},{96,64},{112,80},{1... | collective-permute-start | bytes 122888 | tf_op jit(solution)/shard_map/ppermute | solution.py:376
  16.6 0.9 %collective-permute-start.2 = (f32[80,128]{1,0:T(8,128)}, f32[80,128]{1,0:T(8,128)S(1)}, u32[]{:S(2)}, u32[]{:S(2)}) collective-permute-start(f32[80,128]{1,0:T(8,128)} %get-tuple-element.30), channel_id=1, source_target_pairs={{0,48},{16,32},{32,16},{48,0},{64,112},{80,96},{96,80},{112,64},{1... | collective-permute-start | bytes 122888 | tf_op jit(solution)/shard_map/ppermute | solution.py:376
  17.6 1.7 %table_kernel.1 = (bf16[2048,256]{1,0:T(8,128)(2,1)S(1)}, bf16[2304,256]{1,0:T(8,128)(2,1)S(1)}, bf16[128,256]{1,0:T(8,128)(2,1)S(1)}, bf16[256,128]{1,0:T(8,128...) custom-call(bf16[2048,256]{1,0:T(8,128)(2,1)} %constant.20.clone.refs_0_, ...), custom_call_target="tpu_custom_call" | custom-call | tf_op jit(solution)/shard_map/table_kernel/pallas_call | solution.py:367
  19.3 5.7 %all-to-all-done = f32[128,1,640]{2,1,0:T(1,128)S(1)} async-done(((f32[128,1,640]{2,1,0:T(1,128)}), f32[128,1,640]{2,1,0:T(1,128)S(1)}, u32[]{:S(2)}, u32[]{:S(2)}) %all-to-all-start) | async-done | bytes 327712 | tf_op jit(solution)/shard_map/all_to_all | solution.py:327
  25.0 0.0 copy-start.4
  25.0 1.1 %z_forward_kernel.1 = f32[640,128]{1,0:T(8,128)S(1)} custom-call(f32[640,128]{1,0:T(8,128)S(1)} %bitcast.10, bf16[2048,256]{1,0:T(8,128)(2,1)S(1)} %get-tuple-element.24.mix_ref, bf16[2304,256]{1,0:T(8,128)(2,1)S(1)} %get-tuple-element.25.wave_ref), custom_call_target="tpu_custom_call" | custom-call | tf_op jit(solution)/shard_map/z_forward_kernel/pallas_call | solution.py:377
  26.1 0.0 copy-start
  26.1 0.0 copy-start.1
  26.1 0.0 copy-start.2
  26.1 0.0 copy-start.3
  26.1 0.0 collective-permute-done.refs_1_
  26.1 0.0 collective-permute-done.1.refs_2_
  26.2 0.0 collective-permute-done.2.refs_3_
  26.2 15.9 %all_to_all.20 = f32[128,1,640]{2,1,0:T(1,128)S(1)} all-to-all(f32[128,1,640]{2,1,0:T(1,128)S(1)} %bitcast.13), channel_id=1, replica_groups=mesh['px'=8,'pz'=16] {'px','pz'}, dimensions={0} | all-to-all | bytes 655360 | tf_op jit(solution)/shard_map/all_to_all | solution.py:327
  42.1 0.0 copy-done.4
  42.1 1.7 %plane_kernel.1 = f32[512,128]{1,0:T(8,128)S(1)} custom-call(f32[640,128]{1,0:T(8,128)S(1)} %bitcast.12, f32[80,128]{1,0:T(8,128)S(1)} %copy-done.4, f32[80,128]{1,0:T(8,128)S(1)} %collective-permute-done.refs_1_, f32[80,128]{1,0:T(8,128)S(1)} %collective-permute-done.1.refs_2_, f32[80,128]{1,0:T(8,128)S(1)} %collective-permute-done.2.refs_3_, ...), custom_call_target="tpu_custom_call" | custom-call | tf_op jit(solution)/shard_map/plane_kernel/pallas_call | solution.py:380
  43.8 15.7 %all_to_all.21 = f32[128,4,128]{2,1,0:T(4,128)S(1)} all-to-all(f32[128,4,128]{2,1,0:T(4,128)S(1)} %bitcast.17), channel_id=1, replica_groups=mesh['px'=8,'pz'=16] {'px','pz'}, dimensions={0} | all-to-all | bytes 524288 | tf_op jit(solution)/shard_map/all_to_all | solution.py:327
  59.4 0.0 copy-done
  59.5 0.0 copy-done.1
  59.5 0.0 copy-done.2
  59.5 0.0 copy-done.3
  59.5 1.2 %z_back_kernel.1 = f32[512,128]{1,0:T(8,128)S(1)} custom-call(f32[512,128]{1,0:T(8,128)S(1)} %bitcast.14, f32[640,128]{1,0:T(8,128)S(1)} %bitcast.11, bf16[1152,256]{1,0:T(8,128)(2,1)S(1)} %copy-done.1, bf16[1152,256]{1,0:T(8,128)(2,1)S(1)} %copy-done, bf16[256,1024]{1,0:T(8,128)(2,1)S(1)} %copy-done.3, bf16[256,1024]{1,0:T(8,128)(2,1)S(1)} %copy-done.2), custom_call_target="tpu_custom_call" | custom-call | tf_op jit(solution)/shard_map/z_back_kernel/pallas_call | solution.py:391
  60.6 15.2 %all_to_all.22 = f32[128,4,128]{2,1,0:T(4,128)S(1)} all-to-all(f32[128,4,128]{2,1,0:T(4,128)S(1)} %bitcast.15), channel_id=1, replica_groups=mesh['px'=8,'pz'=16] {'px','pz'}, dimensions={0} | all-to-all | bytes 524288 | tf_op jit(solution)/shard_map/all_to_all | solution.py:327
  75.9 1.0 %unpack_kernel.1 = f32[256,128]{1,0:T(8,128)} custom-call(f32[512,128]{1,0:T(8,128)S(1)} %bitcast.16, f32[1,256]{1,0:T(1,128)S(1)} %get-tuple-element.40.place_ref), custom_call_target="tpu_custom_call" | custom-call | tf_op jit(solution)/shard_map/unpack_kernel/pallas_call | solution.py:395
Async XLA Ops:
  2.1 22.9 %all-to-all-start = ((f32[128,1,640]{2,1,0:T(1,128)}), f32[128,1,640]{2,1,0:T(1,128)S(1)}, u32[]{:S(2)}, u32[]{:S(2)}) async-start(f32[128,1,640]{2,1,0:T(1,128)} %bitcast.2), calls=%async_computation | async-start | bytes 655360 | tf_op jit(solution)/shard_map/all_to_all | solution.py:327
  14.7 11.5 %collective-permute-start = (f32[80,128]{1,0:T(8,128)}, f32[80,128]{1,0:T(8,128)S(1)}, u32[]{:S(2)}, u32[]{:S(2)}) collective-permute-start(f32[80,128]{1,0:T(8,128)} %get-tuple-element.28), channel_id=1, source_target_pairs={{0,16},{16,0},{32,48},{48,32},{64,80},{80,64},{96,112},{112,96},{1... | collective-permute-start | bytes 122888 | tf_op jit(solution)/shard_map/ppermute | solution.py:376
  15.8 10.3 %collective-permute-start.1 = (f32[80,128]{1,0:T(8,128)}, f32[80,128]{1,0:T(8,128)S(1)}, u32[]{:S(2)}, u32[]{:S(2)}) collective-permute-start(f32[80,128]{1,0:T(8,128)} %get-tuple-element.29), channel_id=1, source_target_pairs={{0,32},{16,48},{32,0},{48,16},{64,96},{80,112},{96,64},{112,80},{1... | collective-permute-start | bytes 122888 | tf_op jit(solution)/shard_map/ppermute | solution.py:376
  16.6 9.5 %collective-permute-start.2 = (f32[80,128]{1,0:T(8,128)}, f32[80,128]{1,0:T(8,128)S(1)}, u32[]{:S(2)}, u32[]{:S(2)}) collective-permute-start(f32[80,128]{1,0:T(8,128)} %get-tuple-element.30), channel_id=1, source_target_pairs={{0,48},{16,32},{32,16},{48,0},{64,112},{80,96},{96,80},{112,64},{1... | collective-permute-start | bytes 122888 | tf_op jit(solution)/shard_map/ppermute | solution.py:376
  25.0 17.1 %copy-start.4 = (f32[80,128]{1,0:T(8,128)S(1)}, f32[80,128]{1,0:T(8,128)}, u32[]{:S(2)}) copy-start(f32[80,128]{1,0:T(8,128)} %get-tuple-element.32.refs_0_) | copy-start | bytes 122884
  26.1 33.4 %copy-start = (bf16[1152,256]{1,0:T(8,128)(2,1)S(1)}, bf16[1152,256]{1,0:T(8,128)(2,1)}, u32[]{:S(2)}) copy-start(bf16[1152,256]{1,0:T(8,128)(2,1)} %constant.27.clone.wave_lo_ref) | copy-start | bytes 1769476
  26.1 33.4 %copy-start.1 = (bf16[1152,256]{1,0:T(8,128)(2,1)S(1)}, bf16[1152,256]{1,0:T(8,128)(2,1)}, u32[]{:S(2)}) copy-start(bf16[1152,256]{1,0:T(8,128)(2,1)} %constant.26.clone.wave_hi_ref) | copy-start | bytes 1769476
  26.1 33.3 %copy-start.2 = (bf16[256,1024]{1,0:T(8,128)(2,1)S(1)}, bf16[256,1024]{1,0:T(8,128)(2,1)}, u32[]{:S(2)}) copy-start(bf16[256,1024]{1,0:T(8,128)(2,1)} %constant.29.clone.mix_lo_ref) | copy-start | bytes 1572868
  26.1 33.3 %copy-start.3 = (bf16[256,1024]{1,0:T(8,128)(2,1)S(1)}, bf16[256,1024]{1,0:T(8,128)(2,1)}, u32[]{:S(2)}) copy-start(bf16[256,1024]{1,0:T(8,128)(2,1)} %constant.28.clone.mix_hi_ref) | copy-start | bytes 1572868

commit v9 on v8

--- a/solution.py
+++ b/solution.py
@@ -191,7 +191,7 @@
 
 def plane_kernel(spec_ref, *refs):
     pieces, refs = refs[:4], refs[4:]
-    x_fwd_ref, x_back_ref, y_fwd_ref, y_back_ref, out_ref, green_ref, first_ref, second_ref, line_ref = refs
+    x_fwd_ref, x_back_ref, y_fwd_ref, y_back_ref, out_ref, green_ref, first_ref, second_ref = refs
     me = lax.axis_index("px")
     half, place = me // 4, me % 4
     left, middle = iota((8, 128), 1) < 64, iota((8, 128), 1) == 64
@@ -208,14 +208,15 @@
     lane = iota((16, 128), 1)
     ends = jnp.where(lane <= 64, ends, pltpu.roll(ends, 64, 1))
     y_fwd, y_back, x_fwd, x_back = y_fwd_ref[half], y_back_ref[half], x_fwd_ref[...], x_back_ref[...]
-    for i in range(N_PX):
-        rows = jnp.concatenate([spec_ref[pl.ds(i * 80 + b, 16, stride=5), :] for b in range(CYP)], axis=0)
-        line_ref[i * 128 : (i + 1) * 128, :] = turned_pair(rows)
-    turned = halves(dot(line_ref[...], y_fwd), 128)
-    for i in range(N_PX):
+    for pair in range(4):
+        rows = []
+        for i in (2 * pair, 2 * pair + 1):
+            cells = [spec_ref[pl.ds(i * 80 + b, 16, stride=5), :] for b in range(CYP)]
+            rows.append(turned_pair(jnp.concatenate(cells, axis=0)))
+        turned = halves(dot(jnp.concatenate(rows, axis=0), y_fwd), 128)
         for kk in range(16):
-            row = i * 128 + kk * 8
-            first_ref[kk, i * 8 : (i + 1) * 8, :] = turned[row : row + 8]
+            first_ref[kk, pair * 16 : pair * 16 + 8, :] = turned[kk * 8 : kk * 8 + 8]
+            first_ref[kk, pair * 16 + 8 : pair * 16 + 16, :] = turned[128 + kk * 8 : 136 + kk * 8]
     top = iota((64, 128), 0) == 0
     for group in range(4):
         rows = jnp.concatenate([turned_pair(first_ref[group * 4 + n]) for n in range(4)], axis=0)
@@ -384,7 +385,6 @@
             pltpu.VMEM((9, 64, 128), F32),
             pltpu.VMEM((16, 64, 128), F32),
             pltpu.VMEM((16, 64, 128), F32),
-            pltpu.VMEM((1024, 128), BF),
         ],
     )(planes, *green, x_fwd, x_back, y_fwd, y_back)
     lines = all_to_all(planes.reshape(N_DEV, 4, 128), BOTH).reshape(512, 128)

time: 77.1 us -> 77 us (level)
  no operation moved by 1% of the time
where the time goes in v9:
time: 77 us; the launch traced here: 76.7 us
  blocking collectives  46.8 us (61%)
  starting transfers between devices  14.4 us (19%)
  Pallas kernels  9.73 us (13%)
  waiting for transfers between devices  5.7 us (7%)
    all_to_all x3, blocking collectives, all_to_all(): return lax.all_to_all(x, axes, split_axis=0, concat_axis=0, tiled=True)  46.8 us
    all_to_all x1, starting transfers between devices, all_to_all(): return lax.all_to_all(x, axes, split_axis=0, concat_axis=0, tiled=True)  11.5 us
    all_to_all x1, waiting for transfers between devices, all_to_all(): return lax.all_to_all(x, axes, split_axis=0, concat_axis=0, tiled=True)  5.69 us
    ppermute x3, starting transfers between devices, local(): green.append(lax.ppermute(pieces[n], 'px', pairs))  2.87 us
    pallas_call x1, Pallas kernels, local(): call(pack_kernel, [(640, 128), (1, 256), (72, 16, 128)], [pltpu.VMEM((256...  2.08 us
    pallas_call x1, Pallas kernels, local(): call(table_kernel, [jax.ShapeDtypeStruct(x.shape, BF) for x in tables], [...  1.7 us
    pallas_call x1, Pallas kernels, local(): call(plane_kernel, (512, 128), [pltpu.VMEM((9, 64, 128), F32), pltpu.VMEM...  1.55 us
  transfers between devices with their start and end apart: 4, of which 1 were waited for; matrix products, arithmetic and copies ran while one was open for 0% of the time, Pallas kernels for 5%

profile of v9, /device:TPU:1, one launch (start us, length us, event | category | flops | bytes accessed | tf_op | source)
XLA Modules:
  0.0 76.7 jit_solution(9579212320865239981)
XLA Ops:
  0.0 2.1 %pack_kernel.1 = (f32[640,128]{1,0:T(8,128)}, f32[1,256]{1,0:T(1,128)S(1)}, f32[72,16,128]{2,1,0:T(8,128)S(1)}) custom-call(f32[256,128]{1,0:T(8,128)} %charge_any.1, s32[1,256]{1,0:T(1,128)} %bitcast.18, s32[1,256]{1,0:T(1,128)} %bitcast.19, f32[128,16,128]{2,1,0:T(8,128)} %green_any.1), custom_call_target="tpu_custom_call" | custom-call | tf_op jit(solution)/shard_map/pack_kernel/pallas_call | solution.py:346
  2.1 11.5 %all-to-all-start = ((f32[128,1,640]{2,1,0:T(1,128)}), f32[128,1,640]{2,1,0:T(1,128)S(1)}, u32[]{:S(2)}, u32[]{:S(2)}) async-start(f32[128,1,640]{2,1,0:T(1,128)} %bitcast.2), calls=%async_computation | async-start | bytes 655360 | tf_op jit(solution)/shard_map/all_to_all | solution.py:328
  13.6 1.1 %green_kernel.1 = (f32[80,128]{1,0:T(8,128)}, f32[80,128]{1,0:T(8,128)}, f32[80,128]{1,0:T(8,128)}, f32[80,128]{1,0:T(8,128)}) custom-call(f32[72,16,128]{2,1,0:T(8,128)S(1)} %get-tuple-element.26.green_ref), custom_call_target="tpu_custom_call" | custom-call | tf_op jit(solution)/shard_map/green_kernel/pallas_call | solution.py:362
  14.7 1.1 %collective-permute-start = (f32[80,128]{1,0:T(8,128)}, f32[80,128]{1,0:T(8,128)S(1)}, u32[]{:S(2)}, u32[]{:S(2)}) collective-permute-start(f32[80,128]{1,0:T(8,128)} %get-tuple-element.28), channel_id=1, source_target_pairs={{0,16},{16,0},{32,48},{48,32},{64,80},{80,64},{96,112},{112,96},{1... | collective-permute-start | bytes 122888 | tf_op jit(solution)/shard_map/ppermute | solution.py:377
  15.8 0.8 %collective-permute-start.1 = (f32[80,128]{1,0:T(8,128)}, f32[80,128]{1,0:T(8,128)S(1)}, u32[]{:S(2)}, u32[]{:S(2)}) collective-permute-start(f32[80,128]{1,0:T(8,128)} %get-tuple-element.29), channel_id=1, source_target_pairs={{0,32},{16,48},{32,0},{48,16},{64,96},{80,112},{96,64},{112,80},{1... | collective-permute-start | bytes 122888 | tf_op jit(solution)/shard_map/ppermute | solution.py:377
  16.6 0.9 %collective-permute-start.2 = (f32[80,128]{1,0:T(8,128)}, f32[80,128]{1,0:T(8,128)S(1)}, u32[]{:S(2)}, u32[]{:S(2)}) collective-permute-start(f32[80,128]{1,0:T(8,128)} %get-tuple-element.30), channel_id=1, source_target_pairs={{0,48},{16,32},{32,16},{48,0},{64,112},{80,96},{96,80},{112,64},{1... | collective-permute-start | bytes 122888 | tf_op jit(solution)/shard_map/ppermute | solution.py:377
  17.6 1.7 %table_kernel.1 = (bf16[2048,256]{1,0:T(8,128)(2,1)S(1)}, bf16[2304,256]{1,0:T(8,128)(2,1)S(1)}, bf16[128,256]{1,0:T(8,128)(2,1)S(1)}, bf16[256,128]{1,0:T(8,128...) custom-call(bf16[2048,256]{1,0:T(8,128)(2,1)} %constant.20.clone.refs_0_, ...), custom_call_target="tpu_custom_call" | custom-call | tf_op jit(solution)/shard_map/table_kernel/pallas_call | solution.py:368
  19.3 5.7 %all-to-all-done = f32[128,1,640]{2,1,0:T(1,128)S(1)} async-done(((f32[128,1,640]{2,1,0:T(1,128)}), f32[128,1,640]{2,1,0:T(1,128)S(1)}, u32[]{:S(2)}, u32[]{:S(2)}) %all-to-all-start) | async-done | bytes 327712 | tf_op jit(solution)/shard_map/all_to_all | solution.py:328
  25.0 0.0 copy-start.4
  25.0 1.1 %z_forward_kernel.1 = f32[640,128]{1,0:T(8,128)S(1)} custom-call(f32[640,128]{1,0:T(8,128)S(1)} %bitcast.10, bf16[2048,256]{1,0:T(8,128)(2,1)S(1)} %get-tuple-element.24.mix_ref, bf16[2304,256]{1,0:T(8,128)(2,1)S(1)} %get-tuple-element.25.wave_ref), custom_call_target="tpu_custom_call" | custom-call | tf_op jit(solution)/shard_map/z_forward_kernel/pallas_call | solution.py:378
  26.1 0.0 copy-start
  26.1 0.0 copy-start.1
  26.1 0.0 copy-start.2
  26.1 0.0 copy-start.3
  26.1 0.0 collective-permute-done.refs_1_
  26.1 0.0 collective-permute-done.1.refs_2_
  26.2 0.0 collective-permute-done.2.refs_3_
  26.2 15.9 %all_to_all.20 = f32[128,1,640]{2,1,0:T(1,128)S(1)} all-to-all(f32[128,1,640]{2,1,0:T(1,128)S(1)} %bitcast.13), channel_id=1, replica_groups=mesh['px'=8,'pz'=16] {'px','pz'}, dimensions={0} | all-to-all | bytes 655360 | tf_op jit(solution)/shard_map/all_to_all | solution.py:328
  42.1 0.0 copy-done.4
  42.1 1.6 %plane_kernel.1 = f32[512,128]{1,0:T(8,128)S(1)} custom-call(f32[640,128]{1,0:T(8,128)S(1)} %bitcast.12, f32[80,128]{1,0:T(8,128)S(1)} %copy-done.4, f32[80,128]{1,0:T(8,128)S(1)} %collective-permute-done.refs_1_, f32[80,128]{1,0:T(8,128)S(1)} %collective-permute-done.1.refs_2_, f32[80,128]{1,0:T(8,128)S(1)} %collective-permute-done.2.refs_3_, ...), custom_call_target="tpu_custom_call" | custom-call | tf_op jit(solution)/shard_map/plane_kernel/pallas_call | solution.py:381
  43.6 15.7 %all_to_all.21 = f32[128,4,128]{2,1,0:T(4,128)S(1)} all-to-all(f32[128,4,128]{2,1,0:T(4,128)S(1)} %bitcast.17), channel_id=1, replica_groups=mesh['px'=8,'pz'=16] {'px','pz'}, dimensions={0} | all-to-all | bytes 524288 | tf_op jit(solution)/shard_map/all_to_all | solution.py:328
  59.3 0.0 copy-done
  59.3 0.0 copy-done.1
  59.3 0.0 copy-done.2
  59.3 0.0 copy-done.3
  59.3 1.2 %z_back_kernel.1 = f32[512,128]{1,0:T(8,128)S(1)} custom-call(f32[512,128]{1,0:T(8,128)S(1)} %bitcast.14, f32[640,128]{1,0:T(8,128)S(1)} %bitcast.11, bf16[1152,256]{1,0:T(8,128)(2,1)S(1)} %copy-done.1, bf16[1152,256]{1,0:T(8,128)(2,1)S(1)} %copy-done, bf16[256,1024]{1,0:T(8,128)(2,1)S(1)} %copy-done.3, bf16[256,1024]{1,0:T(8,128)(2,1)S(1)} %copy-done.2), custom_call_target="tpu_custom_call" | custom-call | tf_op jit(solution)/shard_map/z_back_kernel/pallas_call | solution.py:391
  60.5 15.2 %all_to_all.22 = f32[128,4,128]{2,1,0:T(4,128)S(1)} all-to-all(f32[128,4,128]{2,1,0:T(4,128)S(1)} %bitcast.15), channel_id=1, replica_groups=mesh['px'=8,'pz'=16] {'px','pz'}, dimensions={0} | all-to-all | bytes 524288 | tf_op jit(solution)/shard_map/all_to_all | solution.py:328
  75.7 1.0 %unpack_kernel.1 = f32[256,128]{1,0:T(8,128)} custom-call(f32[512,128]{1,0:T(8,128)S(1)} %bitcast.16, f32[1,256]{1,0:T(1,128)S(1)} %get-tuple-element.40.place_ref), custom_call_target="tpu_custom_call" | custom-call | tf_op jit(solution)/shard_map/unpack_kernel/pallas_call | solution.py:395
Async XLA Ops:
  2.1 22.9 %all-to-all-start = ((f32[128,1,640]{2,1,0:T(1,128)}), f32[128,1,640]{2,1,0:T(1,128)S(1)}, u32[]{:S(2)}, u32[]{:S(2)}) async-start(f32[128,1,640]{2,1,0:T(1,128)} %bitcast.2), calls=%async_computation | async-start | bytes 655360 | tf_op jit(solution)/shard_map/all_to_all | solution.py:328
  14.7 11.5 %collective-permute-start = (f32[80,128]{1,0:T(8,128)}, f32[80,128]{1,0:T(8,128)S(1)}, u32[]{:S(2)}, u32[]{:S(2)}) collective-permute-start(f32[80,128]{1,0:T(8,128)} %get-tuple-element.28), channel_id=1, source_target_pairs={{0,16},{16,0},{32,48},{48,32},{64,80},{80,64},{96,112},{112,96},{1... | collective-permute-start | bytes 122888 | tf_op jit(solution)/shard_map/ppermute | solution.py:377
  15.8 10.3 %collective-permute-start.1 = (f32[80,128]{1,0:T(8,128)}, f32[80,128]{1,0:T(8,128)S(1)}, u32[]{:S(2)}, u32[]{:S(2)}) collective-permute-start(f32[80,128]{1,0:T(8,128)} %get-tuple-element.29), channel_id=1, source_target_pairs={{0,32},{16,48},{32,0},{48,16},{64,96},{80,112},{96,64},{112,80},{1... | collective-permute-start | bytes 122888 | tf_op jit(solution)/shard_map/ppermute | solution.py:377
  16.6 9.5 %collective-permute-start.2 = (f32[80,128]{1,0:T(8,128)}, f32[80,128]{1,0:T(8,128)S(1)}, u32[]{:S(2)}, u32[]{:S(2)}) collective-permute-start(f32[80,128]{1,0:T(8,128)} %get-tuple-element.30), channel_id=1, source_target_pairs={{0,48},{16,32},{32,16},{48,0},{64,112},{80,96},{96,80},{112,64},{1... | collective-permute-start | bytes 122888 | tf_op jit(solution)/shard_map/ppermute | solution.py:377
  25.0 17.1 %copy-start.4 = (f32[80,128]{1,0:T(8,128)S(1)}, f32[80,128]{1,0:T(8,128)}, u32[]{:S(2)}) copy-start(f32[80,128]{1,0:T(8,128)} %get-tuple-element.32.refs_0_) | copy-start | bytes 122884
  26.1 33.2 %copy-start = (bf16[1152,256]{1,0:T(8,128)(2,1)S(1)}, bf16[1152,256]{1,0:T(8,128)(2,1)}, u32[]{:S(2)}) copy-start(bf16[1152,256]{1,0:T(8,128)(2,1)} %constant.27.clone.wave_lo_ref) | copy-start | bytes 1769476
  26.1 33.2 %copy-start.1 = (bf16[1152,256]{1,0:T(8,128)(2,1)S(1)}, bf16[1152,256]{1,0:T(8,128)(2,1)}, u32[]{:S(2)}) copy-start(bf16[1152,256]{1,0:T(8,128)(2,1)} %constant.26.clone.wave_hi_ref) | copy-start | bytes 1769476
  26.1 33.2 %copy-start.2 = (bf16[256,1024]{1,0:T(8,128)(2,1)S(1)}, bf16[256,1024]{1,0:T(8,128)(2,1)}, u32[]{:S(2)}) copy-start(bf16[256,1024]{1,0:T(8,128)(2,1)} %constant.29.clone.mix_lo_ref) | copy-start | bytes 1572868
  26.1 33.2 %copy-start.3 = (bf16[256,1024]{1,0:T(8,128)(2,1)S(1)}, bf16[256,1024]{1,0:T(8,128)(2,1)}, u32[]{:S(2)}) copy-start(bf16[256,1024]{1,0:T(8,128)(2,1)} %constant.28.clone.mix_hi_ref) | copy-start | bytes 1572868

commit v10 on v9

--- a/solution.py
+++ b/solution.py
@@ -232,11 +232,15 @@
         for n in range(4):
             pair = cells[n * 128 : (n + 1) * 128].T
             second_ref[group * 4 + n] = pair[:64] + pair[64:]
-    for i in range(N_PX):
-        rows = jnp.concatenate([second_ref[kk, i * 8 : (i + 1) * 8, :] for kk in range(16)], axis=0)
-        high, low = two(rows)
-        pair = dot(y_back, jnp.concatenate([high, low], axis=1), 0, 1)
-        out_ref[i * 64 : (i + 1) * 64, :] = pair[:64] + pair[64:]
+    for pair in range(4):
+        rows = [
+            second_ref[kk, i * 8 : (i + 1) * 8, :] for i in (2 * pair, 2 * pair + 1) for kk in range(16)
+        ]
+        high, low = two(jnp.concatenate(rows, axis=0))
+        cells = dot(y_back, jnp.concatenate([high, low], axis=1), 0, 1)
+        cells = cells[:64] + cells[64:]
+        out_ref[pair * 128 : pair * 128 + 64, :] = cells[:, :128]
+        out_ref[pair * 128 + 64 : pair * 128 + 128, :] = cells[:, 128:]
 
 
 def z_back_kernel(spec_ref, recv_ref, wave_hi_ref, wave_lo_ref, mix_hi_ref, mix_lo_ref, out_ref, turned_ref, line_ref):

time: 77 us -> 77 us (level)
  no operation moved by 1% of the time
where the time goes in v10:
time: 77 us; the launch traced here: 76.7 us
  blocking collectives  46.8 us (61%)
  starting transfers between devices  14.4 us (19%)
  Pallas kernels  9.7 us (13%)
  waiting for transfers between devices  5.7 us (7%)
    all_to_all x3, blocking collectives, all_to_all(): return lax.all_to_all(x, axes, split_axis=0, concat_axis=0, tiled=True)  46.8 us
    all_to_all x1, starting transfers between devices, all_to_all(): return lax.all_to_all(x, axes, split_axis=0, concat_axis=0, tiled=True)  11.5 us
    all_to_all x1, waiting for transfers between devices, all_to_all(): return lax.all_to_all(x, axes, split_axis=0, concat_axis=0, tiled=True)  5.69 us
    ppermute x3, starting transfers between devices, local(): green.append(lax.ppermute(pieces[n], 'px', pairs))  2.87 us
    pallas_call x1, Pallas kernels, local(): call(pack_kernel, [(640, 128), (1, 256), (72, 16, 128)], [pltpu.VMEM((256...  2.08 us
    pallas_call x1, Pallas kernels, local(): call(table_kernel, [jax.ShapeDtypeStruct(x.shape, BF) for x in tables], [...  1.7 us
    pallas_call x1, Pallas kernels, local(): call(plane_kernel, (512, 128), [pltpu.VMEM((9, 64, 128), F32), pltpu.VMEM...  1.54 us
  transfers between devices with their start and end apart: 4, of which 1 were waited for; matrix products, arithmetic and copies ran while one was open for 0% of the time, Pallas kernels for 5%

profile of v10, /device:TPU:1, one launch (start us, length us, event | category | flops | bytes accessed | tf_op | source)
XLA Modules:
  0.0 76.7 jit_solution(13116846015708987853)
XLA Ops:
  0.0 2.1 %pack_kernel.1 = (f32[640,128]{1,0:T(8,128)}, f32[1,256]{1,0:T(1,128)S(1)}, f32[72,16,128]{2,1,0:T(8,128)S(1)}) custom-call(f32[256,128]{1,0:T(8,128)} %charge_any.1, s32[1,256]{1,0:T(1,128)} %bitcast.18, s32[1,256]{1,0:T(1,128)} %bitcast.19, f32[128,16,128]{2,1,0:T(8,128)} %green_any.1), custom_call_target="tpu_custom_call" | custom-call | tf_op jit(solution)/shard_map/pack_kernel/pallas_call | solution.py:350
  2.1 11.5 %all-to-all-start = ((f32[128,1,640]{2,1,0:T(1,128)}), f32[128,1,640]{2,1,0:T(1,128)S(1)}, u32[]{:S(2)}, u32[]{:S(2)}) async-start(f32[128,1,640]{2,1,0:T(1,128)} %bitcast.2), calls=%async_computation | async-start | bytes 655360 | tf_op jit(solution)/shard_map/all_to_all | solution.py:332
  13.6 1.1 %green_kernel.1 = (f32[80,128]{1,0:T(8,128)}, f32[80,128]{1,0:T(8,128)}, f32[80,128]{1,0:T(8,128)}, f32[80,128]{1,0:T(8,128)}) custom-call(f32[72,16,128]{2,1,0:T(8,128)S(1)} %get-tuple-element.26.green_ref), custom_call_target="tpu_custom_call" | custom-call | tf_op jit(solution)/shard_map/green_kernel/pallas_call | solution.py:366
  14.7 1.1 %collective-permute-start = (f32[80,128]{1,0:T(8,128)}, f32[80,128]{1,0:T(8,128)S(1)}, u32[]{:S(2)}, u32[]{:S(2)}) collective-permute-start(f32[80,128]{1,0:T(8,128)} %get-tuple-element.28), channel_id=1, source_target_pairs={{0,16},{16,0},{32,48},{48,32},{64,80},{80,64},{96,112},{112,96},{1... | collective-permute-start | bytes 122888 | tf_op jit(solution)/shard_map/ppermute | solution.py:381
  15.8 0.8 %collective-permute-start.1 = (f32[80,128]{1,0:T(8,128)}, f32[80,128]{1,0:T(8,128)S(1)}, u32[]{:S(2)}, u32[]{:S(2)}) collective-permute-start(f32[80,128]{1,0:T(8,128)} %get-tuple-element.29), channel_id=1, source_target_pairs={{0,32},{16,48},{32,0},{48,16},{64,96},{80,112},{96,64},{112,80},{1... | collective-permute-start | bytes 122888 | tf_op jit(solution)/shard_map/ppermute | solution.py:381
  16.6 0.9 %collective-permute-start.2 = (f32[80,128]{1,0:T(8,128)}, f32[80,128]{1,0:T(8,128)S(1)}, u32[]{:S(2)}, u32[]{:S(2)}) collective-permute-start(f32[80,128]{1,0:T(8,128)} %get-tuple-element.30), channel_id=1, source_target_pairs={{0,48},{16,32},{32,16},{48,0},{64,112},{80,96},{96,80},{112,64},{1... | collective-permute-start | bytes 122888 | tf_op jit(solution)/shard_map/ppermute | solution.py:381
  17.6 1.7 %table_kernel.1 = (bf16[2048,256]{1,0:T(8,128)(2,1)S(1)}, bf16[2304,256]{1,0:T(8,128)(2,1)S(1)}, bf16[128,256]{1,0:T(8,128)(2,1)S(1)}, bf16[256,128]{1,0:T(8,128...) custom-call(bf16[2048,256]{1,0:T(8,128)(2,1)} %constant.20.clone.refs_0_, ...), custom_call_target="tpu_custom_call" | custom-call | tf_op jit(solution)/shard_map/table_kernel/pallas_call | solution.py:372
  19.3 5.7 %all-to-all-done = f32[128,1,640]{2,1,0:T(1,128)S(1)} async-done(((f32[128,1,640]{2,1,0:T(1,128)}), f32[128,1,640]{2,1,0:T(1,128)S(1)}, u32[]{:S(2)}, u32[]{:S(2)}) %all-to-all-start) | async-done | bytes 327712 | tf_op jit(solution)/shard_map/all_to_all | solution.py:332
  25.0 0.0 copy-start.4
  25.0 1.1 %z_forward_kernel.1 = f32[640,128]{1,0:T(8,128)S(1)} custom-call(f32[640,128]{1,0:T(8,128)S(1)} %bitcast.10, bf16[2048,256]{1,0:T(8,128)(2,1)S(1)} %get-tuple-element.24.mix_ref, bf16[2304,256]{1,0:T(8,128)(2,1)S(1)} %get-tuple-element.25.wave_ref), custom_call_target="tpu_custom_call" | custom-call | tf_op jit(solution)/shard_map/z_forward_kernel/pallas_call | solution.py:382
  26.1 0.0 copy-start
  26.1 0.0 copy-start.1
  26.1 0.0 copy-start.2
  26.1 0.0 copy-start.3
  26.1 0.0 collective-permute-done.refs_1_
  26.1 0.0 collective-permute-done.1.refs_2_
  26.2 0.0 collective-permute-done.2.refs_3_
  26.2 15.9 %all_to_all.20 = f32[128,1,640]{2,1,0:T(1,128)S(1)} all-to-all(f32[128,1,640]{2,1,0:T(1,128)S(1)} %bitcast.13), channel_id=1, replica_groups=mesh['px'=8,'pz'=16] {'px','pz'}, dimensions={0} | all-to-all | bytes 655360 | tf_op jit(solution)/shard_map/all_to_all | solution.py:332
  42.1 0.0 copy-done.4
  42.1 1.5 %plane_kernel.1 = f32[512,128]{1,0:T(8,128)S(1)} custom-call(f32[640,128]{1,0:T(8,128)S(1)} %bitcast.12, f32[80,128]{1,0:T(8,128)S(1)} %copy-done.4, f32[80,128]{1,0:T(8,128)S(1)} %collective-permute-done.refs_1_, f32[80,128]{1,0:T(8,128)S(1)} %collective-permute-done.1.refs_2_, f32[80,128]{1,0:T(8,128)S(1)} %collective-permute-done.2.refs_3_, ...), custom_call_target="tpu_custom_call" | custom-call | tf_op jit(solution)/shard_map/plane_kernel/pallas_call | solution.py:385
  43.6 15.7 %all_to_all.21 = f32[128,4,128]{2,1,0:T(4,128)S(1)} all-to-all(f32[128,4,128]{2,1,0:T(4,128)S(1)} %bitcast.17), channel_id=1, replica_groups=mesh['px'=8,'pz'=16] {'px','pz'}, dimensions={0} | all-to-all | bytes 524288 | tf_op jit(solution)/shard_map/all_to_all | solution.py:332
  59.3 0.0 copy-done
  59.3 0.0 copy-done.1
  59.3 0.0 copy-done.2
  59.3 0.0 copy-done.3
  59.3 1.2 %z_back_kernel.1 = f32[512,128]{1,0:T(8,128)S(1)} custom-call(f32[512,128]{1,0:T(8,128)S(1)} %bitcast.14, f32[640,128]{1,0:T(8,128)S(1)} %bitcast.11, bf16[1152,256]{1,0:T(8,128)(2,1)S(1)} %copy-done.1, bf16[1152,256]{1,0:T(8,128)(2,1)S(1)} %copy-done, bf16[256,1024]{1,0:T(8,128)(2,1)S(1)} %copy-done.3, bf16[256,1024]{1,0:T(8,128)(2,1)S(1)} %copy-done.2), custom_call_target="tpu_custom_call" | custom-call | tf_op jit(solution)/shard_map/z_back_kernel/pallas_call | solution.py:395
  60.4 15.2 %all_to_all.22 = f32[128,4,128]{2,1,0:T(4,128)S(1)} all-to-all(f32[128,4,128]{2,1,0:T(4,128)S(1)} %bitcast.15), channel_id=1, replica_groups=mesh['px'=8,'pz'=16] {'px','pz'}, dimensions={0} | all-to-all | bytes 524288 | tf_op jit(solution)/shard_map/all_to_all | solution.py:332
  75.7 1.0 %unpack_kernel.1 = f32[256,128]{1,0:T(8,128)} custom-call(f32[512,128]{1,0:T(8,128)S(1)} %bitcast.16, f32[1,256]{1,0:T(1,128)S(1)} %get-tuple-element.40.place_ref), custom_call_target="tpu_custom_call" | custom-call | tf_op jit(solution)/shard_map/unpack_kernel/pallas_call | solution.py:399
Async XLA Ops:
  2.1 22.9 %all-to-all-start = ((f32[128,1,640]{2,1,0:T(1,128)}), f32[128,1,640]{2,1,0:T(1,128)S(1)}, u32[]{:S(2)}, u32[]{:S(2)}) async-start(f32[128,1,640]{2,1,0:T(1,128)} %bitcast.2), calls=%async_computation | async-start | bytes 655360 | tf_op jit(solution)/shard_map/all_to_all | solution.py:332
  14.7 11.5 %collective-permute-start = (f32[80,128]{1,0:T(8,128)}, f32[80,128]{1,0:T(8,128)S(1)}, u32[]{:S(2)}, u32[]{:S(2)}) collective-permute-start(f32[80,128]{1,0:T(8,128)} %get-tuple-element.28), channel_id=1, source_target_pairs={{0,16},{16,0},{32,48},{48,32},{64,80},{80,64},{96,112},{112,96},{1... | collective-permute-start | bytes 122888 | tf_op jit(solution)/shard_map/ppermute | solution.py:381
  15.8 10.3 %collective-permute-start.1 = (f32[80,128]{1,0:T(8,128)}, f32[80,128]{1,0:T(8,128)S(1)}, u32[]{:S(2)}, u32[]{:S(2)}) collective-permute-start(f32[80,128]{1,0:T(8,128)} %get-tuple-element.29), channel_id=1, source_target_pairs={{0,32},{16,48},{32,0},{48,16},{64,96},{80,112},{96,64},{112,80},{1... | collective-permute-start | bytes 122888 | tf_op jit(solution)/shard_map/ppermute | solution.py:381
  16.6 9.5 %collective-permute-start.2 = (f32[80,128]{1,0:T(8,128)}, f32[80,128]{1,0:T(8,128)S(1)}, u32[]{:S(2)}, u32[]{:S(2)}) collective-permute-start(f32[80,128]{1,0:T(8,128)} %get-tuple-element.30), channel_id=1, source_target_pairs={{0,48},{16,32},{32,16},{48,0},{64,112},{80,96},{96,80},{112,64},{1... | collective-permute-start | bytes 122888 | tf_op jit(solution)/shard_map/ppermute | solution.py:381
  25.0 17.1 %copy-start.4 = (f32[80,128]{1,0:T(8,128)S(1)}, f32[80,128]{1,0:T(8,128)}, u32[]{:S(2)}) copy-start(f32[80,128]{1,0:T(8,128)} %get-tuple-element.32.refs_0_) | copy-start | bytes 122884
  26.1 33.2 %copy-start = (bf16[1152,256]{1,0:T(8,128)(2,1)S(1)}, bf16[1152,256]{1,0:T(8,128)(2,1)}, u32[]{:S(2)}) copy-start(bf16[1152,256]{1,0:T(8,128)(2,1)} %constant.27.clone.wave_lo_ref) | copy-start | bytes 1769476
  26.1 33.2 %copy-start.1 = (bf16[1152,256]{1,0:T(8,128)(2,1)S(1)}, bf16[1152,256]{1,0:T(8,128)(2,1)}, u32[]{:S(2)}) copy-start(bf16[1152,256]{1,0:T(8,128)(2,1)} %constant.26.clone.wave_hi_ref) | copy-start | bytes 1769476
  26.1 33.2 %copy-start.2 = (bf16[256,1024]{1,0:T(8,128)(2,1)S(1)}, bf16[256,1024]{1,0:T(8,128)(2,1)}, u32[]{:S(2)}) copy-start(bf16[256,1024]{1,0:T(8,128)(2,1)} %constant.29.clone.mix_lo_ref) | copy-start | bytes 1572868
  26.1 33.2 %copy-start.3 = (bf16[256,1024]{1,0:T(8,128)(2,1)S(1)}, bf16[256,1024]{1,0:T(8,128)(2,1)}, u32[]{:S(2)}) copy-start(bf16[256,1024]{1,0:T(8,128)(2,1)} %constant.28.clone.mix_hi_ref) | copy-start | bytes 1572868
